TPU v7x, 128 devices: a whole 4x4x4 slice. The times are simulated.
128 devices in a mesh: row: 8 (over z, x_hi), col: 16 (over x_lo, y, core).
Axes of the slice: x: 4 (x_hi: 2, x_lo: 2; x = x_hi * 2 + x_lo), y: 4, z: 4, core: 2. Of those that a mesh axis runs over, the one named last changes fastest.
Arguments:
- eigvecs: bfloat16 [81920, 4096], P('row', 'col'), may hold values from -0.09375 to 0.09375
- reflectors: bfloat16 [2, 81920, 128], P(None, 'row'), may hold values from -6 to 6
- factors: float32 [2, 128, 128], replicated, may hold values from -0.00015258789 to 0.00015258789
- frequencies: float32 [4096], replicated, may hold values from 0.3 to 3
- region_blocks: int32 [72], P('row'), may hold values from 0 to 639, as said below
Outputs:
- covariance: float32 [9216, 9216], P('row', 'col')
Inputs may be any that keep to these rules, and one draw needn't show every extreme that they name: `region_blocks`: the 72 block numbers are distinct and ascending; exactly 9 of them lie in each consecutive run of 80 block numbers.
All inputs are finite; a program needn't handle non-finite values.
Results may differ from a plain program's by a relative error of at most 0.004.
Values may be sent and summed in bfloat16 or wider, within the bound.
No kernel may reach another device: no remote copies, remote signals or barrier semaphores. Data moves between devices by JAX's collectives and lax.ppermute only.
A program may use at most 128 MiB of HBM per device.

v0:
```python
import jax
import jax.numpy as jnp
from jax import lax
from jax.sharding import PartitionSpec as P

BLOCK = 128


def from_everyone(shard, axis):
    copies = jnp.broadcast_to(shard, (lax.axis_size(axis), *shard.shape))
    return lax.all_to_all(copies, axis, split_axis=0, concat_axis=0, tiled=True)


def over_copies(shard, axis):
    everything = from_everyone(shard, axis)
    return jnp.sum(everything, axis=0)


def contract_rows(left, right):
    return lax.dot_general(
        left, right, (((0,), (0,)), ((), ())), preferred_element_type=jnp.float32
    )


def contract_cols(left, right):
    return lax.dot_general(
        left, right, (((1,), (1,)), ((), ())), preferred_element_type=jnp.float32
    )


def per_device(eigvecs, reflectors, factors, frequencies, region_blocks):
    highest = lax.Precision.HIGHEST
    first_block = reflectors[0]
    second_block = reflectors[1]
    first_factor = jnp.triu(factors[0])
    second_factor = jnp.triu(factors[1])
    second_local = contract_rows(second_block, eigvecs)
    second_proj = over_copies(second_local, "row")
    second_apply = jnp.dot(second_factor, second_proj, precision=highest).astype(jnp.bfloat16)
    cross_local = contract_rows(first_block, second_block)
    first_local = contract_rows(first_block, eigvecs) - jnp.dot(
        cross_local, second_apply.astype(jnp.float32), precision=highest
    )
    first_proj = over_copies(first_local, "row")
    first_apply = jnp.dot(first_factor, first_proj, precision=highest).astype(jnp.bfloat16)
    local_blocks = eigvecs.shape[0] // BLOCK
    columns = eigvecs.shape[1]
    width = reflectors.shape[2]
    local_index = region_blocks - lax.axis_index("row") * local_blocks
    picked_vecs = jnp.take(
        eigvecs.reshape(local_blocks, BLOCK, columns), local_index, axis=0
    ).reshape(-1, columns)
    picked_refl = jnp.take(
        reflectors.reshape(2, local_blocks, BLOCK, width), local_index, axis=1
    ).reshape(2, -1, width)
    region = picked_vecs.astype(jnp.float32)
    region = region - jnp.dot(picked_refl[1], second_apply, preferred_element_type=jnp.float32)
    region = region - jnp.dot(picked_refl[0], first_apply, preferred_element_type=jnp.float32)
    region = region.astype(jnp.bfloat16)
    weight_all = 1.0 / jnp.tanh(frequencies / 2.0) / (2.0 * frequencies)
    column_index = lax.axis_index("col")
    weight = lax.dynamic_slice_in_dim(weight_all, column_index * columns, columns, 0)
    scaled = (region.astype(jnp.float32) * weight[None, :]).astype(jnp.bfloat16)
    whole = lax.all_gather(region, "row", axis=0, tiled=True)
    partner = lax.all_to_all(whole, "col", split_axis=0, concat_axis=1, tiled=True)
    return contract_cols(lax.all_gather(scaled, "col", axis=1, tiled=True), partner)


def solution(mesh):
    return jax.shard_map(
        per_device,
        mesh=mesh,
        in_specs=(P("row", "col"), P(None, "row", None), P(), P(), P("row")),
        out_specs=P("row", "col"),
        check_vma=False,
    )
```

profile of v0, /device:TPU:1, one launch (start us, length us, event | category | flops | bytes accessed | tf_op | source)
XLA Modules:
  0.0 266.3 jit_solution(2419679412700755586)
XLA Ops:
  6.5 4.3 %fusion.5 = f32[128,256]{1,0:T(8,128)S(1)} fusion(bf16[10240,256]{1,0:T(8,128)(2,1)} %param.5, bf16[2,10240,128]{2,1,0:T(8,128)(2,1)} %param.6), kind=kOutput, calls=%fused_computation.9 | convolution fusion | flops 671088640 | bytes 7995392 | tf_op jit(solution)/shard_map/dot_general | solution.py:20
  10.9 1.1 broadcast_in_dim.46
  11.9 8.3 %all-to-all-start = ((f32[8,128,256]{2,1,0:T(8,128)}), f32[8,128,256]{2,1,0:T(8,128)S(1)}, u32[]{:S(2)}, u32[]{:S(2)}) async-start(f32[8,128,256]{2,1,0:T(8,128)} %broadcast_in_dim.46), calls=%async_computation | async-start | bytes 2097152 | tf_op jit(solution)/shard_map/all_to_all | solution.py:11
  20.3 3.1 %gather_fusion.1 = bf16[9,2,128,128]{3,2,1,0:T(8,128)(2,1)S(1)} fusion(bf16[2,80,128,128]{3,2,1,0:T(8,128)(2,1)} %bitcast.46, s32[1024]{0:T(1024)S(1)} %pad_clamp_fusion), kind=kCustom, calls=%fused_computation.1 | custom fusion | bytes 1179684 | tf_op jit(solution)/shard_map/jit(_take)/gather | solution.py:53
  23.6 3.6 %fusion = f32[128,128]{1,0:T(8,128)S(1)} fusion(bf16[2,10240,128]{2,1,0:T(8,128)(2,1)} %param.6), kind=kOutput, calls=%fused_computation.4 | convolution fusion | flops 335544320 | bytes 5308416 | tf_op jit(solution)/shard_map/dot_general | solution.py:20
  27.3 2.8 %fusion.2 = f32[128,256]{1,0:T(8,128)S(1)} fusion(bf16[10240,256]{1,0:T(8,128)(2,1)S(1)} %bitcast.44, bf16[2,10240,128]{2,1,0:T(8,128)(2,1)} %param.6), kind=kOutput, calls=%fused_computation.6 | convolution fusion | flops 671088640 | bytes 7995392 | tf_op jit(solution)/shard_map/dot_general | solution.py:20
  30.2 6.1 %all-to-all-done = f32[8,128,256]{2,1,0:T(8,128)S(1)} async-done(((f32[8,128,256]{2,1,0:T(8,128)}), f32[8,128,256]{2,1,0:T(8,128)S(1)}, u32[]{:S(2)}, u32[]{:S(2)}) %all-to-all-start) | async-done | bytes 1048608 | tf_op jit(solution)/shard_map/all_to_all | solution.py:11
  36.3 0.3 convolution_convert_fusion.1
  36.6 0.2 convolution_subtract_fusion.2
  36.9 1.1 broadcast_in_dim.47
  37.9 4.1 %all-to-all-start.1 = ((f32[8,128,256]{2,1,0:T(8,128)}), f32[8,128,256]{2,1,0:T(8,128)S(1)}, u32[]{:S(2)}, u32[]{:S(2)}) async-start(f32[8,128,256]{2,1,0:T(8,128)} %broadcast_in_dim.47), calls=%async_computation.1 | async-start | bytes 2097152 | tf_op jit(solution)/shard_map/all_to_all | solution.py:11
  42.2 3.1 %gather_fusion = bf16[9,128,256]{2,1,0:T(8,128)(2,1)S(1)} fusion(bf16[80,128,256]{2,1,0:T(8,128)(2,1)} %bitcast.42, s32[1024]{0:T(1024)S(1)} %pad_clamp_fusion), kind=kCustom, calls=%fused_computation | custom fusion | bytes 1179684 | tf_op jit(solution)/shard_map/jit(_take)/gather | solution.py:50
  45.2 0.8 multiply_divide_fusion
  46.0 0.2 bitcast_select_fusion
  46.2 0.3 convolution_subtract_fusion.1
  46.5 10.9 %all-to-all-done.1 = f32[8,128,256]{2,1,0:T(8,128)S(1)} async-done(((f32[8,128,256]{2,1,0:T(8,128)}), f32[8,128,256]{2,1,0:T(8,128)S(1)}, u32[]{:S(2)}, u32[]{:S(2)}) %all-to-all-start.1) | async-done | bytes 1048608 | tf_op jit(solution)/shard_map/all_to_all | solution.py:11
  57.5 0.3 convolution_convert_fusion
  57.8 1.3 multiply_convert_fusion
  59.2 0.7 all-gather.3.cloned.1.call-update
  59.9 74.4 %all-gather.5.cloned.1.call-done = bf16[9216,256]{1,0:T(8,128)(2,1)} async-done(((bf16[1152,256]{1,0:T(8,128)(2,1)}), bf16[9216,256]{1,0:T(8,128)(2,1)}) %all-gather.5.cloned.1.call-update) | async-done | bytes 4718608 | tf_op jit(solution)/shard_map/all_gather | solution.py:64
  134.3 77.2 %all_to_all.29 = bf16[16,576,256]{2,1,0:T(8,128)(2,1)S(1)} all-to-all(bf16[16,576,256]{2,1,0:T(8,128)(2,1)} %bitcast.47), channel_id=1, replica_groups=mesh['row'=8,'col'=16] {'col'}, dimensions={0} | all-to-all | bytes 9437184 | tf_op jit(solution)/shard_map/all_to_all | solution.py:65
  211.5 2.9 %copy.9 = bf16[16,72,8,256]{3,2,0,1:T(8,128)(2,1)} copy(bf16[16,72,8,256]{3,2,1,0:T(8,128)(2,1)S(1)} %bitcast.45) | data formatting | bytes 9437184 | tf_op jit(solution)/shard_map/all_to_all | solution.py:65
  214.4 33.2 %all-gather.3.cloned.1.call-done = bf16[1152,4096]{1,0:T(8,128)(2,1)} async-done(((bf16[1152,256]{1,0:T(8,128)(2,1)}), bf16[1152,4096]{1,0:T(8,128)(2,1)}) %all-gather.3.cloned.1.call-update) | async-done | bytes 9437200 | tf_op jit(solution)/shard_map/all_gather | solution.py:66
  247.5 12.0 %fusion.21 = f32[1152,576]{0,1:T(8,128)} fusion(bf16[1152,4096]{1,0:T(8,128)(2,1)} %all-gather.3.cloned.1.call-done, bf16[576,4096]{1,0:T(8,128)(2,1)} %bitcast.48), kind=kOutput, calls=%fused_computation.40 | convolution fusion | flops 5435817984 | bytes 16809984 | tf_op jit(solution)/shard_map/dot_general | solution.py:26
  (20 shorter events, 0.6 us)
Async XLA Ops:
  6.5 13.7 %copy-start.1 = (s32[9]{0:T(128)S(1)}, s32[9]{0:T(128)}, u32[]{:S(2)}) copy-start(s32[9]{0:T(128)} %param.9) | copy-start | bytes 112
  10.9 16.4 %slice-start = ((s8[5242880]{0:T(1024)(128)(4,1)}), s8[1048576]{0:T(1024)(128)(4,1)S(1)}, s32[]{:S(2)}) async-start(s8[5242880]{0:T(1024)(128)(4,1)} %bitcast.43), calls=%async_computation.5 | async-start | bytes 2097152
  11.9 24.3 %all-to-all-start = ((f32[8,128,256]{2,1,0:T(8,128)}), f32[8,128,256]{2,1,0:T(8,128)S(1)}, u32[]{:S(2)}, u32[]{:S(2)}) async-start(f32[8,128,256]{2,1,0:T(8,128)} %broadcast_in_dim.46), calls=%async_computation | async-start | bytes 2097152 | tf_op jit(solution)/shard_map/all_to_all | solution.py:11
  23.6 3.8 %slice-start.1 = ((s8[5242880]{0:T(1024)(128)(4,1)}), s8[4194304]{0:T(1024)(128)(4,1)S(1)}, s32[]{:S(2)}) async-start(s8[5242880]{0:T(1024)(128)(4,1)} %bitcast.43), calls=%async_computation.6 | async-start | bytes 8388608
  27.3 9.0 %copy-start = (f32[2,128,128]{2,1,0:T(8,128)S(1)}, f32[2,128,128]{2,1,0:T(8,128)}, u32[]{:S(2)}) copy-start(f32[2,128,128]{2,1,0:T(8,128)} %param.7) | copy-start | bytes 393220
  37.9 19.5 %all-to-all-start.1 = ((f32[8,128,256]{2,1,0:T(8,128)}), f32[8,128,256]{2,1,0:T(8,128)S(1)}, u32[]{:S(2)}, u32[]{:S(2)}) async-start(f32[8,128,256]{2,1,0:T(8,128)} %broadcast_in_dim.47), calls=%async_computation.1 | async-start | bytes 2097152 | tf_op jit(solution)/shard_map/all_to_all | solution.py:11
  42.0 92.3 %all-gather.5.cloned.1.call-start = ((), (), s32[]{:S(2)}) async-start(), calls=%async_computation.4 | async-start | bytes 5308416 | tf_op jit(solution)/shard_map/all_gather | solution.py:64
  59.2 188.4 %all-gather.3.cloned.1.call-start = ((), (), s32[]{:S(2)}) async-start(), calls=%async_computation.3 | async-start | bytes 10027008 | tf_op jit(solution)/shard_map/all_gather | solution.py:66
Sparse Core Ops, SparseCore 0:
  59.3 74.9 all-gather.4
  135.9 111.5 all-gather.2
where the time goes:
time: 267 us; the launch traced here: 266 us
  waiting for transfers between devices  125 us (47%)
  blocking collectives  77.2 us (29%)
  matrix products  25.1 us (9%)
  between operations  13.6 us (5%)
  starting transfers between devices  12.5 us (5%)
  local copies, waits for them, and re-layouts  11.4 us (4%)
    all_to_all x1, blocking collectives, per_device(): lax.all_to_all(whole, 'col', split_axis=0, concat_axis=1, tiled=True)  77.2 us
    all_gather x1, waiting for transfers between devices, per_device(): whole = lax.all_gather(region, 'row', axis=0, tiled=True)  74.4 us
    all_gather x1, waiting for transfers between devices, per_device(): lax.all_gather(scaled, 'col', axis=1, tiled=True)  33.2 us
    all_to_all x2, waiting for transfers between devices, from_everyone(): return lax.all_to_all(copies, axis, split_axis=0, concat_axis=0, tiled=True)  17 us
    all_to_all x2, starting transfers between devices, from_everyone(): return lax.all_to_all(copies, axis, split_axis=0, concat_axis=0, tiled=True)  12.4 us
    dot_general x1, matrix products, contract_cols(): lax.dot_general(left, right, (((1,), (1,)), ((), ())), preferred_element_...  12 us
    dot_general x3, matrix products, contract_rows(): lax.dot_general(left, right, (((0,), (0,)), ((), ())), preferred_element_...  10.7 us
  transfers between devices with their start and end apart: 4, of which 4 were waited for; matrix products, arithmetic and copies ran while one was open for 6% of the time, Pallas kernels for 0%

commit v1 on v0

v1 whole, which is shorter than its diff:
```python
import jax
import jax.numpy as jnp
from jax import lax
from jax.experimental import pallas as pl
from jax.experimental.pallas import tpu as pltpu
from jax.sharding import Mesh, PartitionSpec as P

BLOCK = 128
F32 = jnp.float32
BF16 = jnp.bfloat16
ALL = ("z", "xh", "xl", "y", "core")
NZ, NX, NL, NY, NC = 4, 2, 2, 4, 2


def shift(x, axis, size, step):
    return lax.ppermute(x, axis, [(i, (i + step) % size) for i in range(size)])


def flip(x, axis, size, bit):
    return lax.ppermute(x, axis, [(i, i ^ bit) for i in range(size)])


def place(z, xh, xl, y, k):
    return (((z * NX + xh) * NL + xl) * NY + y) * NC + k


def turn_pairs():
    pairs = []
    for z in range(NZ):
        for xh in range(NX):
            for xl in range(NL):
                for y in range(NY):
                    to = ((z + y) % NZ, xh ^ xl ^ (z >> 1), z >> 1, 2 * (z & 1) + xh)
                    for k in range(NC):
                        pairs.append((place(z, xh, xl, y, k), place(*to, k)))
    return pairs


def first_dims(left, right):
    return lax.dot_general(
        left, right, (((0,), (0,)), ((), ())), preferred_element_type=F32
    )


def last_dims(left, right):
    return lax.dot_general(
        left, right, (((1,), (1,)), ((), ())), preferred_element_type=F32
    )


def last_dims_exact(left, right):
    return lax.dot_general(
        left,
        right,
        (((1,), (1,)), ((), ())),
        precision=lax.Precision.HIGHEST,
        preferred_element_type=F32,
    )


STEPS = 4


def head_kernel(
    index,
    coords,
    vecs_block,
    refl_block,
    eigvecs,
    reflectors,
    keep,
    send,
    own,
    carry,
    turned,
    refl,
    sums,
    cross,
    own_v,
    refl_v,
    sem_in,
    sem_out,
):
    step = pl.program_id(0)
    rows, width = own_v.shape[0], reflectors.shape[2]
    share = turned.shape[0] - rows
    loads = []
    for i in range(rows // BLOCK):
        take = pl.ds(pl.multiple_of(index[i] * BLOCK, BLOCK), BLOCK)
        to = pl.ds(i * BLOCK, BLOCK)
        loads.append((eigvecs.at[take], own_v.at[to]))
        for n in range(2):
            loads.append(
                (reflectors.at[n, take], refl_v.at[to, pl.ds(n * width, width)])
            )
    loads = [
        pltpu.make_async_copy(a, b, sem_in.at[n]) for n, (a, b) in enumerate(loads)
    ]
    part = pl.ds(pl.multiple_of((coords[2] * NY + coords[3]) * share, 16), share)
    stores = [
        (own_v, own),
        (own_v, carry.at[pl.ds(0, rows)]),
        (own_v, turned.at[pl.ds(0, rows)]),
        (refl_v.at[part], turned.at[pl.ds(rows, share)]),
        (refl_v, refl),
    ]
    stores = [
        pltpu.make_async_copy(a, b, sem_out.at[n]) for n, (a, b) in enumerate(stores)
    ]

    @pl.when(step == 0)
    def _():
        for copy in loads:
            copy.start()
        sums[...] = jnp.zeros_like(sums)
        cross[...] = jnp.zeros_like(cross)

    both = jnp.concatenate([refl_block[0], refl_block[1]], axis=1)
    sums[...] += first_dims(vecs_block[...], both)
    cross[...] += first_dims(refl_block[1], refl_block[0])

    @pl.when(step == 1)
    def _():
        for copy in loads:
            copy.wait()
        for copy in stores:
            copy.start()

    @pl.when(step == STEPS - 1)
    def _():
        half = sums.shape[0] // 2
        mine = coords[0] & 1
        wide = jnp.concatenate([cross[:64, :], cross[64:, :]], axis=1)
        keep[:half, :] = sums[pl.ds(pl.multiple_of(mine * half, half), half), :]
        keep[half:, :] = wide
        send[:half, :] = sums[pl.ds(pl.multiple_of((1 - mine) * half, half), half), :]
        send[half:, :] = wide
        for copy in stores:
            copy.wait()


def head(index, coords, eigvecs, reflectors):
    rows = index.shape[0] * BLOCK
    local, columns = eigvecs.shape
    width = reflectors.shape[2]
    block = local // STEPS
    smem = pl.BlockSpec(memory_space=pltpu.SMEM)
    hbm = pl.BlockSpec(memory_space=pltpu.HBM)
    fixed = pl.BlockSpec((192, 256), lambda i: (0, 0))
    return pl.pallas_call(
        head_kernel,
        grid=(STEPS,),
        in_specs=[
            smem,
            smem,
            pl.BlockSpec((block, columns), lambda i: (i, 0)),
            pl.BlockSpec((2, block, width), lambda i: (0, i, 0)),
            hbm,
            hbm,
        ],
        out_specs=[fixed, fixed] + [hbm] * 4,
        out_shape=[
            jax.ShapeDtypeStruct((192, 256), F32),
            jax.ShapeDtypeStruct((192, 256), F32),
            jax.ShapeDtypeStruct((rows, columns), BF16),
            jax.ShapeDtypeStruct((rows + 256, columns), BF16),
            jax.ShapeDtypeStruct((rows + rows // 8, columns), BF16),
            jax.ShapeDtypeStruct((rows, 2 * width), BF16),
        ],
        scratch_shapes=[
            pltpu.VMEM((256, 256), F32),
            pltpu.VMEM((128, 128), F32),
            pltpu.VMEM((rows, columns), BF16),
            pltpu.VMEM((rows, 2 * width), BF16),
            pltpu.SemaphoreType.DMA((3 * index.shape[0],)),
            pltpu.SemaphoreType.DMA((5,)),
        ],
        compiler_params=pltpu.CompilerParams(vmem_limit_bytes=32 * 2**20),
        name="head",
    )(index, coords, eigvecs, reflectors, eigvecs, reflectors)


def source_of(z, xh, xl, y, dxh, dz):
    zz = lax.rem(z + dz, NZ)
    xx = jnp.bitwise_xor(xh, dxh)
    from_y = lax.rem(zz - (2 * xl + (y >> 1)) + NZ, NZ)
    from_l = jnp.bitwise_xor(jnp.bitwise_xor(xx, y & 1), xl)
    return from_y, from_l


def final_kernel(slots_a, slots_b, coords, weight, ya, *rest):
    a_refs, rest = rest[: len(slots_a)], rest[len(slots_a) :]
    b_refs, rest = rest[: len(slots_b)], rest[len(slots_b) :]
    other, own, c_other, c_own, a_all, b_all, b_raw, yb, p_raw, p_all = rest[:10]
    sem_a, sem_b, sem_y, sem_p, sem_c = rest[10:]
    z, xh, xl, y, k = (coords[i] for i in range(5))
    rows = ya.shape[0]
    share = rows // 8
    copies_b, copies_a, copies_p = [], [], []
    for n, ((dxh, dz, start), ref) in enumerate(zip(slots_b, b_refs)):
        count = min(ref.shape[0], rows - start)
        copies_b.append(
            pltpu.make_async_copy(
                ref.at[pl.ds(0, count)],
                b_raw.at[dxh * NZ + dz, pl.ds(start, count)],
                sem_b.at[n],
            )
        )
        if count < ref.shape[0]:
            from_y, from_l = source_of(z, xh, xl, y, dxh, dz)
            to = pl.multiple_of((from_l * NY + from_y) * share, 16)
            copies_b.append(
                pltpu.make_async_copy(
                    ref.at[pl.ds(count, share)], yb.at[pl.ds(to, share)], sem_y.at[n]
                )
            )
    for n, ((slot, start), ref) in enumerate(zip(slots_a, a_refs)):
        count = min(ref.shape[0], rows - start)
        copies_a.append(
            pltpu.make_async_copy(
                ref.at[pl.ds(0, count)],
                a_all.at[pl.ds(start, count), pl.ds(slot * 256, 256)],
                sem_a.at[n],
            )
        )
        if count < ref.shape[0]:
            copies_p.append(
                pltpu.make_async_copy(
                    ref.at[pl.ds(count, 256)], p_raw.at[slot], sem_p.at[n]
                )
            )
    for copy in copies_p + copies_b + copies_a:
        copy.start()
    for copy in copies_p:
        copy.wait()

    def order(slot, carry):
        for dxh in range(NX):
            for dz in range(NZ):
                zz = lax.rem(z + dz, NZ)
                xx = jnp.bitwise_xor(xh, dxh)
                sub = (zz & 1) * 4 + xx * 2 + (zz >> 1)
                start = pl.multiple_of(slot * 256 + sub * 32, 32)
                chunk = (dxh * NZ + dz) * 32
                p_all[pl.ds(start, 32), :] = p_raw[slot, chunk : chunk + 32, :]
        return carry

    lax.fori_loop(0, NL * NY, order, 0)
    for copy in copies_b:
        copy.wait()

    def back_b(p, carry):
        from_y, from_l = source_of(z, xh, xl, y, p // NZ, p % NZ)
        dx = jnp.bitwise_xor(from_l, xl)
        slot = dx * NY + lax.rem(from_y - y + NY, NY)
        whole = (from_l * NY + from_y) * NC + k
        start = pl.multiple_of(slot * 256, 256)
        value = b_raw[p].astype(F32) - last_dims(yb[...], p_all[pl.ds(start, 256), :])
        value = value * weight[pl.ds(whole, 1), :]
        b_all[:, pl.ds(start, 256)] = value.astype(BF16)
        return carry

    lax.fori_loop(0, NX * NZ, back_b, 0)
    for copy in copies_a:
        copy.wait()

    def back_a(slot, carry):
        cols = pl.ds(pl.multiple_of(slot * 256, 256), 256)
        value = a_all[:, cols].astype(F32) - last_dims(ya[...], p_all[cols, :])
        a_all[:, cols] = value.astype(BF16)
        return carry

    lax.fori_loop(0, NL * NY, back_a, 0)
    half = c_own.shape[1]

    def product(which):
        return last_dims(
            a_all[...], b_all[pl.ds(pl.multiple_of(which * half, half), half), :]
        )

    c_other[...] = product(1 - k).astype(BF16)
    out = [
        pltpu.make_async_copy(c_other, other, sem_c.at[0]),
        pltpu.make_async_copy(c_own, own, sem_c.at[1]),
    ]
    out[0].start()
    c_own[...] = product(k)
    out[1].start()
    out[0].wait()
    out[1].wait()


def final(coords, weight, ya, a_list, b_list):
    slots_a = [s for s, _ in a_list]
    slots_b = [s for s, _ in b_list]
    smem = pl.BlockSpec(memory_space=pltpu.SMEM)
    vmem = pl.BlockSpec(memory_space=pltpu.VMEM)
    hbm = pl.BlockSpec(memory_space=pltpu.HBM)
    rows = ya.shape[0]
    half = rows // 2
    slots = NL * NY

    def body(*refs):
        final_kernel(slots_a, slots_b, *refs)

    other, own = pl.pallas_call(
        body,
        out_shape=[
            jax.ShapeDtypeStruct((rows, half), BF16),
            jax.ShapeDtypeStruct((rows, half), F32),
        ],
        in_specs=[smem, vmem, vmem] + [hbm] * (len(a_list) + len(b_list)),
        out_specs=[hbm, hbm],
        scratch_shapes=[
            pltpu.VMEM((rows, half), BF16),
            pltpu.VMEM((rows, half), F32),
            pltpu.VMEM((rows, 256 * slots), BF16),
            pltpu.VMEM((rows, 256 * slots), BF16),
            pltpu.VMEM((slots, rows, 256), BF16),
            pltpu.VMEM((rows, 256), BF16),
            pltpu.VMEM((slots, 256, 256), BF16),
            pltpu.VMEM((256 * slots, 256), BF16),
            pltpu.SemaphoreType.DMA((len(a_list),)),
            pltpu.SemaphoreType.DMA((len(b_list),)),
            pltpu.SemaphoreType.DMA((len(b_list),)),
            pltpu.SemaphoreType.DMA((len(a_list),)),
            pltpu.SemaphoreType.DMA((2,)),
        ],
        compiler_params=pltpu.CompilerParams(vmem_limit_bytes=48 * 2**20),
        name="covariance",
    )(coords, weight, ya, *[v for _, v in a_list], *[v for _, v in b_list])
    return own + flip(other, "core", NC, 1).astype(F32)


def halve(both, mine):
    half = (both.shape[0] - 64) // 2
    cross = both[2 * half :]
    keep = lax.dynamic_slice_in_dim(both, mine * half, half, 0)
    send = lax.dynamic_slice_in_dim(both, (1 - mine) * half, half, 0)
    return jnp.concatenate([keep, cross], axis=0), jnp.concatenate([send, cross], axis=0)


def apply_factors(both, factors):
    part, cross = both[:32], both[32:]
    cross = jnp.concatenate([cross[:, :128], cross[:, 128:]], axis=0)
    t1, t2 = jnp.triu(factors[0]), jnp.triu(factors[1])
    second_apply = last_dims_exact(part[:, 128:], t2).astype(BF16)
    first_part = part[:, :128] - jnp.dot(
        second_apply.astype(F32), cross, precision=lax.Precision.HIGHEST
    )
    first_apply = last_dims_exact(first_part, t1).astype(BF16)
    return jnp.concatenate([first_apply, second_apply], axis=1)


def ahead(x, axis, size):
    return [x, shift(x, axis, size, -1), shift(x, axis, size, 2), shift(x, axis, size, 1)]


def per_device(eigvecs, reflectors, factors, frequencies, region_blocks):
    z, xh, xl, y, k = (lax.axis_index(a) for a in ALL)
    local_blocks = eigvecs.shape[0] // BLOCK
    index = region_blocks - (z * NX + xh) * local_blocks
    coords = jnp.stack([z, xh, xl, y, k]).astype(jnp.int32)
    keep, send, own, carry, turned, refl = head(index, coords, eigvecs, reflectors)
    rows = own.shape[0]
    mid, low = rows // 2, turned.shape[0] // 32 * 16 + 16
    together = lax.optimization_barrier

    a, b = {}, {}
    b[0, 0] = lax.ppermute(turned, ALL, turn_pairs())
    across = flip(own, "xl", NL, 1)
    both = keep + flip(send, "z", NZ, 1)
    keep, send = halve(both, xh)
    both = keep + flip(send, "xh", NX, 1)
    keep, send = halve(both, z >> 1)
    both = keep + flip(send, "z", NZ, 2)
    p = apply_factors(both, factors)
    p = jnp.concatenate(ahead(p, "z", NZ), axis=0)
    p = jnp.concatenate([p, flip(p, "xh", NX, 1)], axis=0)

    b[0, 0], across, p = together((b[0, 0], across, p))
    a[0, 0] = lax.dynamic_update_slice(carry, p, (rows, 0))
    b[0, 1] = shift(b[0, 0], "z", NZ, -1)
    b[0, 3] = shift(b[0, 0], "z", NZ, 1)
    b[1, 0] = flip(b[0, 0], "xh", NX, 1)
    a[0, 1] = shift(a[0, 0], "y", NY, -1)
    a[0, 3] = shift(a[0, 0], "y", NY, 1)
    a[1, 0] = jnp.concatenate([across, flip(p, "xl", NL, 1)], axis=0)

    a[1, 0], a[0, 1], a[0, 3], b[0, 1], b[0, 3], b[1, 0] = together(
        (a[1, 0], a[0, 1], a[0, 3], b[0, 1], b[0, 3], b[1, 0])
    )
    b[1, 1] = shift(b[1, 0], "z", NZ, -1)
    b[1, 3] = shift(b[1, 0], "z", NZ, 1)
    b02 = [shift(b[0, 1][:low], "z", NZ, -1), shift(b[0, 3][low:], "z", NZ, 1)]
    a[0, 2] = shift(a[0, 1], "y", NY, -1)
    a[1, 3] = shift(a[1, 0], "y", NY, 1)
    a[1, 1] = flip(a[0, 1], "xl", NL, 1)

    a[0, 2], a[1, 3], a[1, 1], b[1, 1], b[1, 3], *b02 = together(
        (a[0, 2], a[1, 3], a[1, 1], b[1, 1], b[1, 3], *b02)
    )
    a12 = [shift(a[1, 1][:mid], "y", NY, -1), shift(a[1, 3][mid:], "y", NY, 1)]
    b12 = [shift(b[1, 1][:low], "z", NZ, -1), shift(b[1, 3][low:], "z", NZ, 1)]

    a_list = [((dx * NY + dy, 0), v) for (dx, dy), v in a.items()]
    a_list += [((NY + 2, 0), a12[0]), ((NY + 2, mid), a12[1])]
    b_list = [((dx, dz, 0), v) for (dx, dz), v in b.items()]
    for dx, (top, rest) in enumerate((b02, b12)):
        b_list += [((dx, 2, 0), top), ((dx, 2, low), rest)]
    weight = 1.0 / jnp.tanh(frequencies / 2.0) / (2.0 * frequencies)
    return final(coords, weight.reshape(16, 256), refl, a_list, b_list)


def solution(mesh):
    grid = Mesh(mesh.devices.reshape(NZ, NX, NL, NY, NC), ALL)
    row, col = ("z", "xh"), ("xl", "y", "core")
    return jax.shard_map(
        per_device,
        mesh=grid,
        in_specs=(P(row, col), P(None, row, None), P(), P(), P(row)),
        out_specs=P(row, col),
        check_vma=False,
    )
```

time: 267 us -> 181 us (0.68)
  blocking collectives: 77.2 us -> 0 us
  waiting for transfers between devices: 125 us -> 70.9 us
  starting transfers between devices: 12.5 us -> 57.9 us
  Pallas kernels: 0 us -> 26 us
  matrix products: 25.1 us -> 0.71 us
  between operations: 13.6 us -> 0.4 us
  local copies, waits for them, and re-layouts: 11.4 us -> 20.6 us
  other arithmetic: 1.27 us -> 4.39 us
    all_gather x2 -> x0, waiting for transfers between devices: 108 us -> none  [the longest x1 74.4 us: per_device(): whole = lax.all_gather(region, 'row', axis=0, tiled=True)]
    all_to_all x1 -> x0, blocking collectives: 77.2 us -> none  [per_device(): lax.all_to_all(whole, 'col', split_axis=0, concat_axis=1, tiled=True)]
    ppermute x0 -> x27, waiting for transfers between devices: none -> 70.9 us  [the longest x9 50 us: flip(): return lax.ppermute(x, axis, [(i, i ^ bit) for i in range(size)])]
    ppermute x0 -> x27, starting transfers between devices: none -> 57.9 us  [the longest x9 31.3 us: flip(): return lax.ppermute(x, axis, [(i, i ^ bit) for i in range(size)])]
    pallas_call x0 -> x2, Pallas kernels: none -> 26 us  [the longest x1 20.2 us: final(): pl.pallas_call(body, out_shape=[jax.ShapeDtypeStruct((rows, half), BF16),...]
    dot_general x9 -> x3, matrix products: 25.1 us -> 0.71 us  [the longest x2 0.55 us: last_dims_exact(): lax.dot_general(left, right, (((1,), (1,)), ((), ())), precision=lax.Prec...]
    all_to_all x2 -> x0, waiting for transfers between devices: 17 us -> none  [from_everyone(): return lax.all_to_all(copies, axis, split_axis=0, concat_axis=0, tiled=True)]
    all_to_all x2 -> x0, starting transfers between devices: 12.4 us -> none  [from_everyone(): return lax.all_to_all(copies, axis, split_axis=0, concat_axis=0, tiled=True)]
  transfers between devices with their start and end apart: 4 -> 27, of which waited for: 4 -> 11; matrix products, arithmetic and copies ran while one was open for 6% -> 2% of each run, Pallas kernels for 0% -> 0%
where the time goes in v1:
time: 181 us
  waiting for transfers between devices  70.9 us (39%)
  starting transfers between devices  57.9 us (32%)
  Pallas kernels  26 us (14%)
  local copies, waits for them, and re-layouts  20.6 us (11%)
  other arithmetic  4.39 us (2%)
    ppermute x9, waiting for transfers between devices, flip(): return lax.ppermute(x, axis, [(i, i ^ bit) for i in range(size)])  50 us
    ppermute x9, starting transfers between devices, flip(): return lax.ppermute(x, axis, [(i, i ^ bit) for i in range(size)])  31.3 us
    ppermute x17, starting transfers between devices, shift(): return lax.ppermute(x, axis, [(i, (i + step) % size) for i in range(size)])  25.9 us
    ppermute x17, waiting for transfers between devices, shift(): return lax.ppermute(x, axis, [(i, (i + step) % size) for i in range(size)])  20.9 us
    pallas_call x1, Pallas kernels, final(): pl.pallas_call(body, out_shape=[jax.ShapeDtypeStruct((rows, half), BF16),...  20.2 us
    unnamed x43, local copies, waits for them, and re-layouts  11.4 us
    pallas_call x1, Pallas kernels, head(): pl.pallas_call(head_kernel, grid=(STEPS,), in_specs=[smem, smem, pl.Block...  5.84 us
  transfers between devices with their start and end apart: 27, of which 11 were waited for; matrix products, arithmetic and copies ran while one was open for 2% of the time, Pallas kernels for 0%

profile of v1, /device:TPU:1, one launch (start us, length us, event | category | flops | bytes accessed | tf_op | source)
XLA Modules:
  0.0 180.9 jit_solution(6124803217235630693)
XLA Ops:
  0.7 2.5 %copy-done = bf16[10240,256]{1,0:T(8,128)(2,1)S(1)} copy-done((bf16[10240,256]{1,0:T(8,128)(2,1)S(1)}, bf16[10240,256]{1,0:T(8,128)(2,1)}, u32[]{:S(2)}) %copy-start) | copy-done | bytes 5242904
  3.2 2.5 %copy-done.1 = bf16[2,10240,128]{2,1,0:T(8,128)(2,1)S(1)} copy-done((bf16[2,10240,128]{2,1,0:T(8,128)(2,1)S(1)}, bf16[2,10240,128]{2,1,0:T(8,128)(2,1)}, u32[]{:S(2)}) %copy-start.1) | copy-done | bytes 5242904
  5.7 5.8 %head.1 = (f32[192,256]{1,0:T(8,128)S(1)}, f32[192,256]{1,0:T(8,128)S(1)}, bf16[1152,256]{1,0:T(8,128)(2,1)S(1)}, bf16[1408,256]{1,0:T(8,128)(2,1)S(1)}, bf16[12...) custom-call(s32[9]{0:T(128)S(1)} %broadcast_subtract_fusion.index, s32[5]{0:T(128)S(1)} %stack.23.coords.refs_0_, ...), custom_call_target="tpu_custom_call" | custom-call | tf_op jit(solution)/shard_map/head/pallas_call | solution.py:150
  12.4 2.5 %collective-permute-start.2 = (f32[192,256]{1,0:T(8,128)S(1)}, f32[192,256]{1,0:T(8,128)S(1)}, u32[]{:S(2)}, u32[]{:S(2)}) collective-permute-start(f32[192,256]{1,0:T(8,128)S(1)} %get-tuple-element.34), channel_id=1, source_target_pairs={{0,32},{32,0},{64,96},{96,64},{1,33},{33,1},{65,97},{97,65},{2,34}... | collective-permute-start | bytes 589832 | tf_op jit(solution)/shard_map/ppermute | solution.py:20
  14.9 4.6 %collective-permute-done.2 = f32[192,256]{1,0:T(8,128)S(1)} collective-permute-done((f32[192,256]{1,0:T(8,128)S(1)}, f32[192,256]{1,0:T(8,128)S(1)}, u32[]{:S(2)}, u32[]{:S(2)}) %collective-permute-start.2) | collective-permute-done | bytes 196640 | tf_op jit(solution)/shard_map/ppermute | solution.py:20
  19.5 2.7 %collective-permute-start.3 = (f32[128,256]{1,0:T(8,128)S(1)}, f32[128,256]{1,0:T(8,128)S(1)}, u32[]{:S(2)}, u32[]{:S(2)}) collective-permute-start(f32[128,256]{1,0:T(8,128)S(1)} %pad_maximum_fusion.1), channel_id=1, source_target_pairs={{0,16},{16,0},{1,17},{17,1},{2,18},{18,2},{3,19},{19,3},{4,20},{20... | collective-permute-start | bytes 393224 | tf_op jit(solution)/shard_map/ppermute | solution.py:20
  25.0 3.4 %collective-permute-start.4 = (f32[96,256]{1,0:T(8,128)S(1)}, f32[96,256]{1,0:T(8,128)S(1)}, u32[]{:S(2)}, u32[]{:S(2)}) collective-permute-start(f32[96,256]{1,0:T(8,128)S(1)} %pad_maximum_fusion.3), channel_id=1, source_target_pairs={{0,64},{32,96},{64,0},{96,32},{1,65},{33,97},{65,1},{97,33},{2,66}... | collective-permute-start | bytes 294920 | tf_op jit(solution)/shard_map/ppermute | solution.py:20
  28.4 29.1 %collective-permute-done.4 = f32[96,256]{1,0:T(8,128)S(1)} collective-permute-done((f32[96,256]{1,0:T(8,128)S(1)}, f32[96,256]{1,0:T(8,128)S(1)}, u32[]{:S(2)}, u32[]{:S(2)}) %collective-permute-start.4) | collective-permute-done | bytes 98336 | tf_op jit(solution)/shard_map/ppermute | solution.py:20
  58.4 3.8 %collective-permute-start.6 = (bf16[32,256]{1,0:T(8,128)(2,1)S(1)}, bf16[32,256]{1,0:T(8,128)(2,1)S(1)}, u32[]{:S(2)}, u32[]{:S(2)}) collective-permute-start(bf16[32,256]{1,0:T(8,128)(2,1)S(1)} %get-tuple-element.60), channel_id=1, source_target_pairs={{0,64},{32,96},{64,0},{96,32},{1,65},{33,97},{65,1},{97,33},{2,66}... | collective-permute-start | bytes 49160 | tf_op jit(solution)/shard_map/ppermute | solution.py:16
  66.0 3.3 %collective-permute-start.8 = (bf16[128,256]{1,0:T(8,128)(2,1)S(1)}, bf16[128,256]{1,0:T(8,128)(2,1)S(1)}, u32[]{:S(2)}, u32[]{:S(2)}) collective-permute-start(bf16[128,256]{1,0:T(8,128)(2,1)S(1)} %pad_maximum_fusion.5), channel_id=1, source_target_pairs={{0,16},{16,0},{1,17},{17,1},{2,18},{18,2},{3,19},{19,3},{4,20},{20... | collective-permute-start | bytes 196616 | tf_op jit(solution)/shard_map/ppermute | solution.py:20
  73.0 3.1 %collective-permute-start.10 = (bf16[1408,256]{1,0:T(8,128)(2,1)S(1)}, bf16[1408,256]{1,0:T(8,128)(2,1)S(1)}, u32[]{:S(2)}, u32[]{:S(2)}) collective-permute-start(bf16[1408,256]{1,0:T(8,128)(2,1)S(1)} %constant_dynamic-update-slice_fusion.5.refs_3_), channel_id=1, source_target_pairs={{0,6},{2,0},{4,2},{6,4},{1,7},{3,1},{5,3},{7,5},{8,14},{10,8},{12,... | collective-permute-start | bytes 2162696 | tf_op jit(solution)/shard_map/ppermute | solution.py:16
  77.1 2.4 %collective-permute-start.12 = (bf16[1296,256]{1,0:T(8,128)(2,1)S(1)}, bf16[1296,256]{1,0:T(8,128)(2,1)S(1)}, u32[]{:S(2)}, u32[]{:S(2)}) collective-permute-start(bf16[1296,256]{1,0:T(8,128)(2,1)S(1)} %collective-permute-done.refs_12_), channel_id=1, source_target_pairs={{0,96},{32,0},{64,32},{96,64},{1,97},{33,1},{65,33},{97,65},{2,98}... | collective-permute-start | bytes 1990664 | tf_op jit(solution)/shard_map/ppermute | solution.py:16
  80.6 10.3 %collective-permute-done.14.refs_15_ = bf16[1296,256]{1,0:T(8,128)(2,1)S(1)} collective-permute-done((bf16[1296,256]{1,0:T(8,128)(2,1)S(1)}, bf16[1296,256]{1,0:T(8,128)(2,1)S(1)}, u32[]{:S(2)}, u32[]{:S(2)}) %collective-permute-start.14) | collective-permute-done | bytes 663584 | tf_op jit(solution)/shard_map/ppermute | solution.py:20
  92.6 2.1 %collective-permute-start.16 = (bf16[1408,256]{1,0:T(8,128)(2,1)S(1)}, bf16[1408,256]{1,0:T(8,128)(2,1)S(1)}, u32[]{:S(2)}, u32[]{:S(2)}) collective-permute-start(bf16[1408,256]{1,0:T(8,128)(2,1)S(1)} %pad_maximum_fusion.refs_6_), channel_id=1, source_target_pairs={{0,2},{2,4},{4,6},{6,0},{1,3},{3,5},{5,7},{7,1},{8,10},{10,12},{12... | collective-permute-start | bytes 2162696 | tf_op jit(solution)/shard_map/ppermute | solution.py:16
  96.8 3.0 %collective-permute-done.21.refs_19_ = bf16[640,256]{1,0:T(8,128)(2,1)S(1)} collective-permute-done((bf16[640,256]{1,0:T(8,128)(2,1)S(1)}, bf16[640,256]{1,0:T(8,128)(2,1)S(1)}, u32[]{:S(2)}, u32[]{:S(2)}) %collective-permute-start.21) | collective-permute-done | bytes 327712 | tf_op jit(solution)/shard_map/ppermute | solution.py:16
  101.2 2.7 %collective-permute-start.18 = (bf16[1296,256]{1,0:T(8,128)(2,1)S(1)}, bf16[1296,256]{1,0:T(8,128)(2,1)S(1)}, u32[]{:S(2)}, u32[]{:S(2)}) collective-permute-start(bf16[1296,256]{1,0:T(8,128)(2,1)S(1)} %collective-permute-done.14.refs_15_), channel_id=1, source_target_pairs={{0,96},{32,0},{64,32},{96,64},{1,97},{33,1},{65,33},{97,65},{2,98}... | collective-permute-start | bytes 1990664 | tf_op jit(solution)/shard_map/ppermute | solution.py:16
  103.9 10.5 %collective-permute-done.19.refs_17_ = bf16[1296,256]{1,0:T(8,128)(2,1)S(1)} collective-permute-done((bf16[1296,256]{1,0:T(8,128)(2,1)S(1)}, bf16[1296,256]{1,0:T(8,128)(2,1)S(1)}, u32[]{:S(2)}, u32[]{:S(2)}) %collective-permute-start.19) | collective-permute-done | bytes 663584 | tf_op jit(solution)/shard_map/ppermute | solution.py:16
  115.4 2.4 %collective-permute-start.23 = (bf16[832,256]{1,0:T(8,128)(2,1)}, bf16[832,256]{1,0:T(8,128)(2,1)}, u32[]{:S(2)}, u32[]{:S(2)}) collective-permute-start(bf16[832,256]{1,0:T(8,128)(2,1)} %slice.59), channel_id=1, source_target_pairs={{0,2},{2,4},{4,6},{6,0},{1,3},{3,5},{5,7},{7,1},{8,10},{10,12},{12... | collective-permute-start | bytes 1277960 | tf_op jit(solution)/shard_map/ppermute | solution.py:16
  122.3 5.1 %collective-permute-done.22.refs_10_ = bf16[576,256]{1,0:T(8,128)(2,1)} collective-permute-done((bf16[576,256]{1,0:T(8,128)(2,1)}, bf16[576,256]{1,0:T(8,128)(2,1)}, u32[]{:S(2)}, u32[]{:S(2)}) %collective-permute-start.22) | collective-permute-done | bytes 294944 | tf_op jit(solution)/shard_map/ppermute | solution.py:16
  131.5 20.2 %covariance.1 = (bf16[1152,576]{1,0:T(8,128)(2,1)}, f32[1152,576]{1,0:T(8,128)}) custom-call(s32[5]{0:T(128)S(1)} %stack.23.coords.refs_0_, f32[16,256]{1,0:T(8,128)S(1)} %reshape.3.refs_1_, bf16[1152,256]{1,0:T(8,128)(2,1)S(1)} %copy-done.6, bf16[1408,256]{1,0:T(8,128)(2,1)} %copy-done.2, bf16[1408,256]{1,0:T(8,128)(2,1)} %copy-done.16, ...), custom_call_target="tpu_custom_call" | custom-call | tf_op jit(solution)/shard_map/covariance/pallas_call | solution.py:306
  153.6 18.2 %collective-permute-start.26 = (bf16[1152,576]{0,1:T(8,128)(2,1)S(1)}, bf16[1152,576]{0,1:T(8,128)(2,1)S(1)}, u32[]{:S(2)}, u32[]{:S(2)}) collective-permute-start(bf16[1152,576]{0,1:T(8,128)(2,1)S(1)} %copy.7), channel_id=1, source_target_pairs={{0,1},{1,0},{2,3},{3,2},{4,5},{5,4},{6,7},{7,6},{8,9},{9,8},{10,11... | collective-permute-start | bytes 3981320 | tf_op jit(solution)/shard_map/ppermute | solution.py:20
  171.8 2.7 %collective-permute-done.26 = bf16[1152,576]{0,1:T(8,128)(2,1)S(1)} collective-permute-done((bf16[1152,576]{0,1:T(8,128)(2,1)S(1)}, bf16[1152,576]{0,1:T(8,128)(2,1)S(1)}, u32[]{:S(2)}, u32[]{:S(2)}) %collective-permute-start.26) | collective-permute-done | bytes 1327136 | tf_op jit(solution)/shard_map/ppermute | solution.py:20
  176.1 2.5 %convert_add_fusion = f32[1152,576]{1,0:T(8,128)S(1)} fusion(f32[1152,576]{1,0:T(8,128)} %get-tuple-element.51, bf16[1152,576]{1,0:T(8,128)(2,1)} %copy.8), kind=kLoop, calls=%fused_computation | loop fusion | flops 1327104 | bytes 6635520 | tf_op jit(solution)/shard_map/add | solution.py:332
  178.6 2.3 %copy.9 = f32[1152,576]{0,1:T(8,128)} copy(f32[1152,576]{1,0:T(8,128)S(1)} %convert_add_fusion) | data formatting | bytes 5308416 | tf_op jit(solution)/shard_map/add | solution.py:332
  (107 shorter events, 33.0 us)
Async XLA Ops:
  12.4 7.1 %collective-permute-start.2 = (f32[192,256]{1,0:T(8,128)S(1)}, f32[192,256]{1,0:T(8,128)S(1)}, u32[]{:S(2)}, u32[]{:S(2)}) collective-permute-start(f32[192,256]{1,0:T(8,128)S(1)} %get-tuple-element.34), channel_id=1, source_target_pairs={{0,32},{32,0},{64,96},{96,64},{1,33},{33,1},{65,97},{97,65},{2,34}... | collective-permute-start | bytes 589832 | tf_op jit(solution)/shard_map/ppermute | solution.py:20
  19.5 5.4 %collective-permute-start.3 = (f32[128,256]{1,0:T(8,128)S(1)}, f32[128,256]{1,0:T(8,128)S(1)}, u32[]{:S(2)}, u32[]{:S(2)}) collective-permute-start(f32[128,256]{1,0:T(8,128)S(1)} %pad_maximum_fusion.1), channel_id=1, source_target_pairs={{0,16},{16,0},{1,17},{17,1},{2,18},{18,2},{3,19},{19,3},{4,20},{20... | collective-permute-start | bytes 393224 | tf_op jit(solution)/shard_map/ppermute | solution.py:20
  22.3 48.7 %collective-permute-start.1 = (bf16[1152,256]{1,0:T(8,128)(2,1)S(1)}, bf16[1152,256]{1,0:T(8,128)(2,1)}, u32[]{:S(2)}, u32[]{:S(2)}) collective-permute-start(bf16[1152,256]{1,0:T(8,128)(2,1)S(1)} %get-tuple-element.32), channel_id=1, source_target_pairs={{0,8},{8,0},{1,9},{9,1},{2,10},{10,2},{3,11},{11,3},{4,12},{12,4},... | collective-permute-start | bytes 1769480 | tf_op jit(solution)/shard_map/ppermute | solution.py:20
  22.6 48.4 %collective-permute-start = (bf16[1296,256]{1,0:T(8,128)(2,1)S(1)}, bf16[1296,256]{1,0:T(8,128)(2,1)S(1)}, u32[]{:S(2)}, u32[]{:S(2)}) collective-permute-start(bf16[1296,256]{1,0:T(8,128)(2,1)S(1)} %get-tuple-element.31), channel_id=1, source_target_pairs={{0,0},{1,1},{2,32},{3,33},{4,64},{5,65},{6,96},{7,97},{8,16},{9,17... | collective-permute-start | bytes 1990664 | tf_op jit(solution)/shard_map/ppermute | solution.py:370
  25.0 32.6 %collective-permute-start.4 = (f32[96,256]{1,0:T(8,128)S(1)}, f32[96,256]{1,0:T(8,128)S(1)}, u32[]{:S(2)}, u32[]{:S(2)}) collective-permute-start(f32[96,256]{1,0:T(8,128)S(1)} %pad_maximum_fusion.3), channel_id=1, source_target_pairs={{0,64},{32,96},{64,0},{96,32},{1,65},{33,97},{65,1},{97,33},{2,66}... | collective-permute-start | bytes 294920 | tf_op jit(solution)/shard_map/ppermute | solution.py:20
  58.4 5.3 %collective-permute-start.6 = (bf16[32,256]{1,0:T(8,128)(2,1)S(1)}, bf16[32,256]{1,0:T(8,128)(2,1)S(1)}, u32[]{:S(2)}, u32[]{:S(2)}) collective-permute-start(bf16[32,256]{1,0:T(8,128)(2,1)S(1)} %get-tuple-element.60), channel_id=1, source_target_pairs={{0,64},{32,96},{64,0},{96,32},{1,65},{33,97},{65,1},{97,33},{2,66}... | collective-permute-start | bytes 49160 | tf_op jit(solution)/shard_map/ppermute | solution.py:16
  71.0 6.1 %collective-permute-start.9 = (bf16[256,256]{1,0:T(8,128)(2,1)S(1)}, bf16[256,256]{1,0:T(8,128)(2,1)S(1)}, u32[]{:S(2)}, u32[]{:S(2)}) collective-permute-start(bf16[256,256]{1,0:T(8,128)(2,1)S(1)} %constant_dynamic-update-slice_fusion), channel_id=1, source_target_pairs={{0,8},{8,0},{1,9},{9,1},{2,10},{10,2},{3,11},{11,3},{4,12},{12,4},... | collective-permute-start | bytes 393224 | tf_op jit(solution)/shard_map/ppermute | solution.py:20
  71.1 19.8 %collective-permute-start.11 = (bf16[1408,256]{1,0:T(8,128)(2,1)S(1)}, bf16[1408,256]{1,0:T(8,128)(2,1)S(1)}, u32[]{:S(2)}, u32[]{:S(2)}) collective-permute-start(bf16[1408,256]{1,0:T(8,128)(2,1)S(1)} %constant_dynamic-update-slice_fusion.5.refs_3_), channel_id=1, source_target_pairs={{0,2},{2,4},{4,6},{6,0},{1,3},{3,5},{5,7},{7,1},{8,10},{10,12},{12... | collective-permute-start | bytes 2162696 | tf_op jit(solution)/shard_map/ppermute | solution.py:16
  73.0 17.9 %collective-permute-start.10 = (bf16[1408,256]{1,0:T(8,128)(2,1)S(1)}, bf16[1408,256]{1,0:T(8,128)(2,1)S(1)}, u32[]{:S(2)}, u32[]{:S(2)}) collective-permute-start(bf16[1408,256]{1,0:T(8,128)(2,1)S(1)} %constant_dynamic-update-slice_fusion.5.refs_3_), channel_id=1, source_target_pairs={{0,6},{2,0},{4,2},{6,4},{1,7},{3,1},{5,3},{7,5},{8,14},{10,8},{12,... | collective-permute-start | bytes 2162696 | tf_op jit(solution)/shard_map/ppermute | solution.py:16
  76.1 14.8 %collective-permute-start.14 = (bf16[1296,256]{1,0:T(8,128)(2,1)S(1)}, bf16[1296,256]{1,0:T(8,128)(2,1)S(1)}, u32[]{:S(2)}, u32[]{:S(2)}) collective-permute-start(bf16[1296,256]{1,0:T(8,128)(2,1)S(1)} %collective-permute-done.refs_12_), channel_id=1, source_target_pairs={{0,16},{16,0},{1,17},{17,1},{2,18},{18,2},{3,19},{19,3},{4,20},{20... | collective-permute-start | bytes 1990664 | tf_op jit(solution)/shard_map/ppermute | solution.py:20
  76.8 14.1 %collective-permute-start.13 = (bf16[1296,256]{1,0:T(8,128)(2,1)S(1)}, bf16[1296,256]{1,0:T(8,128)(2,1)S(1)}, u32[]{:S(2)}, u32[]{:S(2)}) collective-permute-start(bf16[1296,256]{1,0:T(8,128)(2,1)S(1)} %collective-permute-done.refs_12_), channel_id=1, source_target_pairs={{0,32},{32,64},{64,96},{96,0},{1,33},{33,65},{65,97},{97,1},{2,34}... | collective-permute-start | bytes 1990664 | tf_op jit(solution)/shard_map/ppermute | solution.py:16
  77.1 13.8 %collective-permute-start.12 = (bf16[1296,256]{1,0:T(8,128)(2,1)S(1)}, bf16[1296,256]{1,0:T(8,128)(2,1)S(1)}, u32[]{:S(2)}, u32[]{:S(2)}) collective-permute-start(bf16[1296,256]{1,0:T(8,128)(2,1)S(1)} %collective-permute-done.refs_12_), channel_id=1, source_target_pairs={{0,96},{32,0},{64,32},{96,64},{1,97},{33,1},{65,33},{97,65},{2,98}... | collective-permute-start | bytes 1990664 | tf_op jit(solution)/shard_map/ppermute | solution.py:16
  91.0 9.5 %collective-permute-start.20 = (bf16[656,256]{1,0:T(8,128)(2,1)S(1)}, bf16[656,256]{1,0:T(8,128)(2,1)S(1)}, u32[]{:S(2)}, u32[]{:S(2)}) collective-permute-start(bf16[656,256]{1,0:T(8,128)(2,1)S(1)} %slice.56), channel_id=1, source_target_pairs={{0,96},{32,0},{64,32},{96,64},{1,97},{33,1},{65,33},{97,65},{2,98}... | collective-permute-start | bytes 1007624 | tf_op jit(solution)/shard_map/ppermute | solution.py:16
  92.6 7.2 %collective-permute-start.21 = (bf16[640,256]{1,0:T(8,128)(2,1)S(1)}, bf16[640,256]{1,0:T(8,128)(2,1)S(1)}, u32[]{:S(2)}, u32[]{:S(2)}) collective-permute-start(bf16[640,256]{1,0:T(8,128)(2,1)S(1)} %slice.57), channel_id=1, source_target_pairs={{0,32},{32,64},{64,96},{96,0},{1,33},{33,65},{65,97},{97,1},{2,34}... | collective-permute-start | bytes 983048 | tf_op jit(solution)/shard_map/ppermute | solution.py:16
  92.6 21.7 %collective-permute-start.16 = (bf16[1408,256]{1,0:T(8,128)(2,1)S(1)}, bf16[1408,256]{1,0:T(8,128)(2,1)S(1)}, u32[]{:S(2)}, u32[]{:S(2)}) collective-permute-start(bf16[1408,256]{1,0:T(8,128)(2,1)S(1)} %pad_maximum_fusion.refs_6_), channel_id=1, source_target_pairs={{0,2},{2,4},{4,6},{6,0},{1,3},{3,5},{5,7},{7,1},{8,10},{10,12},{12... | collective-permute-start | bytes 2162696 | tf_op jit(solution)/shard_map/ppermute | solution.py:16
  94.7 19.7 %collective-permute-start.17 = (bf16[1408,256]{1,0:T(8,128)(2,1)S(1)}, bf16[1408,256]{1,0:T(8,128)(2,1)S(1)}, u32[]{:S(2)}, u32[]{:S(2)}) collective-permute-start(bf16[1408,256]{1,0:T(8,128)(2,1)S(1)} %collective-permute-done.10.refs_4_), channel_id=1, source_target_pairs={{0,8},{8,0},{1,9},{9,1},{2,10},{10,2},{3,11},{11,3},{4,12},{12,4},... | collective-permute-start | bytes 2162696 | tf_op jit(solution)/shard_map/ppermute | solution.py:20
  94.7 19.7 %collective-permute-start.15 = (bf16[1408,256]{1,0:T(8,128)(2,1)S(1)}, bf16[1408,256]{1,0:T(8,128)(2,1)S(1)}, u32[]{:S(2)}, u32[]{:S(2)}) collective-permute-start(bf16[1408,256]{1,0:T(8,128)(2,1)S(1)} %collective-permute-done.10.refs_4_), channel_id=1, source_target_pairs={{0,6},{2,0},{4,2},{6,4},{1,7},{3,1},{5,3},{7,5},{8,14},{10,8},{12,... | collective-permute-start | bytes 2162696 | tf_op jit(solution)/shard_map/ppermute | solution.py:16
  100.5 13.9 %collective-permute-start.19 = (bf16[1296,256]{1,0:T(8,128)(2,1)S(1)}, bf16[1296,256]{1,0:T(8,128)(2,1)S(1)}, u32[]{:S(2)}, u32[]{:S(2)}) collective-permute-start(bf16[1296,256]{1,0:T(8,128)(2,1)S(1)} %collective-permute-done.14.refs_15_), channel_id=1, source_target_pairs={{0,32},{32,64},{64,96},{96,0},{1,33},{33,65},{65,97},{97,1},{2,34}... | collective-permute-start | bytes 1990664 | tf_op jit(solution)/shard_map/ppermute | solution.py:16
  101.2 13.1 %collective-permute-start.18 = (bf16[1296,256]{1,0:T(8,128)(2,1)S(1)}, bf16[1296,256]{1,0:T(8,128)(2,1)S(1)}, u32[]{:S(2)}, u32[]{:S(2)}) collective-permute-start(bf16[1296,256]{1,0:T(8,128)(2,1)S(1)} %collective-permute-done.14.refs_15_), channel_id=1, source_target_pairs={{0,96},{32,0},{64,32},{96,64},{1,97},{33,1},{65,33},{97,65},{2,98}... | collective-permute-start | bytes 1990664 | tf_op jit(solution)/shard_map/ppermute | solution.py:16
  115.4 12.0 %collective-permute-start.23 = (bf16[832,256]{1,0:T(8,128)(2,1)}, bf16[832,256]{1,0:T(8,128)(2,1)}, u32[]{:S(2)}, u32[]{:S(2)}) collective-permute-start(bf16[832,256]{1,0:T(8,128)(2,1)} %slice.59), channel_id=1, source_target_pairs={{0,2},{2,4},{4,6},{6,0},{1,3},{3,5},{5,7},{7,1},{8,10},{10,12},{12... | collective-permute-start | bytes 1277960 | tf_op jit(solution)/shard_map/ppermute | solution.py:16
  118.5 8.9 %collective-permute-start.24 = (bf16[656,256]{1,0:T(8,128)(2,1)}, bf16[656,256]{1,0:T(8,128)(2,1)}, u32[]{:S(2)}, u32[]{:S(2)}) collective-permute-start(bf16[656,256]{1,0:T(8,128)(2,1)} %slice.60), channel_id=1, source_target_pairs={{0,96},{32,0},{64,32},{96,64},{1,97},{33,1},{65,33},{97,65},{2,98}... | collective-permute-start | bytes 1007624 | tf_op jit(solution)/shard_map/ppermute | solution.py:16
  119.3 8.1 %collective-permute-start.25 = (bf16[640,256]{1,0:T(8,128)(2,1)}, bf16[640,256]{1,0:T(8,128)(2,1)}, u32[]{:S(2)}, u32[]{:S(2)}) collective-permute-start(bf16[640,256]{1,0:T(8,128)(2,1)} %slice.61), channel_id=1, source_target_pairs={{0,32},{32,64},{64,96},{96,0},{1,33},{33,65},{65,97},{97,1},{2,34}... | collective-permute-start | bytes 983048 | tf_op jit(solution)/shard_map/ppermute | solution.py:16
  121.5 5.9 %collective-permute-start.22 = (bf16[576,256]{1,0:T(8,128)(2,1)}, bf16[576,256]{1,0:T(8,128)(2,1)}, u32[]{:S(2)}, u32[]{:S(2)}) collective-permute-start(bf16[576,256]{1,0:T(8,128)(2,1)} %slice.58), channel_id=1, source_target_pairs={{0,6},{2,0},{4,2},{6,4},{1,7},{3,1},{5,3},{7,5},{8,14},{10,8},{12,... | collective-permute-start | bytes 884744 | tf_op jit(solution)/shard_map/ppermute | solution.py:16
  153.6 20.9 %collective-permute-start.26 = (bf16[1152,576]{0,1:T(8,128)(2,1)S(1)}, bf16[1152,576]{0,1:T(8,128)(2,1)S(1)}, u32[]{:S(2)}, u32[]{:S(2)}) collective-permute-start(bf16[1152,576]{0,1:T(8,128)(2,1)S(1)} %copy.7), channel_id=1, source_target_pairs={{0,1},{1,0},{2,3},{3,2},{4,5},{5,4},{6,7},{7,6},{8,9},{9,8},{10,11... | collective-permute-start | bytes 3981320 | tf_op jit(solution)/shard_map/ppermute | solution.py:20
  (23 other events, 343.0 us)

commit v2 on v0

v2 whole, which is shorter than its diff:
```python
import jax
import jax.numpy as jnp
from jax import lax
from jax.experimental import pallas as pl
from jax.experimental.pallas import tpu as pltpu
from jax.sharding import Mesh, PartitionSpec as P

BLOCK = 128
F32 = jnp.float32
BF16 = jnp.bfloat16
ALL = ("z", "xh", "xl", "y", "core")
NZ, NX, NL, NY, NC = 4, 2, 2, 4, 2


def shift(x, axis, size, step):
    return lax.ppermute(x, axis, [(i, (i + step) % size) for i in range(size)])


def flip(x, axis, size, bit):
    return lax.ppermute(x, axis, [(i, i ^ bit) for i in range(size)])


def place(z, xh, xl, y, k):
    return (((z * NX + xh) * NL + xl) * NY + y) * NC + k


def turn_pairs():
    pairs = []
    for z in range(NZ):
        for xh in range(NX):
            for xl in range(NL):
                for y in range(NY):
                    turn = 2 * (z & 1) + xh
                    to = (
                        (z - y + turn) % NZ,
                        xh ^ xl ^ (z >> 1) ^ (y & 1),
                        z >> 1,
                        turn,
                    )
                    for k in range(NC):
                        pairs.append((place(z, xh, xl, y, k), place(*to, k)))
    return pairs


def first_dims(left, right):
    return lax.dot_general(
        left, right, (((0,), (0,)), ((), ())), preferred_element_type=F32
    )


def last_dims(left, right):
    return lax.dot_general(
        left, right, (((1,), (1,)), ((), ())), preferred_element_type=F32
    )


def last_dims_exact(left, right):
    return lax.dot_general(
        left,
        right,
        (((1,), (1,)), ((), ())),
        precision=lax.Precision.HIGHEST,
        preferred_element_type=F32,
    )


STEPS = 4


def head_kernel(
    index,
    coords,
    vecs_block,
    refl_block,
    eigvecs,
    reflectors,
    keep,
    send_1,
    send_2,
    send_3,
    own,
    turned,
    refl,
    sums,
    cross,
    sem,
    sem_refl,
):
    step = pl.program_id(0)
    rows, width = own.shape[0], reflectors.shape[2]
    share = turned.shape[0] - rows
    copies, copies_refl = [], []
    for i in range(rows // BLOCK):
        take = pl.ds(pl.multiple_of(index[i] * BLOCK, BLOCK), BLOCK)
        to = pl.ds(i * BLOCK, BLOCK)
        for n, out in enumerate((own, turned)):
            copies.append(
                pltpu.make_async_copy(eigvecs.at[take], out.at[to], sem.at[2 * i + n])
            )
        for n in range(2):
            copies_refl.append(
                pltpu.make_async_copy(
                    reflectors.at[n, take],
                    refl.at[to, pl.ds(n * width, width)],
                    sem_refl.at[2 * i + n],
                )
            )

    @pl.when(step == 0)
    def _():
        for copy in copies_refl + copies:
            copy.start()
        sums[...] = jnp.zeros_like(sums)
        cross[...] = jnp.zeros_like(cross)

    both = jnp.concatenate([refl_block[0], refl_block[1]], axis=1)
    sums[...] += first_dims(vecs_block[...], both)
    cross[...] += first_dims(refl_block[1], refl_block[0])

    @pl.when(step == STEPS - 1)
    def _():
        part = sums.shape[0] // NZ
        wide = jnp.concatenate([cross[:part, :], cross[part:, :]], axis=1)
        for n, out in enumerate((keep, send_1, send_2, send_3)):
            to = lax.rem(coords[0] + n, NZ)
            out[:part, :] = sums[pl.ds(pl.multiple_of(to * part, part), part), :]
            out[part:, :] = wide
        for copy in copies_refl:
            copy.wait()
        start = pl.multiple_of((coords[2] * NY + coords[3]) * share, 16)
        for copy in copies:
            copy.wait()
        turned[rows:, :] = refl[pl.ds(start, share), :]


def head(index, coords, eigvecs, reflectors):
    rows = index.shape[0] * BLOCK
    local, columns = eigvecs.shape
    width = reflectors.shape[2]
    block = local // STEPS
    smem = pl.BlockSpec(memory_space=pltpu.SMEM)
    vmem = pl.BlockSpec(memory_space=pltpu.VMEM)
    hbm = pl.BlockSpec(memory_space=pltpu.HBM)
    sums = jax.ShapeDtypeStruct((128, 256), F32)
    return pl.pallas_call(
        head_kernel,
        grid=(STEPS,),
        in_specs=[
            smem,
            smem,
            pl.BlockSpec((block, columns), lambda i: (i, 0)),
            pl.BlockSpec((2, block, width), lambda i: (0, i, 0)),
            hbm,
            hbm,
        ],
        out_specs=[vmem] * 7,
        out_shape=[sums] * 4
        + [
            jax.ShapeDtypeStruct((rows, columns), BF16),
            jax.ShapeDtypeStruct((rows + rows // 8, columns), BF16),
            jax.ShapeDtypeStruct((rows, 2 * width), BF16),
        ],
        scratch_shapes=[
            pltpu.VMEM((256, 256), F32),
            pltpu.VMEM((128, 128), F32),
            pltpu.SemaphoreType.DMA((2 * index.shape[0],)),
            pltpu.SemaphoreType.DMA((2 * index.shape[0],)),
        ],
        compiler_params=pltpu.CompilerParams(vmem_limit_bytes=20 * 2**20),
        name="head",
    )(
        index,
        coords,
        *[pltpu.with_memory_space_constraint(v, pltpu.HBM) for v in (eigvecs, reflectors)] * 2,
    )


def source_of(z, xh, xl, y, dxh, dz):
    zz = lax.rem(z + dz, NZ)
    from_y = lax.rem(2 * xl + (y >> 1) + y - zz + NZ, NZ)
    from_l = (xh + dxh + (y & 1) + xl + (from_y & 1)) & 1
    return from_y, from_l


def weigh(freqs):
    return 1.0 / jnp.tanh(freqs / 2.0) / (2.0 * freqs)


def final_kernel(slots_a, slots_b, coords, freqs, ya, *rest):
    a_refs, rest = rest[: len(slots_a)], rest[len(slots_a) :]
    b_refs, rest = rest[: len(slots_b)], rest[len(slots_b) :]
    c_other, c_own, a_all, b_all, yb, p_all = rest
    z, xh, xl, y, k = (coords[i] for i in range(5))
    rows = ya.shape[0]
    share = rows // 8

    for (slot, (first, _)), ref in zip(slots_a, a_refs):
        for dz in range(NZ):
            for dxh in range(NX):
                zz = lax.rem(z + dz, NZ)
                xx = jnp.bitwise_xor(xh, dxh)
                to = pl.multiple_of(slot * 256 + (zz * NX + xx) * 32, 32)
                chunk = first + rows + (dz * NX + dxh) * 32
                p_all[pl.ds(to, 32), :] = ref[chunk : chunk + 32, :]
    for ((dxh, dz), (first, _)), ref in zip(slots_b, b_refs):
        from_y, from_l = source_of(z, xh, xl, y, dxh, dz)
        to = pl.multiple_of((from_l * NY + from_y) * share, 16)
        yb[pl.ds(to, share), :] = ref[first + rows : first + rows + share, :]

    for ((dxh, dz), (first, _)), ref in zip(slots_b, b_refs):
        from_y, from_l = source_of(z, xh, xl, y, dxh, dz)
        dx = jnp.bitwise_xor(from_l, xl)
        slot = dx * NY + lax.rem(from_y - y + NY, NY)
        whole = (from_l * NY + from_y) * NC + k
        at = pl.multiple_of(slot * 256, 256)
        value = ref[first : first + rows, :].astype(F32) - last_dims(
            yb[...], p_all[pl.ds(at, 256), :]
        )
        value = value * weigh(
            jnp.concatenate(
                [freqs[pl.ds(2 * whole, 1), :], freqs[pl.ds(2 * whole + 1, 1), :]],
                axis=1,
            )
        )
        b_all[:, pl.ds(at, 256)] = value.astype(BF16)
    for (slot, (first, _)), ref in zip(slots_a, a_refs):
        cols = slice(slot * 256, slot * 256 + 256)
        value = ref[first : first + rows, :].astype(F32) - last_dims(
            ya[...], p_all[cols, :]
        )
        a_all[:, cols] = value.astype(BF16)
    half = c_own.shape[0]

    def product(which):
        return last_dims(
            b_all[pl.ds(pl.multiple_of(which * half, half), half), :], a_all[...]
        )

    c_other[...] = product(1 - k).astype(BF16)
    c_own[...] = product(k)


def add_kernel(own, other, out):
    rows = out.shape[0]
    at = pl.ds(pl.multiple_of(pl.program_id(0) * rows, rows), rows)
    out[...] = own[at, :] + other[at, :].astype(F32)


def final(coords, freqs, ya, a_list, b_list):
    slots_a = [(s, take) for s, take, _ in a_list]
    slots_b = [(s, take) for s, take, _ in b_list]
    smem = pl.BlockSpec(memory_space=pltpu.SMEM)
    vmem = pl.BlockSpec(memory_space=pltpu.VMEM)
    rows = ya.shape[0]
    half = rows // 2
    depth = 256 * NL * NY

    def body(*refs):
        final_kernel(slots_a, slots_b, *refs)

    other, own = pl.pallas_call(
        body,
        out_shape=[
            jax.ShapeDtypeStruct((half, rows), BF16),
            jax.ShapeDtypeStruct((half, rows), F32),
        ],
        in_specs=[smem, vmem, vmem] + [vmem] * (len(a_list) + len(b_list)),
        out_specs=[vmem, vmem],
        scratch_shapes=[
            pltpu.VMEM((rows, depth), BF16),
            pltpu.VMEM((rows, depth), BF16),
            pltpu.VMEM((rows, 256), BF16),
            pltpu.VMEM((depth, 256), BF16),
        ],
        compiler_params=pltpu.CompilerParams(vmem_limit_bytes=24 * 2**20),
        name="covariance",
    )(coords, freqs, ya, *[v for _, _, v in a_list], *[v for _, _, v in b_list])
    got = flip(other, "core", NC, 1)
    return pl.pallas_call(
        add_kernel,
        grid=(4,),
        in_specs=[vmem, vmem],
        out_specs=pl.BlockSpec((half // 4, rows), lambda i: (i, 0)),
        out_shape=jax.ShapeDtypeStruct((half, rows), F32),
        compiler_params=pltpu.CompilerParams(vmem_limit_bytes=4 * 2**20),
        name="add",
    )(own, got).T


def apply_factors(both, factors):
    part, cross = both[:32], both[32:]
    cross = jnp.concatenate([cross[:, :128], cross[:, 128:]], axis=0)
    t1, t2 = jnp.triu(factors[0]), jnp.triu(factors[1])
    second_apply = last_dims_exact(part[:, 128:], t2).astype(BF16)
    first_part = part[:, :128] - jnp.dot(
        second_apply.astype(F32), cross, precision=lax.Precision.HIGHEST
    )
    first_apply = last_dims_exact(first_part, t1).astype(BF16)
    return jnp.concatenate([first_apply, second_apply], axis=1)


def ahead(x, axis, size):
    return [x, shift(x, axis, size, -1), shift(x, axis, size, 2), shift(x, axis, size, 1)]


def per_device(eigvecs, reflectors, factors, frequencies, region_blocks):
    z, xh, xl, y, k = (lax.axis_index(a) for a in ALL)
    local_blocks = eigvecs.shape[0] // BLOCK
    index = region_blocks - (z * NX + xh) * local_blocks
    coords = jnp.stack([z, xh, xl, y, k]).astype(jnp.int32)
    keep, *sends, own, turned, refl = head(index, coords, eigvecs, reflectors)
    rows = own.shape[0]

    turned = lax.ppermute(turned, ALL, turn_pairs())
    both = keep
    for n, send in enumerate(sends):
        both = both + shift(send, "z", NZ, n + 1)
    cross = both[64:]
    half = [
        jnp.concatenate(
            [lax.dynamic_slice_in_dim(both, which * 32, 32, 0), cross], axis=0
        )
        for which in (xh, 1 - xh)
    ]
    both = half[0] + flip(half[1], "xh", NX, 1)
    p = apply_factors(both, factors)
    p = jnp.concatenate([p, flip(p, "xh", NX, 1)], axis=0)
    across = flip(own, "xl", NL, 1)
    p, turned = lax.optimization_barrier((p, turned))
    p = jnp.concatenate([p, flip(p, "xl", NL, 1)], axis=0)
    p = ahead(p, "z", NZ)

    a, b = {}, {}
    b[0] = jnp.concatenate([turned, flip(turned, "xh", NX, 1)], axis=0)
    a[0] = jnp.concatenate(
        [own] + [v[:64] for v in p] + [across] + [v[64:] for v in p], axis=0
    )
    size_a, size_b = rows + 256, turned.shape[0]
    b[1] = shift(b[0], "z", NZ, -1)
    b[3] = shift(b[0], "z", NZ, 1)
    a[1] = shift(a[0], "y", NY, -1)
    a[3] = shift(a[0], "y", NY, 1)
    b2 = [shift(b[1][:size_b], "z", NZ, -1), shift(b[3][size_b:], "z", NZ, 1)]
    a2 = [shift(a[1][:size_a], "y", NY, -1), shift(a[3][size_a:], "y", NY, 1)]

    a_list, b_list = [], []
    for n in range(2):
        a_list += [(n * NY + d, (n * size_a, size_a), v) for d, v in a.items()]
        a_list += [(n * NY + 2, (0, size_a), a2[n])]
        b_list += [((n, d), (n * size_b, size_b), v) for d, v in b.items()]
        b_list += [((n, 2), (0, size_b), b2[n])]
    return final(coords, frequencies.reshape(-1, 128), refl, a_list, b_list)


def solution(mesh):
    grid = Mesh(mesh.devices.reshape(NZ, NX, NL, NY, NC), ALL)
    row, col = ("z", "xh"), ("xl", "y", "core")
    return jax.shard_map(
        per_device,
        mesh=grid,
        in_specs=(P(row, col), P(None, row, None), P(), P(), P(row)),
        out_specs=P(row, col),
        check_vma=False,
    )
```

time: 267 us -> 137 us (0.51)
  blocking collectives: 77.2 us -> 0 us
  waiting for transfers between devices: 125 us -> 53 us
  starting transfers between devices: 12.5 us -> 62.1 us
  matrix products: 25.1 us -> 0.71 us
  Pallas kernels: 0 us -> 18.4 us
  between operations: 13.6 us -> 0.23 us
  local copies, waits for them, and re-layouts: 11.4 us -> 1.58 us
    all_gather x2 -> x0, waiting for transfers between devices: 108 us -> none  [the longest x1 74.4 us: per_device(): whole = lax.all_gather(region, 'row', axis=0, tiled=True)]
    all_to_all x1 -> x0, blocking collectives: 77.2 us -> none  [per_device(): lax.all_to_all(whole, 'col', split_axis=0, concat_axis=1, tiled=True)]
    ppermute x0 -> x21, starting transfers between devices: none -> 62.1 us  [the longest x14 31.1 us: shift(): return lax.ppermute(x, axis, [(i, (i + step) % size) for i in range(size)])]
    ppermute x0 -> x21, waiting for transfers between devices: none -> 53 us  [the longest x14 37.3 us: shift(): return lax.ppermute(x, axis, [(i, (i + step) % size) for i in range(size)])]
    dot_general x9 -> x3, matrix products: 25.1 us -> 0.71 us  [the longest x2 0.55 us: last_dims_exact(): lax.dot_general(left, right, (((1,), (1,)), ((), ())), precision=lax.Prec...]
    pallas_call x0 -> x3, Pallas kernels: none -> 18.4 us  [the longest x1 10 us: final(): pl.pallas_call(body, out_shape=[jax.ShapeDtypeStruct((half, rows), BF16),...]
    all_to_all x2 -> x0, waiting for transfers between devices: 17 us -> none  [from_everyone(): return lax.all_to_all(copies, axis, split_axis=0, concat_axis=0, tiled=True)]
    all_to_all x2 -> x0, starting transfers between devices: 12.4 us -> none  [from_everyone(): return lax.all_to_all(copies, axis, split_axis=0, concat_axis=0, tiled=True)]
  transfers between devices with their start and end apart: 4 -> 21, of which waited for: 4 -> 9; matrix products, arithmetic and copies ran while one was open for 6% -> 2% of each run, Pallas kernels for 0% -> 0%
where the time goes in v2:
time: 137 us
  starting transfers between devices  62.1 us (45%)
  waiting for transfers between devices  53 us (39%)
  Pallas kernels  18.4 us (13%)
  local copies, waits for them, and re-layouts  1.58 us (1%)
    ppermute x14, waiting for transfers between devices, shift(): return lax.ppermute(x, axis, [(i, (i + step) % size) for i in range(size)])  37.3 us
    ppermute x14, starting transfers between devices, shift(): return lax.ppermute(x, axis, [(i, (i + step) % size) for i in range(size)])  31.1 us
    ppermute x6, starting transfers between devices, flip(): return lax.ppermute(x, axis, [(i, i ^ bit) for i in range(size)])  30.3 us
    ppermute x6, waiting for transfers between devices, flip(): return lax.ppermute(x, axis, [(i, i ^ bit) for i in range(size)])  15.7 us
    pallas_call x1, Pallas kernels, final(): pl.pallas_call(body, out_shape=[jax.ShapeDtypeStruct((half, rows), BF16),...  10 us
    pallas_call x1, Pallas kernels, head(): pl.pallas_call(head_kernel, grid=(STEPS,), in_specs=[smem, smem, pl.Block...  6.35 us
  transfers between devices with their start and end apart: 21, of which 9 were waited for; matrix products, arithmetic and copies ran while one was open for 2% of the time, Pallas kernels for 0%

profile of v2, /device:TPU:1, one launch (start us, length us, event | category | flops | bytes accessed | tf_op | source)
XLA Modules:
  0.0 136.8 jit_solution(9663874083295122749)
XLA Ops:
  0.7 6.4 %head.1 = (f32[128,256]{1,0:T(8,128)S(1)}, f32[128,256]{1,0:T(8,128)S(1)}, f32[128,256]{1,0:T(8,128)S(1)}, f32[128,256]{1,0:T(8,128)S(1)}, bf16[1152,256]{1,0:T(...) custom-call(s32[9]{0:T(128)S(1)} %broadcast_subtract_fusion.index, ...), custom_call_target="tpu_custom_call" | custom-call | tf_op jit(solution)/shard_map/head/pallas_call | solution.py:145
  7.1 2.6 %collective-permute-start = (f32[128,256]{1,0:T(8,128)S(1)}, f32[128,256]{1,0:T(8,128)S(1)}, u32[]{:S(2)}, u32[]{:S(2)}) collective-permute-start(f32[128,256]{1,0:T(8,128)S(1)} %get-tuple-element.19), channel_id=1, source_target_pairs={{0,32},{32,64},{64,96},{96,0},{1,33},{33,65},{65,97},{97,1},{2,34}... | collective-permute-start | bytes 393224 | tf_op jit(solution)/shard_map/ppermute | solution.py:16
  9.7 3.3 %collective-permute-start.1 = (f32[128,256]{1,0:T(8,128)S(1)}, f32[128,256]{1,0:T(8,128)S(1)}, u32[]{:S(2)}, u32[]{:S(2)}) collective-permute-start(f32[128,256]{1,0:T(8,128)S(1)} %get-tuple-element.20), channel_id=1, source_target_pairs={{0,64},{32,96},{64,0},{96,32},{1,65},{33,97},{65,1},{97,33},{2,66}... | collective-permute-start | bytes 393224 | tf_op jit(solution)/shard_map/ppermute | solution.py:16
  13.7 1.2 collective-permute-start.10
  15.6 3.0 %collective-permute-done.1 = f32[128,256]{1,0:T(8,128)S(1)} collective-permute-done((f32[128,256]{1,0:T(8,128)S(1)}, f32[128,256]{1,0:T(8,128)S(1)}, u32[]{:S(2)}, u32[]{:S(2)}) %collective-permute-start.1) | collective-permute-done | bytes 131104 | tf_op jit(solution)/shard_map/ppermute | solution.py:16
  18.7 2.8 %collective-permute-start.3 = (f32[96,256]{1,0:T(8,128)S(1)}, f32[96,256]{1,0:T(8,128)S(1)}, u32[]{:S(2)}, u32[]{:S(2)}) collective-permute-start(f32[96,256]{1,0:T(8,128)S(1)} %pad_maximum_fusion), channel_id=1, source_target_pairs={{0,16},{16,0},{1,17},{17,1},{2,18},{18,2},{3,19},{19,3},{4,20},{20... | collective-permute-start | bytes 294920 | tf_op jit(solution)/shard_map/ppermute | solution.py:20
  21.6 9.4 %collective-permute-done.3 = f32[96,256]{1,0:T(8,128)S(1)} collective-permute-done((f32[96,256]{1,0:T(8,128)S(1)}, f32[96,256]{1,0:T(8,128)S(1)}, u32[]{:S(2)}, u32[]{:S(2)}) %collective-permute-start.3) | collective-permute-done | bytes 98336 | tf_op jit(solution)/shard_map/ppermute | solution.py:20
  32.4 3.6 %collective-permute-done.4 = bf16[32,256]{1,0:T(8,128)(2,1)S(1)} collective-permute-done((bf16[32,256]{1,0:T(8,128)(2,1)S(1)}, bf16[32,256]{1,0:T(8,128)(2,1)S(1)}, u32[]{:S(2)}, u32[]{:S(2)}) %collective-permute-start.4) | collective-permute-done | bytes 16416 | tf_op jit(solution)/shard_map/ppermute | solution.py:20
  36.1 2.7 %collective-permute-start.6 = (bf16[64,256]{1,0:T(8,128)(2,1)S(1)}, bf16[64,256]{1,0:T(8,128)(2,1)S(1)}, u32[]{:S(2)}, u32[]{:S(2)}) collective-permute-start(bf16[64,256]{1,0:T(8,128)(2,1)S(1)} %pad_maximum_fusion.2), channel_id=1, source_target_pairs={{0,8},{8,0},{1,9},{9,1},{2,10},{10,2},{3,11},{11,3},{4,12},{12,4},... | collective-permute-start | bytes 98312 | tf_op jit(solution)/shard_map/ppermute | solution.py:20
  38.8 9.3 %collective-permute-start.15 = (bf16[1296,256]{1,0:T(8,128)(2,1)S(1)}, bf16[1296,256]{1,0:T(8,128)(2,1)S(1)}, u32[]{:S(2)}, u32[]{:S(2)}) collective-permute-start(bf16[1296,256]{1,0:T(8,128)(2,1)S(1)} %collective-permute-done.5), channel_id=1, source_target_pairs={{0,16},{16,0},{1,17},{17,1},{2,18},{18,2},{3,19},{19,3},{4,20},{20... | collective-permute-start | bytes 1990664 | tf_op jit(solution)/shard_map/ppermute | solution.py:20
  48.0 7.2 %collective-permute-start.7 = (bf16[128,256]{1,0:T(8,128)(2,1)S(1)}, bf16[128,256]{1,0:T(8,128)(2,1)S(1)}, u32[]{:S(2)}, u32[]{:S(2)}) collective-permute-start(bf16[128,256]{1,0:T(8,128)(2,1)S(1)} %constant_dynamic-update-slice_fusion), channel_id=1, source_target_pairs={{0,96},{32,0},{64,32},{96,64},{1,97},{33,1},{65,33},{97,65},{2,98}... | collective-permute-start | bytes 196616 | tf_op jit(solution)/shard_map/ppermute | solution.py:16
  55.4 1.2 collective-permute-start.8
  56.6 3.8 %collective-permute-done.8 = bf16[128,256]{1,0:T(8,128)(2,1)S(1)} collective-permute-done((bf16[128,256]{1,0:T(8,128)(2,1)S(1)}, bf16[128,256]{1,0:T(8,128)(2,1)S(1)}, u32[]{:S(2)}, u32[]{:S(2)}) %collective-permute-start.8) | collective-permute-done | bytes 65568 | tf_op jit(solution)/shard_map/ppermute | solution.py:16
  61.8 5.5 %collective-permute-start.12 = (bf16[2816,256]{1,0:T(8,128)(2,1)S(1)}, bf16[2816,256]{1,0:T(8,128)(2,1)S(1)}, u32[]{:S(2)}, u32[]{:S(2)}) collective-permute-start(bf16[2816,256]{1,0:T(8,128)(2,1)S(1)} %slice_dynamic-update-slice_fusion.refs_3_.refs_7_), channel_id=1, source_target_pairs={{0,2},{2,4},{4,6},{6,0},{1,3},{3,5},{5,7},{7,1},{8,10},{10,12},{12... | collective-permute-start | bytes 4325384 | tf_op jit(solution)/shard_map/ppermute | solution.py:16
  68.4 1.2 collective-permute-start.17
  69.7 1.5 %collective-permute-start.16 = (bf16[2592,256]{1,0:T(8,128)(2,1)S(1)}, bf16[2592,256]{1,0:T(8,128)(2,1)S(1)}, u32[]{:S(2)}, u32[]{:S(2)}) collective-permute-start(bf16[2592,256]{1,0:T(8,128)(2,1)S(1)} %constant_dynamic-update-slice_fusion.6.refs_11_.refs_15_), channel_id=1, source_target_pairs={{0,96},{32,0},{64,32},{96,64},{1,97},{33,1},{65,33},{97,65},{2,98}... | collective-permute-start | bytes 3981320 | tf_op jit(solution)/shard_map/ppermute | solution.py:16
  71.2 19.5 %collective-permute-done.12.refs_5_.refs_9_ = bf16[2816,256]{1,0:T(8,128)(2,1)S(1)} collective-permute-done((bf16[2816,256]{1,0:T(8,128)(2,1)S(1)}, bf16[2816,256]{1,0:T(8,128)(2,1)S(1)}, u32[]{:S(2)}, u32[]{:S(2)}) %collective-permute-start.12) | collective-permute-done | bytes 1441824 | tf_op jit(solution)/shard_map/ppermute | solution.py:16
  90.7 2.3 %collective-permute-start.14 = (bf16[1408,256]{1,0:T(8,128)(2,1)S(1)}, bf16[1408,256]{1,0:T(8,128)(2,1)S(1)}, u32[]{:S(2)}, u32[]{:S(2)}) collective-permute-start(bf16[1408,256]{1,0:T(8,128)(2,1)S(1)} %slice.86), channel_id=1, source_target_pairs={{0,2},{2,4},{4,6},{6,0},{1,3},{3,5},{5,7},{7,1},{8,10},{10,12},{12... | collective-permute-start | bytes 2162696 | tf_op jit(solution)/shard_map/ppermute | solution.py:16
  93.6 3.7 %collective-permute-start.19 = (bf16[1296,256]{1,0:T(8,128)(2,1)S(1)}, bf16[1296,256]{1,0:T(8,128)(2,1)S(1)}, u32[]{:S(2)}, u32[]{:S(2)}) collective-permute-start(bf16[1296,256]{1,0:T(8,128)(2,1)S(1)} %slice.88), channel_id=1, source_target_pairs={{0,32},{32,64},{64,96},{96,0},{1,33},{33,65},{65,97},{97,1},{2,34}... | collective-permute-start | bytes 1990664 | tf_op jit(solution)/shard_map/ppermute | solution.py:16
  97.7 10.2 %collective-permute-done.14.refs_10_ = bf16[1408,256]{1,0:T(8,128)(2,1)S(1)} collective-permute-done((bf16[1408,256]{1,0:T(8,128)(2,1)S(1)}, bf16[1408,256]{1,0:T(8,128)(2,1)S(1)}, u32[]{:S(2)}, u32[]{:S(2)}) %collective-permute-start.14) | collective-permute-done | bytes 720928 | tf_op jit(solution)/shard_map/ppermute | solution.py:16
  108.4 10.0 %covariance.1 = (bf16[576,1152]{1,0:T(8,128)(2,1)S(1)}, f32[576,1152]{1,0:T(8,128)S(1)}) custom-call(s32[5]{0:T(128)S(1)} %stack.23.coords.refs_0_, f32[32,128]{1,0:T(8,128)S(1)} %bitcast.14, bf16[1152,256]{1,0:T(8,128)(2,1)S(1)} %get-tuple-element.16.refs_2_, bf16[2816,256]{1,0:T(8,128)(2,1)S(1)} %slice_dynamic-update-slice_fusion.refs_3_.refs_7_, ...), custom_call_target="tpu_custom_call" | custom-call | tf_op jit(solution)/shard_map/covariance/pallas_call | solution.py:261
  118.4 13.7 %collective-permute-start.20 = (bf16[576,1152]{1,0:T(8,128)(2,1)S(1)}, bf16[576,1152]{1,0:T(8,128)(2,1)S(1)}, u32[]{:S(2)}, u32[]{:S(2)}) collective-permute-start(bf16[576,1152]{1,0:T(8,128)(2,1)S(1)} %get-tuple-element.26), channel_id=1, source_target_pairs={{0,1},{1,0},{2,3},{3,2},{4,5},{5,4},{6,7},{7,6},{8,9},{9,8},{10,11... | collective-permute-start | bytes 3981320 | tf_op jit(solution)/shard_map/ppermute | solution.py:20
  132.1 2.7 %collective-permute-done.20.other = bf16[576,1152]{1,0:T(8,128)(2,1)S(1)} collective-permute-done((bf16[576,1152]{1,0:T(8,128)(2,1)S(1)}, bf16[576,1152]{1,0:T(8,128)(2,1)S(1)}, u32[]{:S(2)}, u32[]{:S(2)}) %collective-permute-start.20) | collective-permute-done | bytes 1327136 | tf_op jit(solution)/shard_map/ppermute | solution.py:20
  134.8 2.0 %add.50 = f32[576,1152]{1,0:T(8,128)} custom-call(f32[576,1152]{1,0:T(8,128)S(1)} %get-tuple-element.25.own, bf16[576,1152]{1,0:T(8,128)(2,1)S(1)} %collective-permute-done.20.other), custom_call_target="tpu_custom_call" | custom-call | tf_op jit(solution)/shard_map/add/pallas_call | solution.py:279
  (56 shorter events, 7.8 us)
Async XLA Ops:
  7.1 8.5 %collective-permute-start = (f32[128,256]{1,0:T(8,128)S(1)}, f32[128,256]{1,0:T(8,128)S(1)}, u32[]{:S(2)}, u32[]{:S(2)}) collective-permute-start(f32[128,256]{1,0:T(8,128)S(1)} %get-tuple-element.19), channel_id=1, source_target_pairs={{0,32},{32,64},{64,96},{96,0},{1,33},{33,65},{65,97},{97,1},{2,34}... | collective-permute-start | bytes 393224 | tf_op jit(solution)/shard_map/ppermute | solution.py:16
  9.7 9.0 %collective-permute-start.1 = (f32[128,256]{1,0:T(8,128)S(1)}, f32[128,256]{1,0:T(8,128)S(1)}, u32[]{:S(2)}, u32[]{:S(2)}) collective-permute-start(f32[128,256]{1,0:T(8,128)S(1)} %get-tuple-element.20), channel_id=1, source_target_pairs={{0,64},{32,96},{64,0},{96,32},{1,65},{33,97},{65,1},{97,33},{2,66}... | collective-permute-start | bytes 393224 | tf_op jit(solution)/shard_map/ppermute | solution.py:16
  12.9 5.7 %collective-permute-start.2 = (f32[128,256]{1,0:T(8,128)S(1)}, f32[128,256]{1,0:T(8,128)S(1)}, u32[]{:S(2)}, u32[]{:S(2)}) collective-permute-start(f32[128,256]{1,0:T(8,128)S(1)} %get-tuple-element.21), channel_id=1, source_target_pairs={{0,96},{32,0},{64,32},{96,64},{1,97},{33,1},{65,33},{97,65},{2,98}... | collective-permute-start | bytes 393224 | tf_op jit(solution)/shard_map/ppermute | solution.py:16
  13.7 47.0 %collective-permute-start.10 = (bf16[1152,256]{1,0:T(8,128)(2,1)S(1)}, bf16[1152,256]{1,0:T(8,128)(2,1)}, u32[]{:S(2)}, u32[]{:S(2)}) collective-permute-start(bf16[1152,256]{1,0:T(8,128)(2,1)S(1)} %get-tuple-element.17), channel_id=1, source_target_pairs={{0,8},{8,0},{1,9},{9,1},{2,10},{10,2},{3,11},{11,3},{4,12},{12,4},... | collective-permute-start | bytes 1769480 | tf_op jit(solution)/shard_map/ppermute | solution.py:20
  14.9 21.2 %collective-permute-start.5 = (bf16[1296,256]{1,0:T(8,128)(2,1)S(1)}, bf16[1296,256]{1,0:T(8,128)(2,1)S(1)}, u32[]{:S(2)}, u32[]{:S(2)}) collective-permute-start(bf16[1296,256]{1,0:T(8,128)(2,1)S(1)} %get-tuple-element.22), channel_id=1, source_target_pairs={{0,0},{1,1},{2,112},{3,113},{4,64},{5,65},{6,48},{7,49},{8,16},{9,... | collective-permute-start | bytes 1990664 | tf_op jit(solution)/shard_map/ppermute | solution.py:314
  15.6 15.4 %copy-start.1 = (f32[2,128,128]{2,1,0:T(8,128)S(1)}, f32[2,128,128]{2,1,0:T(8,128)}, u32[]{:S(2)}) copy-start(f32[2,128,128]{2,1,0:T(8,128)} %param.7) | copy-start | bytes 393220
  18.7 12.2 %collective-permute-start.3 = (f32[96,256]{1,0:T(8,128)S(1)}, f32[96,256]{1,0:T(8,128)S(1)}, u32[]{:S(2)}, u32[]{:S(2)}) collective-permute-start(f32[96,256]{1,0:T(8,128)S(1)} %pad_maximum_fusion), channel_id=1, source_target_pairs={{0,16},{16,0},{1,17},{17,1},{2,18},{18,2},{3,19},{19,3},{4,20},{20... | collective-permute-start | bytes 294920 | tf_op jit(solution)/shard_map/ppermute | solution.py:20
  31.8 4.3 %collective-permute-start.4 = (bf16[32,256]{1,0:T(8,128)(2,1)S(1)}, bf16[32,256]{1,0:T(8,128)(2,1)S(1)}, u32[]{:S(2)}, u32[]{:S(2)}) collective-permute-start(bf16[32,256]{1,0:T(8,128)(2,1)S(1)} %pad_maximum_fusion.3), channel_id=1, source_target_pairs={{0,16},{16,0},{1,17},{17,1},{2,18},{18,2},{3,19},{19,3},{4,20},{20... | collective-permute-start | bytes 49160 | tf_op jit(solution)/shard_map/ppermute | solution.py:20
  36.1 11.9 %collective-permute-start.6 = (bf16[64,256]{1,0:T(8,128)(2,1)S(1)}, bf16[64,256]{1,0:T(8,128)(2,1)S(1)}, u32[]{:S(2)}, u32[]{:S(2)}) collective-permute-start(bf16[64,256]{1,0:T(8,128)(2,1)S(1)} %pad_maximum_fusion.2), channel_id=1, source_target_pairs={{0,8},{8,0},{1,9},{9,1},{2,10},{10,2},{3,11},{11,3},{4,12},{12,4},... | collective-permute-start | bytes 98312 | tf_op jit(solution)/shard_map/ppermute | solution.py:20
  38.8 29.6 %collective-permute-start.15 = (bf16[1296,256]{1,0:T(8,128)(2,1)S(1)}, bf16[1296,256]{1,0:T(8,128)(2,1)S(1)}, u32[]{:S(2)}, u32[]{:S(2)}) collective-permute-start(bf16[1296,256]{1,0:T(8,128)(2,1)S(1)} %collective-permute-done.5), channel_id=1, source_target_pairs={{0,16},{16,0},{1,17},{17,1},{2,18},{18,2},{3,19},{19,3},{4,20},{20... | collective-permute-start | bytes 1990664 | tf_op jit(solution)/shard_map/ppermute | solution.py:20
  48.0 8.5 %collective-permute-start.7 = (bf16[128,256]{1,0:T(8,128)(2,1)S(1)}, bf16[128,256]{1,0:T(8,128)(2,1)S(1)}, u32[]{:S(2)}, u32[]{:S(2)}) collective-permute-start(bf16[128,256]{1,0:T(8,128)(2,1)S(1)} %constant_dynamic-update-slice_fusion), channel_id=1, source_target_pairs={{0,96},{32,0},{64,32},{96,64},{1,97},{33,1},{65,33},{97,65},{2,98}... | collective-permute-start | bytes 196616 | tf_op jit(solution)/shard_map/ppermute | solution.py:16
  55.3 5.4 %collective-permute-start.9 = (bf16[128,256]{1,0:T(8,128)(2,1)S(1)}, bf16[128,256]{1,0:T(8,128)(2,1)S(1)}, u32[]{:S(2)}, u32[]{:S(2)}) collective-permute-start(bf16[128,256]{1,0:T(8,128)(2,1)S(1)} %constant_dynamic-update-slice_fusion), channel_id=1, source_target_pairs={{0,32},{32,64},{64,96},{96,0},{1,33},{33,65},{65,97},{97,1},{2,34}... | collective-permute-start | bytes 196616 | tf_op jit(solution)/shard_map/ppermute | solution.py:16
  55.4 5.0 %collective-permute-start.8 = (bf16[128,256]{1,0:T(8,128)(2,1)S(1)}, bf16[128,256]{1,0:T(8,128)(2,1)S(1)}, u32[]{:S(2)}, u32[]{:S(2)}) collective-permute-start(bf16[128,256]{1,0:T(8,128)(2,1)S(1)} %constant_dynamic-update-slice_fusion), channel_id=1, source_target_pairs={{0,64},{32,96},{64,0},{96,32},{1,65},{33,97},{65,1},{97,33},{2,66}... | collective-permute-start | bytes 196616 | tf_op jit(solution)/shard_map/ppermute | solution.py:16
  61.8 28.8 %collective-permute-start.12 = (bf16[2816,256]{1,0:T(8,128)(2,1)S(1)}, bf16[2816,256]{1,0:T(8,128)(2,1)S(1)}, u32[]{:S(2)}, u32[]{:S(2)}) collective-permute-start(bf16[2816,256]{1,0:T(8,128)(2,1)S(1)} %slice_dynamic-update-slice_fusion.refs_3_.refs_7_), channel_id=1, source_target_pairs={{0,2},{2,4},{4,6},{6,0},{1,3},{3,5},{5,7},{7,1},{8,10},{10,12},{12... | collective-permute-start | bytes 4325384 | tf_op jit(solution)/shard_map/ppermute | solution.py:16
  67.3 25.7 %collective-permute-start.11 = (bf16[2816,256]{1,0:T(8,128)(2,1)S(1)}, bf16[2816,256]{1,0:T(8,128)(2,1)S(1)}, u32[]{:S(2)}, u32[]{:S(2)}) collective-permute-start(bf16[2816,256]{1,0:T(8,128)(2,1)S(1)} %slice_dynamic-update-slice_fusion.refs_3_.refs_7_), channel_id=1, source_target_pairs={{0,6},{2,0},{4,2},{6,4},{1,7},{3,1},{5,3},{7,5},{8,14},{10,8},{12,... | collective-permute-start | bytes 4325384 | tf_op jit(solution)/shard_map/ppermute | solution.py:16
  68.4 25.2 %collective-permute-start.17 = (bf16[2592,256]{1,0:T(8,128)(2,1)S(1)}, bf16[2592,256]{1,0:T(8,128)(2,1)S(1)}, u32[]{:S(2)}, u32[]{:S(2)}) collective-permute-start(bf16[2592,256]{1,0:T(8,128)(2,1)S(1)} %constant_dynamic-update-slice_fusion.6.refs_11_.refs_15_), channel_id=1, source_target_pairs={{0,32},{32,64},{64,96},{96,0},{1,33},{33,65},{65,97},{97,1},{2,34}... | collective-permute-start | bytes 3981320 | tf_op jit(solution)/shard_map/ppermute | solution.py:16
  69.7 27.7 %collective-permute-start.16 = (bf16[2592,256]{1,0:T(8,128)(2,1)S(1)}, bf16[2592,256]{1,0:T(8,128)(2,1)S(1)}, u32[]{:S(2)}, u32[]{:S(2)}) collective-permute-start(bf16[2592,256]{1,0:T(8,128)(2,1)S(1)} %constant_dynamic-update-slice_fusion.6.refs_11_.refs_15_), channel_id=1, source_target_pairs={{0,96},{32,0},{64,32},{96,64},{1,97},{33,1},{65,33},{97,65},{2,98}... | collective-permute-start | bytes 3981320 | tf_op jit(solution)/shard_map/ppermute | solution.py:16
  90.7 17.2 %collective-permute-start.14 = (bf16[1408,256]{1,0:T(8,128)(2,1)S(1)}, bf16[1408,256]{1,0:T(8,128)(2,1)S(1)}, u32[]{:S(2)}, u32[]{:S(2)}) collective-permute-start(bf16[1408,256]{1,0:T(8,128)(2,1)S(1)} %slice.86), channel_id=1, source_target_pairs={{0,2},{2,4},{4,6},{6,0},{1,3},{3,5},{5,7},{7,1},{8,10},{10,12},{12... | collective-permute-start | bytes 2162696 | tf_op jit(solution)/shard_map/ppermute | solution.py:16
  93.0 15.3 %copy-start = (f32[4096]{0:T(1024)S(1)}, f32[4096]{0:T(1024)}, u32[]{:S(2)}) copy-start(f32[4096]{0:T(1024)} %param.8) | copy-start | bytes 49156
  93.0 15.3 %collective-permute-start.13 = (bf16[1408,256]{1,0:T(8,128)(2,1)S(1)}, bf16[1408,256]{1,0:T(8,128)(2,1)S(1)}, u32[]{:S(2)}, u32[]{:S(2)}) collective-permute-start(bf16[1408,256]{1,0:T(8,128)(2,1)S(1)} %slice.85), channel_id=1, source_target_pairs={{0,6},{2,0},{4,2},{6,4},{1,7},{3,1},{5,3},{7,5},{8,14},{10,8},{12,... | collective-permute-start | bytes 2162696 | tf_op jit(solution)/shard_map/ppermute | solution.py:16
  93.6 14.7 %collective-permute-start.19 = (bf16[1296,256]{1,0:T(8,128)(2,1)S(1)}, bf16[1296,256]{1,0:T(8,128)(2,1)S(1)}, u32[]{:S(2)}, u32[]{:S(2)}) collective-permute-start(bf16[1296,256]{1,0:T(8,128)(2,1)S(1)} %slice.88), channel_id=1, source_target_pairs={{0,32},{32,64},{64,96},{96,0},{1,33},{33,65},{65,97},{97,1},{2,34}... | collective-permute-start | bytes 1990664 | tf_op jit(solution)/shard_map/ppermute | solution.py:16
  97.4 10.9 %collective-permute-start.18 = (bf16[1296,256]{1,0:T(8,128)(2,1)S(1)}, bf16[1296,256]{1,0:T(8,128)(2,1)S(1)}, u32[]{:S(2)}, u32[]{:S(2)}) collective-permute-start(bf16[1296,256]{1,0:T(8,128)(2,1)S(1)} %slice.87), channel_id=1, source_target_pairs={{0,96},{32,0},{64,32},{96,64},{1,97},{33,1},{65,33},{97,65},{2,98}... | collective-permute-start | bytes 1990664 | tf_op jit(solution)/shard_map/ppermute | solution.py:16
  118.4 16.4 %collective-permute-start.20 = (bf16[576,1152]{1,0:T(8,128)(2,1)S(1)}, bf16[576,1152]{1,0:T(8,128)(2,1)S(1)}, u32[]{:S(2)}, u32[]{:S(2)}) collective-permute-start(bf16[576,1152]{1,0:T(8,128)(2,1)S(1)} %get-tuple-element.26), channel_id=1, source_target_pairs={{0,1},{1,0},{2,3},{3,2},{4,5},{5,4},{6,7},{7,6},{8,9},{9,8},{10,11... | collective-permute-start | bytes 3981320 | tf_op jit(solution)/shard_map/ppermute | solution.py:20

commit v3 on v2

--- a/solution.py
+++ b/solution.py
@@ -187,6 +187,7 @@
 
 
 def final_kernel(slots_a, slots_b, coords, freqs, ya, *rest):
+    p_refs, rest = rest[:NY], rest[NY:]
     a_refs, rest = rest[: len(slots_a)], rest[len(slots_a) :]
     b_refs, rest = rest[: len(slots_b)], rest[len(slots_b) :]
     c_other, c_own, a_all, b_all, yb, p_all = rest
@@ -194,14 +195,16 @@
     rows = ya.shape[0]
     share = rows // 8
 
-    for (slot, (first, _)), ref in zip(slots_a, a_refs):
-        for dz in range(NZ):
+    for dy, p_ref in enumerate(p_refs):
+        for dx in range(NL):
             for dxh in range(NX):
-                zz = lax.rem(z + dz, NZ)
-                xx = jnp.bitwise_xor(xh, dxh)
-                to = pl.multiple_of(slot * 256 + (zz * NX + xx) * 32, 32)
-                chunk = first + rows + (dz * NX + dxh) * 32
-                p_all[pl.ds(to, 32), :] = ref[chunk : chunk + 32, :]
+                for dz in range(NZ):
+                    zz = lax.rem(z + dz, NZ)
+                    xx = jnp.bitwise_xor(xh, dxh)
+                    slot = dx * NY + dy
+                    to = pl.multiple_of(slot * 256 + (zz * NX + xx) * 32, 32)
+                    chunk = ((dx * NX + dxh) * NZ + dz) * 32
+                    p_all[pl.ds(to, 32), :] = p_ref[chunk : chunk + 32, :]
     for ((dxh, dz), (first, _)), ref in zip(slots_b, b_refs):
         from_y, from_l = source_of(z, xh, xl, y, dxh, dz)
         to = pl.multiple_of((from_l * NY + from_y) * share, 16)
@@ -246,7 +249,7 @@
     out[...] = own[at, :] + other[at, :].astype(F32)
 
 
-def final(coords, freqs, ya, a_list, b_list):
+def final(coords, freqs, ya, p_list, a_list, b_list):
     slots_a = [(s, take) for s, take, _ in a_list]
     slots_b = [(s, take) for s, take, _ in b_list]
     smem = pl.BlockSpec(memory_space=pltpu.SMEM)
@@ -264,7 +267,7 @@
             jax.ShapeDtypeStruct((half, rows), BF16),
             jax.ShapeDtypeStruct((half, rows), F32),
         ],
-        in_specs=[smem, vmem, vmem] + [vmem] * (len(a_list) + len(b_list)),
+        in_specs=[smem] + [vmem] * (2 + NY + len(a_list) + len(b_list)),
         out_specs=[vmem, vmem],
         scratch_shapes=[
             pltpu.VMEM((rows, depth), BF16),
@@ -274,7 +277,7 @@
         ],
         compiler_params=pltpu.CompilerParams(vmem_limit_bytes=24 * 2**20),
         name="covariance",
-    )(coords, freqs, ya, *[v for _, _, v in a_list], *[v for _, _, v in b_list])
+    )(coords, freqs, ya, *p_list, *[v for _, _, v in a_list], *[v for _, _, v in b_list])
     got = flip(other, "core", NC, 1)
     return pl.pallas_call(
         add_kernel,
@@ -311,10 +314,13 @@
     keep, *sends, own, turned, refl = head(index, coords, eigvecs, reflectors)
     rows = own.shape[0]
 
-    turned = lax.ppermute(turned, ALL, turn_pairs())
+    together = lax.optimization_barrier
     both = keep
     for n, send in enumerate(sends):
         both = both + shift(send, "z", NZ, n + 1)
+    turned = lax.ppermute(turned, ALL, turn_pairs())
+    across = flip(own, "xl", NL, 1)
+
     cross = both[64:]
     half = [
         jnp.concatenate(
@@ -323,25 +329,27 @@
         for which in (xh, 1 - xh)
     ]
     both = half[0] + flip(half[1], "xh", NX, 1)
+
+    a, b = {}, {}
+    a[0] = jnp.concatenate([own, across], axis=0)
+    both, turned, a[0] = together((both, turned, a[0]))
+    b[0] = jnp.concatenate([turned, flip(turned, "xh", NX, 1)], axis=0)
+    a[1] = shift(a[0], "y", NY, -1)
+    a[3] = shift(a[0], "y", NY, 1)
     p = apply_factors(both, factors)
-    p = jnp.concatenate([p, flip(p, "xh", NX, 1)], axis=0)
-    across = flip(own, "xl", NL, 1)
-    p, turned = lax.optimization_barrier((p, turned))
-    p = jnp.concatenate([p, flip(p, "xl", NL, 1)], axis=0)
-    p = ahead(p, "z", NZ)
-
-    a, b = {}, {}
-    b[0] = jnp.concatenate([turned, flip(turned, "xh", NX, 1)], axis=0)
-    a[0] = jnp.concatenate(
-        [own] + [v[:64] for v in p] + [across] + [v[64:] for v in p], axis=0
-    )
-    size_a, size_b = rows + 256, turned.shape[0]
+    p = jnp.concatenate(ahead(p, "z", NZ), axis=0)
+
+    p, b[0] = together((p, b[0]))
+    size_a, size_b = rows, turned.shape[0]
     b[1] = shift(b[0], "z", NZ, -1)
     b[3] = shift(b[0], "z", NZ, 1)
-    a[1] = shift(a[0], "y", NY, -1)
-    a[3] = shift(a[0], "y", NY, 1)
+    p, a[1], a[3] = together((p, a[1], a[3]))
+    p = jnp.concatenate([p, flip(p, "xh", NX, 1)], axis=0)
+    p = jnp.concatenate([p, flip(p, "xl", NL, 1)], axis=0)
+    p_list = ahead(p, "y", NY)
+    a[1], a[3], *p_list = together((a[1], a[3], *p_list))
+    a2 = [shift(a[1][:size_a], "y", NY, -1), shift(a[3][size_a:], "y", NY, 1)]
     b2 = [shift(b[1][:size_b], "z", NZ, -1), shift(b[3][size_b:], "z", NZ, 1)]
-    a2 = [shift(a[1][:size_a], "y", NY, -1), shift(a[3][size_a:], "y", NY, 1)]
 
     a_list, b_list = [], []
     for n in range(2):
@@ -349,7 +357,7 @@
         a_list += [(n * NY + 2, (0, size_a), a2[n])]
         b_list += [((n, d), (n * size_b, size_b), v) for d, v in b.items()]
         b_list += [((n, 2), (0, size_b), b2[n])]
-    return final(coords, frequencies.reshape(-1, 128), refl, a_list, b_list)
+    return final(coords, frequencies.reshape(-1, 128), refl, p_list, a_list, b_list)
 
 
 def solution(mesh):

time: 137 us -> 132 us (0.964)
  waiting for transfers between devices: 53 us -> 49.9 us
  starting transfers between devices: 62.1 us -> 59.8 us
    ppermute x6, starting transfers between devices: 30.3 us -> 13.3 us  [flip(): return lax.ppermute(x, axis, [(i, i ^ bit) for i in range(size)])]
    ppermute x14 -> x17, starting transfers between devices: 31.1 us -> 45.8 us  [shift(): return lax.ppermute(x, axis, [(i, (i + step) % size) for i in range(size)])]
    ppermute x14 -> x17, waiting for transfers between devices: 37.3 us -> 24.4 us  [shift(): return lax.ppermute(x, axis, [(i, (i + step) % size) for i in range(size)])]
    ppermute x6, waiting for transfers between devices: 15.7 us -> 25.5 us  [flip(): return lax.ppermute(x, axis, [(i, i ^ bit) for i in range(size)])]
  transfers between devices with their start and end apart: 21 -> 24, of which waited for: 9 -> 12; matrix products, arithmetic and copies ran while one was open for 2% -> 2% of each run, Pallas kernels for 0% -> 0%
where the time goes in v3:
time: 132 us; the launch traced here: 131 us
  starting transfers between devices  59.8 us (45%)
  waiting for transfers between devices  49.9 us (38%)
  Pallas kernels  18.4 us (14%)
  other arithmetic  2.03 us (2%)
    ppermute x17, starting transfers between devices, shift(): return lax.ppermute(x, axis, [(i, (i + step) % size) for i in range(size)])  45.8 us
    ppermute x6, waiting for transfers between devices, flip(): return lax.ppermute(x, axis, [(i, i ^ bit) for i in range(size)])  25.5 us
    ppermute x17, waiting for transfers between devices, shift(): return lax.ppermute(x, axis, [(i, (i + step) % size) for i in range(size)])  24.4 us
    ppermute x6, starting transfers between devices, flip(): return lax.ppermute(x, axis, [(i, i ^ bit) for i in range(size)])  13.3 us
    pallas_call x1, Pallas kernels, final(): pl.pallas_call(body, out_shape=[jax.ShapeDtypeStruct((half, rows), BF16),...  10 us
    pallas_call x1, Pallas kernels, head(): pl.pallas_call(head_kernel, grid=(STEPS,), in_specs=[smem, smem, pl.Block...  6.35 us
  transfers between devices with their start and end apart: 24, of which 12 were waited for; matrix products, arithmetic and copies ran while one was open for 2% of the time, Pallas kernels for 0%

profile of v3, /device:TPU:1, one launch (start us, length us, event | category | flops | bytes accessed | tf_op | source)
XLA Modules:
  0.0 131.4 jit_solution(15395361950291732411)
XLA Ops:
  0.7 6.4 %head.1 = (f32[128,256]{1,0:T(8,128)S(1)}, f32[128,256]{1,0:T(8,128)S(1)}, f32[128,256]{1,0:T(8,128)S(1)}, f32[128,256]{1,0:T(8,128)S(1)}, bf16[1152,256]{1,0:T(...) custom-call(s32[9]{0:T(128)S(1)} %broadcast_subtract_fusion.index, ...), custom_call_target="tpu_custom_call" | custom-call | tf_op jit(solution)/shard_map/head/pallas_call | solution.py:145
  7.1 2.6 %collective-permute-start = (f32[128,256]{1,0:T(8,128)S(1)}, f32[128,256]{1,0:T(8,128)S(1)}, u32[]{:S(2)}, u32[]{:S(2)}) collective-permute-start(f32[128,256]{1,0:T(8,128)S(1)} %get-tuple-element.30), channel_id=1, source_target_pairs={{0,32},{32,64},{64,96},{96,0},{1,33},{33,65},{65,97},{97,1},{2,34}... | collective-permute-start | bytes 393224 | tf_op jit(solution)/shard_map/ppermute | solution.py:16
  9.7 3.3 %collective-permute-start.1 = (f32[128,256]{1,0:T(8,128)S(1)}, f32[128,256]{1,0:T(8,128)S(1)}, u32[]{:S(2)}, u32[]{:S(2)}) collective-permute-start(f32[128,256]{1,0:T(8,128)S(1)} %get-tuple-element.31), channel_id=1, source_target_pairs={{0,64},{32,96},{64,0},{96,32},{1,65},{33,97},{65,1},{97,33},{2,66}... | collective-permute-start | bytes 393224 | tf_op jit(solution)/shard_map/ppermute | solution.py:16
  15.6 3.0 %collective-permute-done.1 = f32[128,256]{1,0:T(8,128)S(1)} collective-permute-done((f32[128,256]{1,0:T(8,128)S(1)}, f32[128,256]{1,0:T(8,128)S(1)}, u32[]{:S(2)}, u32[]{:S(2)}) %collective-permute-start.1) | collective-permute-done | bytes 131104 | tf_op jit(solution)/shard_map/ppermute | solution.py:16
  18.7 2.8 %collective-permute-start.3 = (f32[96,256]{1,0:T(8,128)S(1)}, f32[96,256]{1,0:T(8,128)S(1)}, u32[]{:S(2)}, u32[]{:S(2)}) collective-permute-start(f32[96,256]{1,0:T(8,128)S(1)} %pad_maximum_fusion.3), channel_id=1, source_target_pairs={{0,16},{16,0},{1,17},{17,1},{2,18},{18,2},{3,19},{19,3},{4,20},{20... | collective-permute-start | bytes 294920 | tf_op jit(solution)/shard_map/ppermute | solution.py:20
  21.6 9.4 %collective-permute-done.3 = f32[96,256]{1,0:T(8,128)S(1)} collective-permute-done((f32[96,256]{1,0:T(8,128)S(1)}, f32[96,256]{1,0:T(8,128)S(1)}, u32[]{:S(2)}, u32[]{:S(2)}) %collective-permute-start.3) | collective-permute-done | bytes 98336 | tf_op jit(solution)/shard_map/ppermute | solution.py:20
  32.2 15.9 %collective-permute-start.11 = (bf16[2304,256]{1,0:T(8,128)(2,1)S(1)}, bf16[2304,256]{1,0:T(8,128)(2,1)S(1)}, u32[]{:S(2)}, u32[]{:S(2)}) collective-permute-start(bf16[2304,256]{1,0:T(8,128)(2,1)S(1)} %pad_maximum_fusion.1.refs_7_.refs_11_), channel_id=1, source_target_pairs={{0,2},{2,4},{4,6},{6,0},{1,3},{3,5},{5,7},{7,1},{8,10},{10,12},{12... | collective-permute-start | bytes 3538952 | tf_op jit(solution)/shard_map/ppermute | solution.py:16
  48.1 5.4 %collective-permute-start.10 = (bf16[2304,256]{1,0:T(8,128)(2,1)S(1)}, bf16[2304,256]{1,0:T(8,128)(2,1)S(1)}, u32[]{:S(2)}, u32[]{:S(2)}) collective-permute-start(bf16[2304,256]{1,0:T(8,128)(2,1)S(1)} %pad_maximum_fusion.1.refs_7_.refs_11_), channel_id=1, source_target_pairs={{0,6},{2,0},{4,2},{6,4},{1,7},{3,1},{5,3},{7,5},{8,14},{10,8},{12,... | collective-permute-start | bytes 3538952 | tf_op jit(solution)/shard_map/ppermute | solution.py:16
  55.4 2.0 %collective-permute-start.8 = (bf16[32,256]{1,0:T(8,128)(2,1)S(1)}, bf16[32,256]{1,0:T(8,128)(2,1)S(1)}, u32[]{:S(2)}, u32[]{:S(2)}) collective-permute-start(bf16[32,256]{1,0:T(8,128)(2,1)S(1)} %pad_maximum_fusion.6), channel_id=1, source_target_pairs={{0,32},{32,64},{64,96},{96,0},{1,33},{33,65},{65,97},{97,1},{2,34}... | collective-permute-start | bytes 49160 | tf_op jit(solution)/shard_map/ppermute | solution.py:16
  57.4 2.2 %collective-permute-start.7 = (bf16[32,256]{1,0:T(8,128)(2,1)S(1)}, bf16[32,256]{1,0:T(8,128)(2,1)S(1)}, u32[]{:S(2)}, u32[]{:S(2)}) collective-permute-start(bf16[32,256]{1,0:T(8,128)(2,1)S(1)} %pad_maximum_fusion.6), channel_id=1, source_target_pairs={{0,64},{32,96},{64,0},{96,32},{1,65},{33,97},{65,1},{97,33},{2,66}... | collective-permute-start | bytes 49160 | tf_op jit(solution)/shard_map/ppermute | solution.py:16
  62.8 5.6 %collective-permute-done.9 = bf16[1296,256]{1,0:T(8,128)(2,1)S(1)} collective-permute-done((bf16[1296,256]{1,0:T(8,128)(2,1)S(1)}, bf16[1296,256]{1,0:T(8,128)(2,1)S(1)}, u32[]{:S(2)}, u32[]{:S(2)}) %collective-permute-start.9) | collective-permute-done | bytes 663584 | tf_op jit(solution)/shard_map/ppermute | solution.py:20
  69.6 1.6 %collective-permute-start.19 = (bf16[2592,256]{1,0:T(8,128)(2,1)S(1)}, bf16[2592,256]{1,0:T(8,128)(2,1)S(1)}, u32[]{:S(2)}, u32[]{:S(2)}) collective-permute-start(bf16[2592,256]{1,0:T(8,128)(2,1)S(1)} %pad_maximum_fusion.refs_15_.refs_19_), channel_id=1, source_target_pairs={{0,96},{32,0},{64,32},{96,64},{1,97},{33,1},{65,33},{97,65},{2,98}... | collective-permute-start | bytes 3981320 | tf_op jit(solution)/shard_map/ppermute | solution.py:16
  71.3 5.7 %collective-permute-done.11.refs_9_.refs_13_ = bf16[2304,256]{1,0:T(8,128)(2,1)S(1)} collective-permute-done((bf16[2304,256]{1,0:T(8,128)(2,1)S(1)}, bf16[2304,256]{1,0:T(8,128)(2,1)S(1)}, u32[]{:S(2)}, u32[]{:S(2)}) %collective-permute-start.11) | collective-permute-done | bytes 1179680 | tf_op jit(solution)/shard_map/ppermute | solution.py:16
  78.3 3.3 %collective-permute-done.12 = bf16[128,256]{1,0:T(8,128)(2,1)S(1)} collective-permute-done((bf16[128,256]{1,0:T(8,128)(2,1)S(1)}, bf16[128,256]{1,0:T(8,128)(2,1)S(1)}, u32[]{:S(2)}, u32[]{:S(2)}) %collective-permute-start.12) | collective-permute-done | bytes 65568 | tf_op jit(solution)/shard_map/ppermute | solution.py:20
  81.8 4.4 %collective-permute-done.13 = bf16[256,256]{1,0:T(8,128)(2,1)S(1)} collective-permute-done((bf16[256,256]{1,0:T(8,128)(2,1)S(1)}, bf16[256,256]{1,0:T(8,128)(2,1)S(1)}, u32[]{:S(2)}, u32[]{:S(2)}) %collective-permute-start.13) | collective-permute-done | bytes 131104 | tf_op jit(solution)/shard_map/ppermute | solution.py:20
  87.2 2.4 %collective-permute-start.15 = (bf16[512,256]{1,0:T(8,128)(2,1)S(1)}, bf16[512,256]{1,0:T(8,128)(2,1)S(1)}, u32[]{:S(2)}, u32[]{:S(2)}) collective-permute-start(bf16[512,256]{1,0:T(8,128)(2,1)S(1)} %constant_dynamic-update-slice_fusion.refs_3_), channel_id=1, source_target_pairs={{0,4},{2,6},{4,0},{6,2},{1,5},{3,7},{5,1},{7,3},{8,12},{10,14},{12... | collective-permute-start | bytes 786440 | tf_op jit(solution)/shard_map/ppermute | solution.py:16
  90.1 6.4 %collective-permute-done.20.refs_17_.refs_21_ = bf16[2592,256]{1,0:T(8,128)(2,1)S(1)} collective-permute-done((bf16[2592,256]{1,0:T(8,128)(2,1)S(1)}, bf16[2592,256]{1,0:T(8,128)(2,1)S(1)}, u32[]{:S(2)}, u32[]{:S(2)}) %collective-permute-start.20) | collective-permute-done | bytes 1327136 | tf_op jit(solution)/shard_map/ppermute | solution.py:16
  96.7 2.7 %collective-permute-start.21 = (bf16[1296,256]{1,0:T(8,128)(2,1)S(1)}, bf16[1296,256]{1,0:T(8,128)(2,1)S(1)}, u32[]{:S(2)}, u32[]{:S(2)}) collective-permute-start(bf16[1296,256]{1,0:T(8,128)(2,1)S(1)} %slice.51), channel_id=1, source_target_pairs={{0,96},{32,0},{64,32},{96,64},{1,97},{33,1},{65,33},{97,65},{2,98}... | collective-permute-start | bytes 1990664 | tf_op jit(solution)/shard_map/ppermute | solution.py:16
  99.6 2.7 %collective-permute-start.17 = (bf16[1152,256]{1,0:T(8,128)(2,1)S(1)}, bf16[1152,256]{1,0:T(8,128)(2,1)S(1)}, u32[]{:S(2)}, u32[]{:S(2)}) collective-permute-start(bf16[1152,256]{1,0:T(8,128)(2,1)S(1)} %slice.46), channel_id=1, source_target_pairs={{0,6},{2,0},{4,2},{6,4},{1,7},{3,1},{5,3},{7,5},{8,14},{10,8},{12,... | collective-permute-start | bytes 1769480 | tf_op jit(solution)/shard_map/ppermute | solution.py:16
  102.3 7.6 %collective-permute-done.18.refs_14_ = bf16[1152,256]{1,0:T(8,128)(2,1)S(1)} collective-permute-done((bf16[1152,256]{1,0:T(8,128)(2,1)S(1)}, bf16[1152,256]{1,0:T(8,128)(2,1)S(1)}, u32[]{:S(2)}, u32[]{:S(2)}) %collective-permute-start.18) | collective-permute-done | bytes 589856 | tf_op jit(solution)/shard_map/ppermute | solution.py:16
  109.9 10.0 %covariance.1 = (bf16[576,1152]{1,0:T(8,128)(2,1)S(1)}, f32[576,1152]{1,0:T(8,128)S(1)}) custom-call(s32[5]{0:T(128)S(1)} %stack.23.coords.refs_0_, f32[32,128]{1,0:T(8,128)S(1)} %bitcast.14, bf16[1152,256]{1,0:T(8,128)(2,1)S(1)} %get-tuple-element.28.refs_2_, bf16[512,256]{1,0:T(8,128)(2,1)S(1)} %constant_dynamic-update-slice_fusion.refs_3_, ...), custom_call_target="tpu_custom_call" | custom-call | tf_op jit(solution)/shard_map/covariance/pallas_call | solution.py:264
  119.9 6.8 %collective-permute-start.23 = (bf16[576,1152]{1,0:T(8,128)(2,1)S(1)}, bf16[576,1152]{1,0:T(8,128)(2,1)S(1)}, u32[]{:S(2)}, u32[]{:S(2)}) collective-permute-start(bf16[576,1152]{1,0:T(8,128)(2,1)S(1)} %get-tuple-element.50), channel_id=1, source_target_pairs={{0,1},{1,0},{2,3},{3,2},{4,5},{5,4},{6,7},{7,6},{8,9},{9,8},{10,11... | collective-permute-start | bytes 3981320 | tf_op jit(solution)/shard_map/ppermute | solution.py:20
  126.7 2.7 %collective-permute-done.23.other = bf16[576,1152]{1,0:T(8,128)(2,1)S(1)} collective-permute-done((bf16[576,1152]{1,0:T(8,128)(2,1)S(1)}, bf16[576,1152]{1,0:T(8,128)(2,1)S(1)}, u32[]{:S(2)}, u32[]{:S(2)}) %collective-permute-start.23) | collective-permute-done | bytes 1327136 | tf_op jit(solution)/shard_map/ppermute | solution.py:20
  129.4 2.0 %add.50 = f32[576,1152]{1,0:T(8,128)} custom-call(f32[576,1152]{1,0:T(8,128)S(1)} %get-tuple-element.49.own, bf16[576,1152]{1,0:T(8,128)(2,1)S(1)} %collective-permute-done.23.other), custom_call_target="tpu_custom_call" | custom-call | tf_op jit(solution)/shard_map/add/pallas_call | solution.py:282
  (55 shorter events, 14.2 us)
Async XLA Ops:
  7.1 8.5 %collective-permute-start = (f32[128,256]{1,0:T(8,128)S(1)}, f32[128,256]{1,0:T(8,128)S(1)}, u32[]{:S(2)}, u32[]{:S(2)}) collective-permute-start(f32[128,256]{1,0:T(8,128)S(1)} %get-tuple-element.30), channel_id=1, source_target_pairs={{0,32},{32,64},{64,96},{96,0},{1,33},{33,65},{65,97},{97,1},{2,34}... | collective-permute-start | bytes 393224 | tf_op jit(solution)/shard_map/ppermute | solution.py:16
  9.7 9.0 %collective-permute-start.1 = (f32[128,256]{1,0:T(8,128)S(1)}, f32[128,256]{1,0:T(8,128)S(1)}, u32[]{:S(2)}, u32[]{:S(2)}) collective-permute-start(f32[128,256]{1,0:T(8,128)S(1)} %get-tuple-element.31), channel_id=1, source_target_pairs={{0,64},{32,96},{64,0},{96,32},{1,65},{33,97},{65,1},{97,33},{2,66}... | collective-permute-start | bytes 393224 | tf_op jit(solution)/shard_map/ppermute | solution.py:16
  12.9 5.7 %collective-permute-start.2 = (f32[128,256]{1,0:T(8,128)S(1)}, f32[128,256]{1,0:T(8,128)S(1)}, u32[]{:S(2)}, u32[]{:S(2)}) collective-permute-start(f32[128,256]{1,0:T(8,128)S(1)} %get-tuple-element.32), channel_id=1, source_target_pairs={{0,96},{32,0},{64,32},{96,64},{1,97},{33,1},{65,33},{97,65},{2,98}... | collective-permute-start | bytes 393224 | tf_op jit(solution)/shard_map/ppermute | solution.py:16
  13.7 17.3 %collective-permute-start.5 = (bf16[1152,256]{1,0:T(8,128)(2,1)S(1)}, bf16[1152,256]{1,0:T(8,128)(2,1)}, u32[]{:S(2)}, u32[]{:S(2)}) collective-permute-start(bf16[1152,256]{1,0:T(8,128)(2,1)S(1)} %get-tuple-element.34), channel_id=1, source_target_pairs={{0,8},{8,0},{1,9},{9,1},{2,10},{10,2},{3,11},{11,3},{4,12},{12,4},... | collective-permute-start | bytes 1769480 | tf_op jit(solution)/shard_map/ppermute | solution.py:20
  14.9 17.3 %collective-permute-start.4 = (bf16[1296,256]{1,0:T(8,128)(2,1)S(1)}, bf16[1296,256]{1,0:T(8,128)(2,1)S(1)}, u32[]{:S(2)}, u32[]{:S(2)}) collective-permute-start(bf16[1296,256]{1,0:T(8,128)(2,1)S(1)} %get-tuple-element.33), channel_id=1, source_target_pairs={{0,0},{1,1},{2,112},{3,113},{4,64},{5,65},{6,48},{7,49},{8,16},{9,... | collective-permute-start | bytes 1990664 | tf_op jit(solution)/shard_map/ppermute | solution.py:321
  18.7 12.3 %collective-permute-start.3 = (f32[96,256]{1,0:T(8,128)S(1)}, f32[96,256]{1,0:T(8,128)S(1)}, u32[]{:S(2)}, u32[]{:S(2)}) collective-permute-start(f32[96,256]{1,0:T(8,128)S(1)} %pad_maximum_fusion.3), channel_id=1, source_target_pairs={{0,16},{16,0},{1,17},{17,1},{2,18},{18,2},{3,19},{19,3},{4,20},{20... | collective-permute-start | bytes 294920 | tf_op jit(solution)/shard_map/ppermute | solution.py:20
  32.2 44.8 %collective-permute-start.11 = (bf16[2304,256]{1,0:T(8,128)(2,1)S(1)}, bf16[2304,256]{1,0:T(8,128)(2,1)S(1)}, u32[]{:S(2)}, u32[]{:S(2)}) collective-permute-start(bf16[2304,256]{1,0:T(8,128)(2,1)S(1)} %pad_maximum_fusion.1.refs_7_.refs_11_), channel_id=1, source_target_pairs={{0,2},{2,4},{4,6},{6,0},{1,3},{3,5},{5,7},{7,1},{8,10},{10,12},{12... | collective-permute-start | bytes 3538952 | tf_op jit(solution)/shard_map/ppermute | solution.py:16
  48.1 28.9 %collective-permute-start.10 = (bf16[2304,256]{1,0:T(8,128)(2,1)S(1)}, bf16[2304,256]{1,0:T(8,128)(2,1)S(1)}, u32[]{:S(2)}, u32[]{:S(2)}) collective-permute-start(bf16[2304,256]{1,0:T(8,128)(2,1)S(1)} %pad_maximum_fusion.1.refs_7_.refs_11_), channel_id=1, source_target_pairs={{0,6},{2,0},{4,2},{6,4},{1,7},{3,1},{5,3},{7,5},{8,14},{10,8},{12,... | collective-permute-start | bytes 3538952 | tf_op jit(solution)/shard_map/ppermute | solution.py:16
  53.5 14.9 %collective-permute-start.9 = (bf16[1296,256]{1,0:T(8,128)(2,1)S(1)}, bf16[1296,256]{1,0:T(8,128)(2,1)S(1)}, u32[]{:S(2)}, u32[]{:S(2)}) collective-permute-start(bf16[1296,256]{1,0:T(8,128)(2,1)S(1)} %collective-permute-done.4), channel_id=1, source_target_pairs={{0,16},{16,0},{1,17},{17,1},{2,18},{18,2},{3,19},{19,3},{4,20},{20... | collective-permute-start | bytes 1990664 | tf_op jit(solution)/shard_map/ppermute | solution.py:20
  55.4 4.5 %collective-permute-start.8 = (bf16[32,256]{1,0:T(8,128)(2,1)S(1)}, bf16[32,256]{1,0:T(8,128)(2,1)S(1)}, u32[]{:S(2)}, u32[]{:S(2)}) collective-permute-start(bf16[32,256]{1,0:T(8,128)(2,1)S(1)} %pad_maximum_fusion.6), channel_id=1, source_target_pairs={{0,32},{32,64},{64,96},{96,0},{1,33},{33,65},{65,97},{97,1},{2,34}... | collective-permute-start | bytes 49160 | tf_op jit(solution)/shard_map/ppermute | solution.py:16
  57.4 4.4 %collective-permute-start.7 = (bf16[32,256]{1,0:T(8,128)(2,1)S(1)}, bf16[32,256]{1,0:T(8,128)(2,1)S(1)}, u32[]{:S(2)}, u32[]{:S(2)}) collective-permute-start(bf16[32,256]{1,0:T(8,128)(2,1)S(1)} %pad_maximum_fusion.6), channel_id=1, source_target_pairs={{0,64},{32,96},{64,0},{96,32},{1,65},{33,97},{65,1},{97,33},{2,66}... | collective-permute-start | bytes 49160 | tf_op jit(solution)/shard_map/ppermute | solution.py:16
  59.9 2.9 %collective-permute-start.6 = (bf16[32,256]{1,0:T(8,128)(2,1)S(1)}, bf16[32,256]{1,0:T(8,128)(2,1)S(1)}, u32[]{:S(2)}, u32[]{:S(2)}) collective-permute-start(bf16[32,256]{1,0:T(8,128)(2,1)S(1)} %pad_maximum_fusion.6), channel_id=1, source_target_pairs={{0,96},{32,0},{64,32},{96,64},{1,97},{33,1},{65,33},{97,65},{2,98}... | collective-permute-start | bytes 49160 | tf_op jit(solution)/shard_map/ppermute | solution.py:16
  68.5 28.0 %collective-permute-start.20 = (bf16[2592,256]{1,0:T(8,128)(2,1)S(1)}, bf16[2592,256]{1,0:T(8,128)(2,1)S(1)}, u32[]{:S(2)}, u32[]{:S(2)}) collective-permute-start(bf16[2592,256]{1,0:T(8,128)(2,1)S(1)} %pad_maximum_fusion.refs_15_.refs_19_), channel_id=1, source_target_pairs={{0,32},{32,64},{64,96},{96,0},{1,33},{33,65},{65,97},{97,1},{2,34}... | collective-permute-start | bytes 3981320 | tf_op jit(solution)/shard_map/ppermute | solution.py:16
  69.6 27.0 %collective-permute-start.19 = (bf16[2592,256]{1,0:T(8,128)(2,1)S(1)}, bf16[2592,256]{1,0:T(8,128)(2,1)S(1)}, u32[]{:S(2)}, u32[]{:S(2)}) collective-permute-start(bf16[2592,256]{1,0:T(8,128)(2,1)S(1)} %pad_maximum_fusion.refs_15_.refs_19_), channel_id=1, source_target_pairs={{0,96},{32,0},{64,32},{96,64},{1,97},{33,1},{65,33},{97,65},{2,98}... | collective-permute-start | bytes 3981320 | tf_op jit(solution)/shard_map/ppermute | solution.py:16
  77.0 4.6 %collective-permute-start.12 = (bf16[128,256]{1,0:T(8,128)(2,1)S(1)}, bf16[128,256]{1,0:T(8,128)(2,1)S(1)}, u32[]{:S(2)}, u32[]{:S(2)}) collective-permute-start(bf16[128,256]{1,0:T(8,128)(2,1)S(1)} %pad_maximum_fusion.5), channel_id=1, source_target_pairs={{0,16},{16,0},{1,17},{17,1},{2,18},{18,2},{3,19},{19,3},{4,20},{20... | collective-permute-start | bytes 196616 | tf_op jit(solution)/shard_map/ppermute | solution.py:20
  81.6 4.5 %collective-permute-start.13 = (bf16[256,256]{1,0:T(8,128)(2,1)S(1)}, bf16[256,256]{1,0:T(8,128)(2,1)S(1)}, u32[]{:S(2)}, u32[]{:S(2)}) collective-permute-start(bf16[256,256]{1,0:T(8,128)(2,1)S(1)} %pad_maximum_fusion.2), channel_id=1, source_target_pairs={{0,8},{8,0},{1,9},{9,1},{2,10},{10,2},{3,11},{11,3},{4,12},{12,4},... | collective-permute-start | bytes 393224 | tf_op jit(solution)/shard_map/ppermute | solution.py:20
  86.2 13.2 %collective-permute-start.16 = (bf16[512,256]{1,0:T(8,128)(2,1)S(1)}, bf16[512,256]{1,0:T(8,128)(2,1)S(1)}, u32[]{:S(2)}, u32[]{:S(2)}) collective-permute-start(bf16[512,256]{1,0:T(8,128)(2,1)S(1)} %constant_dynamic-update-slice_fusion.refs_3_), channel_id=1, source_target_pairs={{0,2},{2,4},{4,6},{6,0},{1,3},{3,5},{5,7},{7,1},{8,10},{10,12},{12... | collective-permute-start | bytes 786440 | tf_op jit(solution)/shard_map/ppermute | solution.py:16
  87.2 12.2 %collective-permute-start.15 = (bf16[512,256]{1,0:T(8,128)(2,1)S(1)}, bf16[512,256]{1,0:T(8,128)(2,1)S(1)}, u32[]{:S(2)}, u32[]{:S(2)}) collective-permute-start(bf16[512,256]{1,0:T(8,128)(2,1)S(1)} %constant_dynamic-update-slice_fusion.refs_3_), channel_id=1, source_target_pairs={{0,4},{2,6},{4,0},{6,2},{1,5},{3,7},{5,1},{7,3},{8,12},{10,14},{12... | collective-permute-start | bytes 786440 | tf_op jit(solution)/shard_map/ppermute | solution.py:16
  89.6 9.9 %collective-permute-start.14 = (bf16[512,256]{1,0:T(8,128)(2,1)S(1)}, bf16[512,256]{1,0:T(8,128)(2,1)S(1)}, u32[]{:S(2)}, u32[]{:S(2)}) collective-permute-start(bf16[512,256]{1,0:T(8,128)(2,1)S(1)} %constant_dynamic-update-slice_fusion.refs_3_), channel_id=1, source_target_pairs={{0,6},{2,0},{4,2},{6,4},{1,7},{3,1},{5,3},{7,5},{8,14},{10,8},{12,... | collective-permute-start | bytes 786440 | tf_op jit(solution)/shard_map/ppermute | solution.py:16
  96.5 13.3 %collective-permute-start.22 = (bf16[1296,256]{1,0:T(8,128)(2,1)S(1)}, bf16[1296,256]{1,0:T(8,128)(2,1)S(1)}, u32[]{:S(2)}, u32[]{:S(2)}) collective-permute-start(bf16[1296,256]{1,0:T(8,128)(2,1)S(1)} %slice.52), channel_id=1, source_target_pairs={{0,32},{32,64},{64,96},{96,0},{1,33},{33,65},{65,97},{97,1},{2,34}... | collective-permute-start | bytes 1990664 | tf_op jit(solution)/shard_map/ppermute | solution.py:16
  96.7 13.2 %collective-permute-start.21 = (bf16[1296,256]{1,0:T(8,128)(2,1)S(1)}, bf16[1296,256]{1,0:T(8,128)(2,1)S(1)}, u32[]{:S(2)}, u32[]{:S(2)}) collective-permute-start(bf16[1296,256]{1,0:T(8,128)(2,1)S(1)} %slice.51), channel_id=1, source_target_pairs={{0,96},{32,0},{64,32},{96,64},{1,97},{33,1},{65,33},{97,65},{2,98}... | collective-permute-start | bytes 1990664 | tf_op jit(solution)/shard_map/ppermute | solution.py:16
  99.5 10.3 %collective-permute-start.18 = (bf16[1152,256]{1,0:T(8,128)(2,1)S(1)}, bf16[1152,256]{1,0:T(8,128)(2,1)S(1)}, u32[]{:S(2)}, u32[]{:S(2)}) collective-permute-start(bf16[1152,256]{1,0:T(8,128)(2,1)S(1)} %slice.47), channel_id=1, source_target_pairs={{0,2},{2,4},{4,6},{6,0},{1,3},{3,5},{5,7},{7,1},{8,10},{10,12},{12... | collective-permute-start | bytes 1769480 | tf_op jit(solution)/shard_map/ppermute | solution.py:16
  99.6 10.3 %collective-permute-start.17 = (bf16[1152,256]{1,0:T(8,128)(2,1)S(1)}, bf16[1152,256]{1,0:T(8,128)(2,1)S(1)}, u32[]{:S(2)}, u32[]{:S(2)}) collective-permute-start(bf16[1152,256]{1,0:T(8,128)(2,1)S(1)} %slice.46), channel_id=1, source_target_pairs={{0,6},{2,0},{4,2},{6,4},{1,7},{3,1},{5,3},{7,5},{8,14},{10,8},{12,... | collective-permute-start | bytes 1769480 | tf_op jit(solution)/shard_map/ppermute | solution.py:16
  119.9 9.4 %collective-permute-start.23 = (bf16[576,1152]{1,0:T(8,128)(2,1)S(1)}, bf16[576,1152]{1,0:T(8,128)(2,1)S(1)}, u32[]{:S(2)}, u32[]{:S(2)}) collective-permute-start(bf16[576,1152]{1,0:T(8,128)(2,1)S(1)} %get-tuple-element.50), channel_id=1, source_target_pairs={{0,1},{1,0},{2,3},{3,2},{4,5},{5,4},{6,7},{7,6},{8,9},{9,8},{10,11... | collective-permute-start | bytes 3981320 | tf_op jit(solution)/shard_map/ppermute | solution.py:20
  (2 other events, 36.8 us)

commit v4 on v3

--- a/solution.py
+++ b/solution.py
@@ -186,15 +186,20 @@
     return 1.0 / jnp.tanh(freqs / 2.0) / (2.0 * freqs)
 
 
-def final_kernel(slots_a, slots_b, coords, freqs, ya, *rest):
+def back(slots_a, a_refs, ya, p_all, a_all):
+    rows = ya.shape[0]
+    for (slot, (first, _)), ref in zip(slots_a, a_refs):
+        cols = slice(slot * 256, slot * 256 + 256)
+        value = ref[first : first + rows, :].astype(F32) - last_dims(
+            ya[...], p_all[cols, :]
+        )
+        a_all[:, cols] = value.astype(BF16)
+
+
+def early_kernel(slots_a, coords, ya, *rest):
     p_refs, rest = rest[:NY], rest[NY:]
-    a_refs, rest = rest[: len(slots_a)], rest[len(slots_a) :]
-    b_refs, rest = rest[: len(slots_b)], rest[len(slots_b) :]
-    c_other, c_own, a_all, b_all, yb, p_all = rest
-    z, xh, xl, y, k = (coords[i] for i in range(5))
-    rows = ya.shape[0]
-    share = rows // 8
-
+    a_refs, (a_all, p_all) = rest[: len(slots_a)], rest[len(slots_a) :]
+    z, xh = coords[0], coords[1]
     for dy, p_ref in enumerate(p_refs):
         for dx in range(NL):
             for dxh in range(NX):
@@ -205,6 +210,17 @@
                     to = pl.multiple_of(slot * 256 + (zz * NX + xx) * 32, 32)
                     chunk = ((dx * NX + dxh) * NZ + dz) * 32
                     p_all[pl.ds(to, 32), :] = p_ref[chunk : chunk + 32, :]
+    back(slots_a, a_refs, ya, p_all, a_all)
+
+
+def final_kernel(slots_a, slots_b, coords, freqs, ya, p_all, a_early, *rest):
+    a_refs, rest = rest[: len(slots_a)], rest[len(slots_a) :]
+    b_refs, rest = rest[: len(slots_b)], rest[len(slots_b) :]
+    c_other, a_all, b_all, yb = rest
+    z, xh, xl, y, k = (coords[i] for i in range(5))
+    rows = ya.shape[0]
+    share = rows // 8
+
     for ((dxh, dz), (first, _)), ref in zip(slots_b, b_refs):
         from_y, from_l = source_of(z, xh, xl, y, dxh, dz)
         to = pl.multiple_of((from_l * NY + from_y) * share, 16)
@@ -226,21 +242,16 @@
             )
         )
         b_all[:, pl.ds(at, 256)] = value.astype(BF16)
-    for (slot, (first, _)), ref in zip(slots_a, a_refs):
-        cols = slice(slot * 256, slot * 256 + 256)
-        value = ref[first : first + rows, :].astype(F32) - last_dims(
-            ya[...], p_all[cols, :]
-        )
-        a_all[:, cols] = value.astype(BF16)
+    back(slots_a, a_refs, ya, p_all, a_all)
+    half = c_other.shape[0]
+    which = pl.ds(pl.multiple_of((1 - k) * half, half), half)
+    c_other[...] = last_dims(b_all[which, :], a_all[...]).astype(BF16)
+
+
+def own_kernel(coords, a_all, b_all, c_own):
     half = c_own.shape[0]
-
-    def product(which):
-        return last_dims(
-            b_all[pl.ds(pl.multiple_of(which * half, half), half), :], a_all[...]
-        )
-
-    c_other[...] = product(1 - k).astype(BF16)
-    c_own[...] = product(k)
+    which = pl.ds(pl.multiple_of(coords[4] * half, half), half)
+    c_own[...] = last_dims(b_all[which, :], a_all[...])
 
 
 def add_kernel(own, other, out):
@@ -249,35 +260,58 @@
     out[...] = own[at, :] + other[at, :].astype(F32)
 
 
-def final(coords, freqs, ya, p_list, a_list, b_list):
+def final(coords, freqs, ya, p_list, a_list, a_late, b_list):
     slots_a = [(s, take) for s, take, _ in a_list]
+    slots_late = [(s, take) for s, take, _ in a_late]
     slots_b = [(s, take) for s, take, _ in b_list]
     smem = pl.BlockSpec(memory_space=pltpu.SMEM)
     vmem = pl.BlockSpec(memory_space=pltpu.VMEM)
     rows = ya.shape[0]
     half = rows // 2
     depth = 256 * NL * NY
+    whole = jax.ShapeDtypeStruct((rows, depth), BF16)
+
+    def early(*refs):
+        early_kernel(slots_a, *refs)
+
+    a_early, p_all = pl.pallas_call(
+        early,
+        out_shape=[whole, jax.ShapeDtypeStruct((depth, 256), BF16)],
+        in_specs=[smem] + [vmem] * (1 + NY + len(a_list)),
+        out_specs=[vmem, vmem],
+        compiler_params=pltpu.CompilerParams(vmem_limit_bytes=8 * 2**20),
+        name="early",
+    )(coords, ya, *p_list, *[v for _, _, v in a_list])
 
     def body(*refs):
-        final_kernel(slots_a, slots_b, *refs)
-
-    other, own = pl.pallas_call(
+        final_kernel(slots_late, slots_b, *refs)
+
+    other, a_all, b_all = pl.pallas_call(
         body,
-        out_shape=[
-            jax.ShapeDtypeStruct((half, rows), BF16),
-            jax.ShapeDtypeStruct((half, rows), F32),
-        ],
-        in_specs=[smem] + [vmem] * (2 + NY + len(a_list) + len(b_list)),
-        out_specs=[vmem, vmem],
-        scratch_shapes=[
-            pltpu.VMEM((rows, depth), BF16),
-            pltpu.VMEM((rows, depth), BF16),
-            pltpu.VMEM((rows, 256), BF16),
-            pltpu.VMEM((depth, 256), BF16),
-        ],
-        compiler_params=pltpu.CompilerParams(vmem_limit_bytes=24 * 2**20),
-        name="covariance",
-    )(coords, freqs, ya, *p_list, *[v for _, _, v in a_list], *[v for _, _, v in b_list])
+        out_shape=[jax.ShapeDtypeStruct((half, rows), BF16), whole, whole],
+        in_specs=[smem] + [vmem] * (4 + len(a_late) + len(b_list)),
+        out_specs=[vmem] * 3,
+        scratch_shapes=[pltpu.VMEM((rows, 256), BF16)],
+        input_output_aliases={4: 1},
+        compiler_params=pltpu.CompilerParams(vmem_limit_bytes=12 * 2**20),
+        name="other_half",
+    )(
+        coords,
+        freqs,
+        ya,
+        p_all,
+        a_early,
+        *[v for _, _, v in a_late],
+        *[v for _, _, v in b_list],
+    )
+    own = pl.pallas_call(
+        own_kernel,
+        out_shape=jax.ShapeDtypeStruct((half, rows), F32),
+        in_specs=[smem, vmem, vmem],
+        out_specs=vmem,
+        compiler_params=pltpu.CompilerParams(vmem_limit_bytes=8 * 2**20),
+        name="own_half",
+    )(coords, a_all, b_all)
     got = flip(other, "core", NC, 1)
     return pl.pallas_call(
         add_kernel,
@@ -351,13 +385,13 @@
     a2 = [shift(a[1][:size_a], "y", NY, -1), shift(a[3][size_a:], "y", NY, 1)]
     b2 = [shift(b[1][:size_b], "z", NZ, -1), shift(b[3][size_b:], "z", NZ, 1)]
 
-    a_list, b_list = [], []
+    a_list, a_late, b_list = [], [], []
     for n in range(2):
         a_list += [(n * NY + d, (n * size_a, size_a), v) for d, v in a.items()]
-        a_list += [(n * NY + 2, (0, size_a), a2[n])]
+        a_late += [(n * NY + 2, (0, size_a), a2[n])]
         b_list += [((n, d), (n * size_b, size_b), v) for d, v in b.items()]
         b_list += [((n, 2), (0, size_b), b2[n])]
-    return final(coords, frequencies.reshape(-1, 128), refl, p_list, a_list, b_list)
+    return final(coords, frequencies.reshape(-1, 128), refl, p_list, a_list, a_late, b_list)
 
 
 def solution(mesh):

time: 132 us -> 130 us (0.985)
  waiting for transfers between devices: 49.9 us -> 45.4 us
  Pallas kernels: 18.4 us -> 20.6 us
    pallas_call x0 -> x2, Pallas kernels: none -> 5.53 us  [the longest x1 3.79 us: final(): pl.pallas_call(own_kernel, out_shape=jax.ShapeDtypeStruct((half, rows), F...]
    pallas_call x1, Pallas kernels: 10 us -> 6.7 us  [final(): pl.pallas_call(body, out_shape=[jax.ShapeDtypeStruct((half, rows), BF16),...]
    ppermute x6, waiting for transfers between devices: 25.5 us -> 22.7 us  [flip(): return lax.ppermute(x, axis, [(i, i ^ bit) for i in range(size)])]
    ppermute x17, waiting for transfers between devices: 24.4 us -> 22.7 us  [shift(): return lax.ppermute(x, axis, [(i, (i + step) % size) for i in range(size)])]
  transfers between devices with their start and end apart: 24 -> 24, of which waited for: 12 -> 11; matrix products, arithmetic and copies ran while one was open for 2% -> 2% of each run, Pallas kernels for 0% -> 4%
where the time goes in v4:
time: 130 us; the launch traced here: 129 us
  starting transfers between devices  59.8 us (46%)
  waiting for transfers between devices  45.4 us (35%)
  Pallas kernels  20.6 us (16%)
  other arithmetic  2.03 us (2%)
    ppermute x17, starting transfers between devices, shift(): return lax.ppermute(x, axis, [(i, (i + step) % size) for i in range(size)])  45.8 us
    ppermute x6, waiting for transfers between devices, flip(): return lax.ppermute(x, axis, [(i, i ^ bit) for i in range(size)])  22.7 us
    ppermute x17, waiting for transfers between devices, shift(): return lax.ppermute(x, axis, [(i, (i + step) % size) for i in range(size)])  22.7 us
    ppermute x6, starting transfers between devices, flip(): return lax.ppermute(x, axis, [(i, i ^ bit) for i in range(size)])  13.3 us
    pallas_call x1, Pallas kernels, final(): pl.pallas_call(body, out_shape=[jax.ShapeDtypeStruct((half, rows), BF16),...  6.7 us
    pallas_call x1, Pallas kernels, head(): pl.pallas_call(head_kernel, grid=(STEPS,), in_specs=[smem, smem, pl.Block...  6.36 us
    pallas_call x1, Pallas kernels, final(): pl.pallas_call(own_kernel, out_shape=jax.ShapeDtypeStruct((half, rows), F...  3.79 us
  transfers between devices with their start and end apart: 24, of which 11 were waited for; matrix products, arithmetic and copies ran while one was open for 2% of the time, Pallas kernels for 4%

profile of v4, /device:TPU:1, one launch (start us, length us, event | category | flops | bytes accessed | tf_op | source)
XLA Modules:
  0.0 129.2 jit_solution(2287679972057124484)
XLA Ops:
  0.7 6.4 %head.1 = (f32[128,256]{1,0:T(8,128)S(1)}, f32[128,256]{1,0:T(8,128)S(1)}, f32[128,256]{1,0:T(8,128)S(1)}, f32[128,256]{1,0:T(8,128)S(1)}, bf16[1152,256]{1,0:T(...) custom-call(s32[9]{0:T(128)S(1)} %broadcast_subtract_fusion.index, ...), custom_call_target="tpu_custom_call" | custom-call | tf_op jit(solution)/shard_map/head/pallas_call | solution.py:145
  7.1 2.5 %collective-permute-start = (f32[128,256]{1,0:T(8,128)S(1)}, f32[128,256]{1,0:T(8,128)S(1)}, u32[]{:S(2)}, u32[]{:S(2)}) collective-permute-start(f32[128,256]{1,0:T(8,128)S(1)} %get-tuple-element.33), channel_id=1, source_target_pairs={{0,32},{32,64},{64,96},{96,0},{1,33},{33,65},{65,97},{97,1},{2,34}... | collective-permute-start | bytes 393224 | tf_op jit(solution)/shard_map/ppermute | solution.py:16
  9.7 3.3 %collective-permute-start.1 = (f32[128,256]{1,0:T(8,128)S(1)}, f32[128,256]{1,0:T(8,128)S(1)}, u32[]{:S(2)}, u32[]{:S(2)}) collective-permute-start(f32[128,256]{1,0:T(8,128)S(1)} %get-tuple-element.34), channel_id=1, source_target_pairs={{0,64},{32,96},{64,0},{96,32},{1,65},{33,97},{65,1},{97,33},{2,66}... | collective-permute-start | bytes 393224 | tf_op jit(solution)/shard_map/ppermute | solution.py:16
  15.6 3.1 %collective-permute-done.1 = f32[128,256]{1,0:T(8,128)S(1)} collective-permute-done((f32[128,256]{1,0:T(8,128)S(1)}, f32[128,256]{1,0:T(8,128)S(1)}, u32[]{:S(2)}, u32[]{:S(2)}) %collective-permute-start.1) | collective-permute-done | bytes 131104 | tf_op jit(solution)/shard_map/ppermute | solution.py:16
  18.8 2.8 %collective-permute-start.3 = (f32[96,256]{1,0:T(8,128)S(1)}, f32[96,256]{1,0:T(8,128)S(1)}, u32[]{:S(2)}, u32[]{:S(2)}) collective-permute-start(f32[96,256]{1,0:T(8,128)S(1)} %pad_maximum_fusion.3), channel_id=1, source_target_pairs={{0,16},{16,0},{1,17},{17,1},{2,18},{18,2},{3,19},{19,3},{4,20},{20... | collective-permute-start | bytes 294920 | tf_op jit(solution)/shard_map/ppermute | solution.py:20
  21.6 9.4 %collective-permute-done.3 = f32[96,256]{1,0:T(8,128)S(1)} collective-permute-done((f32[96,256]{1,0:T(8,128)S(1)}, f32[96,256]{1,0:T(8,128)S(1)}, u32[]{:S(2)}, u32[]{:S(2)}) %collective-permute-start.3) | collective-permute-done | bytes 98336 | tf_op jit(solution)/shard_map/ppermute | solution.py:20
  32.2 15.9 %collective-permute-start.11 = (bf16[2304,256]{1,0:T(8,128)(2,1)S(1)}, bf16[2304,256]{1,0:T(8,128)(2,1)S(1)}, u32[]{:S(2)}, u32[]{:S(2)}) collective-permute-start(bf16[2304,256]{1,0:T(8,128)(2,1)S(1)} %pad_maximum_fusion.1.refs_6_.refs_9_), channel_id=1, source_target_pairs={{0,2},{2,4},{4,6},{6,0},{1,3},{3,5},{5,7},{7,1},{8,10},{10,12},{12... | collective-permute-start | bytes 3538952 | tf_op jit(solution)/shard_map/ppermute | solution.py:16
  48.1 5.4 %collective-permute-start.10 = (bf16[2304,256]{1,0:T(8,128)(2,1)S(1)}, bf16[2304,256]{1,0:T(8,128)(2,1)S(1)}, u32[]{:S(2)}, u32[]{:S(2)}) collective-permute-start(bf16[2304,256]{1,0:T(8,128)(2,1)S(1)} %pad_maximum_fusion.1.refs_6_.refs_9_), channel_id=1, source_target_pairs={{0,6},{2,0},{4,2},{6,4},{1,7},{3,1},{5,3},{7,5},{8,14},{10,8},{12,... | collective-permute-start | bytes 3538952 | tf_op jit(solution)/shard_map/ppermute | solution.py:16
  55.4 2.0 %collective-permute-start.8 = (bf16[32,256]{1,0:T(8,128)(2,1)S(1)}, bf16[32,256]{1,0:T(8,128)(2,1)S(1)}, u32[]{:S(2)}, u32[]{:S(2)}) collective-permute-start(bf16[32,256]{1,0:T(8,128)(2,1)S(1)} %pad_maximum_fusion.6), channel_id=1, source_target_pairs={{0,32},{32,64},{64,96},{96,0},{1,33},{33,65},{65,97},{97,1},{2,34}... | collective-permute-start | bytes 49160 | tf_op jit(solution)/shard_map/ppermute | solution.py:16
  57.4 2.2 %collective-permute-start.7 = (bf16[32,256]{1,0:T(8,128)(2,1)S(1)}, bf16[32,256]{1,0:T(8,128)(2,1)S(1)}, u32[]{:S(2)}, u32[]{:S(2)}) collective-permute-start(bf16[32,256]{1,0:T(8,128)(2,1)S(1)} %pad_maximum_fusion.6), channel_id=1, source_target_pairs={{0,64},{32,96},{64,0},{96,32},{1,65},{33,97},{65,1},{97,33},{2,66}... | collective-permute-start | bytes 49160 | tf_op jit(solution)/shard_map/ppermute | solution.py:16
  62.8 5.6 %collective-permute-done.9 = bf16[1296,256]{1,0:T(8,128)(2,1)S(1)} collective-permute-done((bf16[1296,256]{1,0:T(8,128)(2,1)S(1)}, bf16[1296,256]{1,0:T(8,128)(2,1)S(1)}, u32[]{:S(2)}, u32[]{:S(2)}) %collective-permute-start.9) | collective-permute-done | bytes 663584 | tf_op jit(solution)/shard_map/ppermute | solution.py:20
  71.3 5.7 %collective-permute-done.11.refs_8_.refs_11_ = bf16[2304,256]{1,0:T(8,128)(2,1)S(1)} collective-permute-done((bf16[2304,256]{1,0:T(8,128)(2,1)S(1)}, bf16[2304,256]{1,0:T(8,128)(2,1)S(1)}, u32[]{:S(2)}, u32[]{:S(2)}) %collective-permute-start.11) | collective-permute-done | bytes 1179680 | tf_op jit(solution)/shard_map/ppermute | solution.py:16
  78.4 3.3 %collective-permute-done.12 = bf16[128,256]{1,0:T(8,128)(2,1)S(1)} collective-permute-done((bf16[128,256]{1,0:T(8,128)(2,1)S(1)}, bf16[128,256]{1,0:T(8,128)(2,1)S(1)}, u32[]{:S(2)}, u32[]{:S(2)}) %collective-permute-start.12) | collective-permute-done | bytes 65568 | tf_op jit(solution)/shard_map/ppermute | solution.py:20
  81.8 4.4 %collective-permute-done.13 = bf16[256,256]{1,0:T(8,128)(2,1)S(1)} collective-permute-done((bf16[256,256]{1,0:T(8,128)(2,1)S(1)}, bf16[256,256]{1,0:T(8,128)(2,1)S(1)}, u32[]{:S(2)}, u32[]{:S(2)}) %collective-permute-start.13) | collective-permute-done | bytes 131104 | tf_op jit(solution)/shard_map/ppermute | solution.py:20
  87.2 2.4 %collective-permute-start.15 = (bf16[512,256]{1,0:T(8,128)(2,1)S(1)}, bf16[512,256]{1,0:T(8,128)(2,1)S(1)}, u32[]{:S(2)}, u32[]{:S(2)}) collective-permute-start(bf16[512,256]{1,0:T(8,128)(2,1)S(1)} %constant_dynamic-update-slice_fusion.refs_2_), channel_id=1, source_target_pairs={{0,4},{2,6},{4,0},{6,2},{1,5},{3,7},{5,1},{7,3},{8,12},{10,14},{12... | collective-permute-start | bytes 786440 | tf_op jit(solution)/shard_map/ppermute | solution.py:16
  90.1 6.4 %collective-permute-done.20.refs_9_.refs_13_ = bf16[2592,256]{1,0:T(8,128)(2,1)S(1)} collective-permute-done((bf16[2592,256]{1,0:T(8,128)(2,1)S(1)}, bf16[2592,256]{1,0:T(8,128)(2,1)S(1)}, u32[]{:S(2)}, u32[]{:S(2)}) %collective-permute-start.20) | collective-permute-done | bytes 1327136 | tf_op jit(solution)/shard_map/ppermute | solution.py:16
  96.7 2.7 %collective-permute-start.21 = (bf16[1296,256]{1,0:T(8,128)(2,1)S(1)}, bf16[1296,256]{1,0:T(8,128)(2,1)S(1)}, u32[]{:S(2)}, u32[]{:S(2)}) collective-permute-start(bf16[1296,256]{1,0:T(8,128)(2,1)S(1)} %slice.51), channel_id=1, source_target_pairs={{0,96},{32,0},{64,32},{96,64},{1,97},{33,1},{65,33},{97,65},{2,98}... | collective-permute-start | bytes 1990664 | tf_op jit(solution)/shard_map/ppermute | solution.py:16
  99.6 2.7 %collective-permute-start.17 = (bf16[1152,256]{1,0:T(8,128)(2,1)S(1)}, bf16[1152,256]{1,0:T(8,128)(2,1)S(1)}, u32[]{:S(2)}, u32[]{:S(2)}) collective-permute-start(bf16[1152,256]{1,0:T(8,128)(2,1)S(1)} %slice.46), channel_id=1, source_target_pairs={{0,6},{2,0},{4,2},{6,4},{1,7},{3,1},{5,3},{7,5},{8,14},{10,8},{12,... | collective-permute-start | bytes 1769480 | tf_op jit(solution)/shard_map/ppermute | solution.py:16
  102.3 1.7 %early.1 = (bf16[1152,2048]{1,0:T(8,128)(2,1)S(1)}, bf16[2048,256]{1,0:T(8,128)(2,1)S(1)}) custom-call(s32[5]{0:T(128)S(1)} %stack.23.coords.refs_0_, bf16[1152,256]{1,0:T(8,128)(2,1)S(1)} %get-tuple-element.31.refs_1_.refs_2_, bf16[512,256]{1,0:T(8,128)(2,1)S(1)} %constant_dynamic-update-slice_fusion.refs_2_, ...), custom_call_target="tpu_custom_call" | custom-call | tf_op jit(solution)/shard_map/early/pallas_call | solution.py:277
  104.0 5.9 %collective-permute-done.18.refs_6_ = bf16[1152,256]{1,0:T(8,128)(2,1)S(1)} collective-permute-done((bf16[1152,256]{1,0:T(8,128)(2,1)S(1)}, bf16[1152,256]{1,0:T(8,128)(2,1)S(1)}, u32[]{:S(2)}, u32[]{:S(2)}) %collective-permute-start.18) | collective-permute-done | bytes 589856 | tf_op jit(solution)/shard_map/ppermute | solution.py:16
  109.9 6.7 %other_half.1 = (bf16[576,1152]{1,0:T(8,128)(2,1)S(1)}, bf16[1152,2048]{1,0:T(8,128)(2,1)S(1)}, bf16[1152,2048]{1,0:T(8,128)(2,1)S(1)}) custom-call(s32[5]{0:T(128)S(1)} %stack.23.coords.refs_0_, f32[32,128]{1,0:T(8,128)S(1)} %bitcast.14, bf16[1152,256]{1,0:T(8,128)(2,1)S(1)} %get-tuple-element.31.refs_1_.refs_2_, ...), custom_call_target="tpu_custom_call", output_to_operand_aliasing={{1}: (4, {})} | custom-call | tf_op jit(solution)/shard_map/other_half/pallas_call | solution.py:289
  116.6 6.8 %collective-permute-start.23 = (bf16[576,1152]{1,0:T(8,128)(2,1)S(1)}, bf16[576,1152]{1,0:T(8,128)(2,1)S(1)}, u32[]{:S(2)}, u32[]{:S(2)}) collective-permute-start(bf16[576,1152]{1,0:T(8,128)(2,1)S(1)} %get-tuple-element.56), channel_id=1, source_target_pairs={{0,1},{1,0},{2,3},{3,2},{4,5},{5,4},{6,7},{7,6},{8,9},{9,8},{10,11... | collective-permute-start | bytes 3981320 | tf_op jit(solution)/shard_map/ppermute | solution.py:20
  123.3 3.8 %own_half.1.own = f32[576,1152]{1,0:T(8,128)S(1)} custom-call(s32[5]{0:T(128)S(1)} %stack.23.coords.refs_0_, bf16[1152,2048]{1,0:T(8,128)(2,1)S(1)} %get-tuple-element.54.a_all, bf16[1152,2048]{1,0:T(8,128)(2,1)S(1)} %get-tuple-element.55.b_all), custom_call_target="tpu_custom_call" | custom-call | tf_op jit(solution)/shard_map/own_half/pallas_call | solution.py:307
  127.2 2.1 %add.50 = f32[576,1152]{1,0:T(8,128)} custom-call(f32[576,1152]{1,0:T(8,128)S(1)} %own_half.1.own, bf16[576,1152]{1,0:T(8,128)(2,1)S(1)} %collective-permute-done.23.other), custom_call_target="tpu_custom_call" | custom-call | tf_op jit(solution)/shard_map/add/pallas_call | solution.py:316
  (57 shorter events, 15.8 us)
Async XLA Ops:
  7.1 8.5 %collective-permute-start = (f32[128,256]{1,0:T(8,128)S(1)}, f32[128,256]{1,0:T(8,128)S(1)}, u32[]{:S(2)}, u32[]{:S(2)}) collective-permute-start(f32[128,256]{1,0:T(8,128)S(1)} %get-tuple-element.33), channel_id=1, source_target_pairs={{0,32},{32,64},{64,96},{96,0},{1,33},{33,65},{65,97},{97,1},{2,34}... | collective-permute-start | bytes 393224 | tf_op jit(solution)/shard_map/ppermute | solution.py:16
  9.7 9.0 %collective-permute-start.1 = (f32[128,256]{1,0:T(8,128)S(1)}, f32[128,256]{1,0:T(8,128)S(1)}, u32[]{:S(2)}, u32[]{:S(2)}) collective-permute-start(f32[128,256]{1,0:T(8,128)S(1)} %get-tuple-element.34), channel_id=1, source_target_pairs={{0,64},{32,96},{64,0},{96,32},{1,65},{33,97},{65,1},{97,33},{2,66}... | collective-permute-start | bytes 393224 | tf_op jit(solution)/shard_map/ppermute | solution.py:16
  13.0 5.7 %collective-permute-start.2 = (f32[128,256]{1,0:T(8,128)S(1)}, f32[128,256]{1,0:T(8,128)S(1)}, u32[]{:S(2)}, u32[]{:S(2)}) collective-permute-start(f32[128,256]{1,0:T(8,128)S(1)} %get-tuple-element.35), channel_id=1, source_target_pairs={{0,96},{32,0},{64,32},{96,64},{1,97},{33,1},{65,33},{97,65},{2,98}... | collective-permute-start | bytes 393224 | tf_op jit(solution)/shard_map/ppermute | solution.py:16
  13.7 17.3 %collective-permute-start.5 = (bf16[1152,256]{1,0:T(8,128)(2,1)S(1)}, bf16[1152,256]{1,0:T(8,128)(2,1)}, u32[]{:S(2)}, u32[]{:S(2)}) collective-permute-start(bf16[1152,256]{1,0:T(8,128)(2,1)S(1)} %get-tuple-element.37), channel_id=1, source_target_pairs={{0,8},{8,0},{1,9},{9,1},{2,10},{10,2},{3,11},{11,3},{4,12},{12,4},... | collective-permute-start | bytes 1769480 | tf_op jit(solution)/shard_map/ppermute | solution.py:20
  14.9 17.3 %collective-permute-start.4 = (bf16[1296,256]{1,0:T(8,128)(2,1)S(1)}, bf16[1296,256]{1,0:T(8,128)(2,1)S(1)}, u32[]{:S(2)}, u32[]{:S(2)}) collective-permute-start(bf16[1296,256]{1,0:T(8,128)(2,1)S(1)} %get-tuple-element.36), channel_id=1, source_target_pairs={{0,0},{1,1},{2,112},{3,113},{4,64},{5,65},{6,48},{7,49},{8,16},{9,... | collective-permute-start | bytes 1990664 | tf_op jit(solution)/shard_map/ppermute | solution.py:355
  18.8 12.2 %collective-permute-start.3 = (f32[96,256]{1,0:T(8,128)S(1)}, f32[96,256]{1,0:T(8,128)S(1)}, u32[]{:S(2)}, u32[]{:S(2)}) collective-permute-start(f32[96,256]{1,0:T(8,128)S(1)} %pad_maximum_fusion.3), channel_id=1, source_target_pairs={{0,16},{16,0},{1,17},{17,1},{2,18},{18,2},{3,19},{19,3},{4,20},{20... | collective-permute-start | bytes 294920 | tf_op jit(solution)/shard_map/ppermute | solution.py:20
  32.2 44.8 %collective-permute-start.11 = (bf16[2304,256]{1,0:T(8,128)(2,1)S(1)}, bf16[2304,256]{1,0:T(8,128)(2,1)S(1)}, u32[]{:S(2)}, u32[]{:S(2)}) collective-permute-start(bf16[2304,256]{1,0:T(8,128)(2,1)S(1)} %pad_maximum_fusion.1.refs_6_.refs_9_), channel_id=1, source_target_pairs={{0,2},{2,4},{4,6},{6,0},{1,3},{3,5},{5,7},{7,1},{8,10},{10,12},{12... | collective-permute-start | bytes 3538952 | tf_op jit(solution)/shard_map/ppermute | solution.py:16
  48.1 28.9 %collective-permute-start.10 = (bf16[2304,256]{1,0:T(8,128)(2,1)S(1)}, bf16[2304,256]{1,0:T(8,128)(2,1)S(1)}, u32[]{:S(2)}, u32[]{:S(2)}) collective-permute-start(bf16[2304,256]{1,0:T(8,128)(2,1)S(1)} %pad_maximum_fusion.1.refs_6_.refs_9_), channel_id=1, source_target_pairs={{0,6},{2,0},{4,2},{6,4},{1,7},{3,1},{5,3},{7,5},{8,14},{10,8},{12,... | collective-permute-start | bytes 3538952 | tf_op jit(solution)/shard_map/ppermute | solution.py:16
  53.5 14.9 %collective-permute-start.9 = (bf16[1296,256]{1,0:T(8,128)(2,1)S(1)}, bf16[1296,256]{1,0:T(8,128)(2,1)S(1)}, u32[]{:S(2)}, u32[]{:S(2)}) collective-permute-start(bf16[1296,256]{1,0:T(8,128)(2,1)S(1)} %collective-permute-done.4), channel_id=1, source_target_pairs={{0,16},{16,0},{1,17},{17,1},{2,18},{18,2},{3,19},{19,3},{4,20},{20... | collective-permute-start | bytes 1990664 | tf_op jit(solution)/shard_map/ppermute | solution.py:20
  55.4 4.5 %collective-permute-start.8 = (bf16[32,256]{1,0:T(8,128)(2,1)S(1)}, bf16[32,256]{1,0:T(8,128)(2,1)S(1)}, u32[]{:S(2)}, u32[]{:S(2)}) collective-permute-start(bf16[32,256]{1,0:T(8,128)(2,1)S(1)} %pad_maximum_fusion.6), channel_id=1, source_target_pairs={{0,32},{32,64},{64,96},{96,0},{1,33},{33,65},{65,97},{97,1},{2,34}... | collective-permute-start | bytes 49160 | tf_op jit(solution)/shard_map/ppermute | solution.py:16
  57.4 4.4 %collective-permute-start.7 = (bf16[32,256]{1,0:T(8,128)(2,1)S(1)}, bf16[32,256]{1,0:T(8,128)(2,1)S(1)}, u32[]{:S(2)}, u32[]{:S(2)}) collective-permute-start(bf16[32,256]{1,0:T(8,128)(2,1)S(1)} %pad_maximum_fusion.6), channel_id=1, source_target_pairs={{0,64},{32,96},{64,0},{96,32},{1,65},{33,97},{65,1},{97,33},{2,66}... | collective-permute-start | bytes 49160 | tf_op jit(solution)/shard_map/ppermute | solution.py:16
  59.9 2.9 %collective-permute-start.6 = (bf16[32,256]{1,0:T(8,128)(2,1)S(1)}, bf16[32,256]{1,0:T(8,128)(2,1)S(1)}, u32[]{:S(2)}, u32[]{:S(2)}) collective-permute-start(bf16[32,256]{1,0:T(8,128)(2,1)S(1)} %pad_maximum_fusion.6), channel_id=1, source_target_pairs={{0,96},{32,0},{64,32},{96,64},{1,97},{33,1},{65,33},{97,65},{2,98}... | collective-permute-start | bytes 49160 | tf_op jit(solution)/shard_map/ppermute | solution.py:16
  68.5 28.0 %collective-permute-start.20 = (bf16[2592,256]{1,0:T(8,128)(2,1)S(1)}, bf16[2592,256]{1,0:T(8,128)(2,1)S(1)}, u32[]{:S(2)}, u32[]{:S(2)}) collective-permute-start(bf16[2592,256]{1,0:T(8,128)(2,1)S(1)} %pad_maximum_fusion.refs_7_.refs_11_), channel_id=1, source_target_pairs={{0,32},{32,64},{64,96},{96,0},{1,33},{33,65},{65,97},{97,1},{2,34}... | collective-permute-start | bytes 3981320 | tf_op jit(solution)/shard_map/ppermute | solution.py:16
  69.6 27.0 %collective-permute-start.19 = (bf16[2592,256]{1,0:T(8,128)(2,1)S(1)}, bf16[2592,256]{1,0:T(8,128)(2,1)S(1)}, u32[]{:S(2)}, u32[]{:S(2)}) collective-permute-start(bf16[2592,256]{1,0:T(8,128)(2,1)S(1)} %pad_maximum_fusion.refs_7_.refs_11_), channel_id=1, source_target_pairs={{0,96},{32,0},{64,32},{96,64},{1,97},{33,1},{65,33},{97,65},{2,98}... | collective-permute-start | bytes 3981320 | tf_op jit(solution)/shard_map/ppermute | solution.py:16
  77.0 4.6 %collective-permute-start.12 = (bf16[128,256]{1,0:T(8,128)(2,1)S(1)}, bf16[128,256]{1,0:T(8,128)(2,1)S(1)}, u32[]{:S(2)}, u32[]{:S(2)}) collective-permute-start(bf16[128,256]{1,0:T(8,128)(2,1)S(1)} %pad_maximum_fusion.5), channel_id=1, source_target_pairs={{0,16},{16,0},{1,17},{17,1},{2,18},{18,2},{3,19},{19,3},{4,20},{20... | collective-permute-start | bytes 196616 | tf_op jit(solution)/shard_map/ppermute | solution.py:20
  81.6 4.5 %collective-permute-start.13 = (bf16[256,256]{1,0:T(8,128)(2,1)S(1)}, bf16[256,256]{1,0:T(8,128)(2,1)S(1)}, u32[]{:S(2)}, u32[]{:S(2)}) collective-permute-start(bf16[256,256]{1,0:T(8,128)(2,1)S(1)} %pad_maximum_fusion.2), channel_id=1, source_target_pairs={{0,8},{8,0},{1,9},{9,1},{2,10},{10,2},{3,11},{11,3},{4,12},{12,4},... | collective-permute-start | bytes 393224 | tf_op jit(solution)/shard_map/ppermute | solution.py:20
  86.2 13.2 %collective-permute-start.16 = (bf16[512,256]{1,0:T(8,128)(2,1)S(1)}, bf16[512,256]{1,0:T(8,128)(2,1)S(1)}, u32[]{:S(2)}, u32[]{:S(2)}) collective-permute-start(bf16[512,256]{1,0:T(8,128)(2,1)S(1)} %constant_dynamic-update-slice_fusion.refs_2_), channel_id=1, source_target_pairs={{0,2},{2,4},{4,6},{6,0},{1,3},{3,5},{5,7},{7,1},{8,10},{10,12},{12... | collective-permute-start | bytes 786440 | tf_op jit(solution)/shard_map/ppermute | solution.py:16
  87.2 12.2 %collective-permute-start.15 = (bf16[512,256]{1,0:T(8,128)(2,1)S(1)}, bf16[512,256]{1,0:T(8,128)(2,1)S(1)}, u32[]{:S(2)}, u32[]{:S(2)}) collective-permute-start(bf16[512,256]{1,0:T(8,128)(2,1)S(1)} %constant_dynamic-update-slice_fusion.refs_2_), channel_id=1, source_target_pairs={{0,4},{2,6},{4,0},{6,2},{1,5},{3,7},{5,1},{7,3},{8,12},{10,14},{12... | collective-permute-start | bytes 786440 | tf_op jit(solution)/shard_map/ppermute | solution.py:16
  89.6 9.8 %collective-permute-start.14 = (bf16[512,256]{1,0:T(8,128)(2,1)S(1)}, bf16[512,256]{1,0:T(8,128)(2,1)S(1)}, u32[]{:S(2)}, u32[]{:S(2)}) collective-permute-start(bf16[512,256]{1,0:T(8,128)(2,1)S(1)} %constant_dynamic-update-slice_fusion.refs_2_), channel_id=1, source_target_pairs={{0,6},{2,0},{4,2},{6,4},{1,7},{3,1},{5,3},{7,5},{8,14},{10,8},{12,... | collective-permute-start | bytes 786440 | tf_op jit(solution)/shard_map/ppermute | solution.py:16
  96.5 13.3 %collective-permute-start.22 = (bf16[1296,256]{1,0:T(8,128)(2,1)S(1)}, bf16[1296,256]{1,0:T(8,128)(2,1)S(1)}, u32[]{:S(2)}, u32[]{:S(2)}) collective-permute-start(bf16[1296,256]{1,0:T(8,128)(2,1)S(1)} %slice.52), channel_id=1, source_target_pairs={{0,32},{32,64},{64,96},{96,0},{1,33},{33,65},{65,97},{97,1},{2,34}... | collective-permute-start | bytes 1990664 | tf_op jit(solution)/shard_map/ppermute | solution.py:16
  96.7 13.2 %collective-permute-start.21 = (bf16[1296,256]{1,0:T(8,128)(2,1)S(1)}, bf16[1296,256]{1,0:T(8,128)(2,1)S(1)}, u32[]{:S(2)}, u32[]{:S(2)}) collective-permute-start(bf16[1296,256]{1,0:T(8,128)(2,1)S(1)} %slice.51), channel_id=1, source_target_pairs={{0,96},{32,0},{64,32},{96,64},{1,97},{33,1},{65,33},{97,65},{2,98}... | collective-permute-start | bytes 1990664 | tf_op jit(solution)/shard_map/ppermute | solution.py:16
  99.5 10.4 %collective-permute-start.18 = (bf16[1152,256]{1,0:T(8,128)(2,1)S(1)}, bf16[1152,256]{1,0:T(8,128)(2,1)S(1)}, u32[]{:S(2)}, u32[]{:S(2)}) collective-permute-start(bf16[1152,256]{1,0:T(8,128)(2,1)S(1)} %slice.47), channel_id=1, source_target_pairs={{0,2},{2,4},{4,6},{6,0},{1,3},{3,5},{5,7},{7,1},{8,10},{10,12},{12... | collective-permute-start | bytes 1769480 | tf_op jit(solution)/shard_map/ppermute | solution.py:16
  99.6 10.3 %collective-permute-start.17 = (bf16[1152,256]{1,0:T(8,128)(2,1)S(1)}, bf16[1152,256]{1,0:T(8,128)(2,1)S(1)}, u32[]{:S(2)}, u32[]{:S(2)}) collective-permute-start(bf16[1152,256]{1,0:T(8,128)(2,1)S(1)} %slice.46), channel_id=1, source_target_pairs={{0,6},{2,0},{4,2},{6,4},{1,7},{3,1},{5,3},{7,5},{8,14},{10,8},{12,... | collective-permute-start | bytes 1769480 | tf_op jit(solution)/shard_map/ppermute | solution.py:16
  116.6 10.6 %collective-permute-start.23 = (bf16[576,1152]{1,0:T(8,128)(2,1)S(1)}, bf16[576,1152]{1,0:T(8,128)(2,1)S(1)}, u32[]{:S(2)}, u32[]{:S(2)}) collective-permute-start(bf16[576,1152]{1,0:T(8,128)(2,1)S(1)} %get-tuple-element.56), channel_id=1, source_target_pairs={{0,1},{1,0},{2,3},{3,2},{4,5},{5,4},{6,7},{7,6},{8,9},{9,8},{10,11... | collective-permute-start | bytes 3981320 | tf_op jit(solution)/shard_map/ppermute | solution.py:20
  (2 other events, 31.3 us)

commit v5 on v4

--- a/solution.py
+++ b/solution.py
@@ -30,13 +30,7 @@
         for xh in range(NX):
             for xl in range(NL):
                 for y in range(NY):
-                    turn = 2 * (z & 1) + xh
-                    to = (
-                        (z - y + turn) % NZ,
-                        xh ^ xl ^ (z >> 1) ^ (y & 1),
-                        z >> 1,
-                        turn,
-                    )
+                    to = ((z + y) % NZ, xh ^ xl ^ (z >> 1), z >> 1, 2 * (z & 1) + xh)
                     for k in range(NC):
                         pairs.append((place(z, xh, xl, y, k), place(*to, k)))
     return pairs
@@ -177,8 +171,8 @@
 
 def source_of(z, xh, xl, y, dxh, dz):
     zz = lax.rem(z + dz, NZ)
-    from_y = lax.rem(2 * xl + (y >> 1) + y - zz + NZ, NZ)
-    from_l = (xh + dxh + (y & 1) + xl + (from_y & 1)) & 1
+    from_y = lax.rem(zz - (2 * xl + (y >> 1)) + NZ, NZ)
+    from_l = (xh + dxh + (y & 1) + xl) & 1
     return from_y, from_l
 
 

time: 130 us -> 130 us (level)
  waiting for transfers between devices: 45.4 us -> 41.9 us
  starting transfers between devices: 59.8 us -> 63.2 us
    ppermute x6, starting transfers between devices: 13.3 us -> 23.8 us  [flip(): return lax.ppermute(x, axis, [(i, i ^ bit) for i in range(size)])]
    ppermute x17, starting transfers between devices: 45.8 us -> 38.7 us  [shift(): return lax.ppermute(x, axis, [(i, (i + step) % size) for i in range(size)])]
    ppermute x17, waiting for transfers between devices: 22.7 us -> 20.7 us  [shift(): return lax.ppermute(x, axis, [(i, (i + step) % size) for i in range(size)])]
    ppermute x6, waiting for transfers between devices: 22.7 us -> 21.3 us  [flip(): return lax.ppermute(x, axis, [(i, i ^ bit) for i in range(size)])]
where the time goes in v5:
time: 130 us; the launch traced here: 129 us
  starting transfers between devices  63.2 us (49%)
  waiting for transfers between devices  41.9 us (32%)
  Pallas kernels  20.6 us (16%)
  other arithmetic  2.03 us (2%)
    ppermute x17, starting transfers between devices, shift(): return lax.ppermute(x, axis, [(i, (i + step) % size) for i in range(size)])  38.7 us
    ppermute x6, starting transfers between devices, flip(): return lax.ppermute(x, axis, [(i, i ^ bit) for i in range(size)])  23.8 us
    ppermute x6, waiting for transfers between devices, flip(): return lax.ppermute(x, axis, [(i, i ^ bit) for i in range(size)])  21.3 us
    ppermute x17, waiting for transfers between devices, shift(): return lax.ppermute(x, axis, [(i, (i + step) % size) for i in range(size)])  20.7 us
    pallas_call x1, Pallas kernels, final(): pl.pallas_call(body, out_shape=[jax.ShapeDtypeStruct((half, rows), BF16),...  6.71 us
    pallas_call x1, Pallas kernels, head(): pl.pallas_call(head_kernel, grid=(STEPS,), in_specs=[smem, smem, pl.Block...  6.34 us
    pallas_call x1, Pallas kernels, final(): pl.pallas_call(own_kernel, out_shape=jax.ShapeDtypeStruct((half, rows), F...  3.78 us
  transfers between devices with their start and end apart: 24, of which 11 were waited for; matrix products, arithmetic and copies ran while one was open for 2% of the time, Pallas kernels for 4%

profile of v5, /device:TPU:1, one launch (start us, length us, event | category | flops | bytes accessed | tf_op | source)
XLA Modules:
  0.0 129.0 jit_solution(3862222835783569968)
XLA Ops:
  0.7 6.3 %head.1 = (f32[128,256]{1,0:T(8,128)S(1)}, f32[128,256]{1,0:T(8,128)S(1)}, f32[128,256]{1,0:T(8,128)S(1)}, f32[128,256]{1,0:T(8,128)S(1)}, bf16[1152,256]{1,0:T(...) custom-call(s32[9]{0:T(128)S(1)} %broadcast_subtract_fusion.index, ...), custom_call_target="tpu_custom_call" | custom-call | tf_op jit(solution)/shard_map/head/pallas_call | solution.py:139
  7.1 2.6 %collective-permute-start = (f32[128,256]{1,0:T(8,128)S(1)}, f32[128,256]{1,0:T(8,128)S(1)}, u32[]{:S(2)}, u32[]{:S(2)}) collective-permute-start(f32[128,256]{1,0:T(8,128)S(1)} %get-tuple-element.33), channel_id=1, source_target_pairs={{0,32},{32,64},{64,96},{96,0},{1,33},{33,65},{65,97},{97,1},{2,34}... | collective-permute-start | bytes 393224 | tf_op jit(solution)/shard_map/ppermute | solution.py:16
  9.6 3.3 %collective-permute-start.1 = (f32[128,256]{1,0:T(8,128)S(1)}, f32[128,256]{1,0:T(8,128)S(1)}, u32[]{:S(2)}, u32[]{:S(2)}) collective-permute-start(f32[128,256]{1,0:T(8,128)S(1)} %get-tuple-element.34), channel_id=1, source_target_pairs={{0,64},{32,96},{64,0},{96,32},{1,65},{33,97},{65,1},{97,33},{2,66}... | collective-permute-start | bytes 393224 | tf_op jit(solution)/shard_map/ppermute | solution.py:16
  15.6 3.0 %collective-permute-done.1 = f32[128,256]{1,0:T(8,128)S(1)} collective-permute-done((f32[128,256]{1,0:T(8,128)S(1)}, f32[128,256]{1,0:T(8,128)S(1)}, u32[]{:S(2)}, u32[]{:S(2)}) %collective-permute-start.1) | collective-permute-done | bytes 131104 | tf_op jit(solution)/shard_map/ppermute | solution.py:16
  18.7 2.9 %collective-permute-start.3 = (f32[96,256]{1,0:T(8,128)S(1)}, f32[96,256]{1,0:T(8,128)S(1)}, u32[]{:S(2)}, u32[]{:S(2)}) collective-permute-start(f32[96,256]{1,0:T(8,128)S(1)} %pad_maximum_fusion.3), channel_id=1, source_target_pairs={{0,16},{16,0},{1,17},{17,1},{2,18},{18,2},{3,19},{19,3},{4,20},{20... | collective-permute-start | bytes 294920 | tf_op jit(solution)/shard_map/ppermute | solution.py:20
  21.6 9.4 %collective-permute-done.3 = f32[96,256]{1,0:T(8,128)S(1)} collective-permute-done((f32[96,256]{1,0:T(8,128)S(1)}, f32[96,256]{1,0:T(8,128)S(1)}, u32[]{:S(2)}, u32[]{:S(2)}) %collective-permute-start.3) | collective-permute-done | bytes 98336 | tf_op jit(solution)/shard_map/ppermute | solution.py:20
  32.2 13.0 %collective-permute-start.11 = (bf16[2304,256]{1,0:T(8,128)(2,1)S(1)}, bf16[2304,256]{1,0:T(8,128)(2,1)S(1)}, u32[]{:S(2)}, u32[]{:S(2)}) collective-permute-start(bf16[2304,256]{1,0:T(8,128)(2,1)S(1)} %pad_maximum_fusion.1.refs_6_.refs_9_), channel_id=1, source_target_pairs={{0,2},{2,4},{4,6},{6,0},{1,3},{3,5},{5,7},{7,1},{8,10},{10,12},{12... | collective-permute-start | bytes 3538952 | tf_op jit(solution)/shard_map/ppermute | solution.py:16
  45.3 2.6 %collective-permute-start.10 = (bf16[2304,256]{1,0:T(8,128)(2,1)S(1)}, bf16[2304,256]{1,0:T(8,128)(2,1)S(1)}, u32[]{:S(2)}, u32[]{:S(2)}) collective-permute-start(bf16[2304,256]{1,0:T(8,128)(2,1)S(1)} %pad_maximum_fusion.1.refs_6_.refs_9_), channel_id=1, source_target_pairs={{0,6},{2,0},{4,2},{6,4},{1,7},{3,1},{5,3},{7,5},{8,14},{10,8},{12,... | collective-permute-start | bytes 3538952 | tf_op jit(solution)/shard_map/ppermute | solution.py:16
  47.8 5.3 %collective-permute-start.9 = (bf16[1296,256]{1,0:T(8,128)(2,1)S(1)}, bf16[1296,256]{1,0:T(8,128)(2,1)S(1)}, u32[]{:S(2)}, u32[]{:S(2)}) collective-permute-start(bf16[1296,256]{1,0:T(8,128)(2,1)S(1)} %collective-permute-done.4), channel_id=1, source_target_pairs={{0,16},{16,0},{1,17},{17,1},{2,18},{18,2},{3,19},{19,3},{4,20},{20... | collective-permute-start | bytes 1990664 | tf_op jit(solution)/shard_map/ppermute | solution.py:20
  55.3 1.7 %collective-permute-start.7 = (bf16[32,256]{1,0:T(8,128)(2,1)S(1)}, bf16[32,256]{1,0:T(8,128)(2,1)S(1)}, u32[]{:S(2)}, u32[]{:S(2)}) collective-permute-start(bf16[32,256]{1,0:T(8,128)(2,1)S(1)} %pad_maximum_fusion.6), channel_id=1, source_target_pairs={{0,64},{32,96},{64,0},{96,32},{1,65},{33,97},{65,1},{97,33},{2,66}... | collective-permute-start | bytes 49160 | tf_op jit(solution)/shard_map/ppermute | solution.py:16
  61.0 5.7 %collective-permute-done.9 = bf16[1296,256]{1,0:T(8,128)(2,1)S(1)} collective-permute-done((bf16[1296,256]{1,0:T(8,128)(2,1)S(1)}, bf16[1296,256]{1,0:T(8,128)(2,1)S(1)}, u32[]{:S(2)}, u32[]{:S(2)}) %collective-permute-start.9) | collective-permute-done | bytes 663584 | tf_op jit(solution)/shard_map/ppermute | solution.py:20
  66.8 2.7 %collective-permute-start.19 = (bf16[2592,256]{1,0:T(8,128)(2,1)S(1)}, bf16[2592,256]{1,0:T(8,128)(2,1)S(1)}, u32[]{:S(2)}, u32[]{:S(2)}) collective-permute-start(bf16[2592,256]{1,0:T(8,128)(2,1)S(1)} %pad_maximum_fusion.refs_7_.refs_11_), channel_id=1, source_target_pairs={{0,96},{32,0},{64,32},{96,64},{1,97},{33,1},{65,33},{97,65},{2,98}... | collective-permute-start | bytes 3981320 | tf_op jit(solution)/shard_map/ppermute | solution.py:16
  69.7 9.5 %collective-permute-start.12 = (bf16[128,256]{1,0:T(8,128)(2,1)S(1)}, bf16[128,256]{1,0:T(8,128)(2,1)S(1)}, u32[]{:S(2)}, u32[]{:S(2)}) collective-permute-start(bf16[128,256]{1,0:T(8,128)(2,1)S(1)} %pad_maximum_fusion.5), channel_id=1, source_target_pairs={{0,16},{16,0},{1,17},{17,1},{2,18},{18,2},{3,19},{19,3},{4,20},{20... | collective-permute-start | bytes 196616 | tf_op jit(solution)/shard_map/ppermute | solution.py:20
  80.9 4.5 %collective-permute-done.13 = bf16[256,256]{1,0:T(8,128)(2,1)S(1)} collective-permute-done((bf16[256,256]{1,0:T(8,128)(2,1)S(1)}, bf16[256,256]{1,0:T(8,128)(2,1)S(1)}, u32[]{:S(2)}, u32[]{:S(2)}) %collective-permute-start.13) | collective-permute-done | bytes 131104 | tf_op jit(solution)/shard_map/ppermute | solution.py:20
  85.5 3.8 %collective-permute-start.15 = (bf16[512,256]{1,0:T(8,128)(2,1)S(1)}, bf16[512,256]{1,0:T(8,128)(2,1)S(1)}, u32[]{:S(2)}, u32[]{:S(2)}) collective-permute-start(bf16[512,256]{1,0:T(8,128)(2,1)S(1)} %constant_dynamic-update-slice_fusion.refs_2_), channel_id=1, source_target_pairs={{0,4},{2,6},{4,0},{6,2},{1,5},{3,7},{5,1},{7,3},{8,12},{10,14},{12... | collective-permute-start | bytes 786440 | tf_op jit(solution)/shard_map/ppermute | solution.py:16
  89.3 6.5 %collective-permute-done.20.refs_9_.refs_13_ = bf16[2592,256]{1,0:T(8,128)(2,1)S(1)} collective-permute-done((bf16[2592,256]{1,0:T(8,128)(2,1)S(1)}, bf16[2592,256]{1,0:T(8,128)(2,1)S(1)}, u32[]{:S(2)}, u32[]{:S(2)}) %collective-permute-start.20) | collective-permute-done | bytes 1327136 | tf_op jit(solution)/shard_map/ppermute | solution.py:16
  96.0 2.7 %collective-permute-start.21 = (bf16[1296,256]{1,0:T(8,128)(2,1)S(1)}, bf16[1296,256]{1,0:T(8,128)(2,1)S(1)}, u32[]{:S(2)}, u32[]{:S(2)}) collective-permute-start(bf16[1296,256]{1,0:T(8,128)(2,1)S(1)} %slice.51), channel_id=1, source_target_pairs={{0,96},{32,0},{64,32},{96,64},{1,97},{33,1},{65,33},{97,65},{2,98}... | collective-permute-start | bytes 1990664 | tf_op jit(solution)/shard_map/ppermute | solution.py:16
  99.2 3.1 %collective-permute-start.17 = (bf16[1152,256]{1,0:T(8,128)(2,1)S(1)}, bf16[1152,256]{1,0:T(8,128)(2,1)S(1)}, u32[]{:S(2)}, u32[]{:S(2)}) collective-permute-start(bf16[1152,256]{1,0:T(8,128)(2,1)S(1)} %slice.46), channel_id=1, source_target_pairs={{0,6},{2,0},{4,2},{6,4},{1,7},{3,1},{5,3},{7,5},{8,14},{10,8},{12,... | collective-permute-start | bytes 1769480 | tf_op jit(solution)/shard_map/ppermute | solution.py:16
  102.3 1.7 %early.1 = (bf16[1152,2048]{1,0:T(8,128)(2,1)S(1)}, bf16[2048,256]{1,0:T(8,128)(2,1)S(1)}) custom-call(s32[5]{0:T(128)S(1)} %stack.23.coords.refs_0_, bf16[1152,256]{1,0:T(8,128)(2,1)S(1)} %get-tuple-element.31.refs_1_.refs_2_, bf16[512,256]{1,0:T(8,128)(2,1)S(1)} %constant_dynamic-update-slice_fusion.refs_2_, ...), custom_call_target="tpu_custom_call" | custom-call | tf_op jit(solution)/shard_map/early/pallas_call | solution.py:271
  104.1 7.5 %collective-permute-done.18.refs_6_ = bf16[1152,256]{1,0:T(8,128)(2,1)S(1)} collective-permute-done((bf16[1152,256]{1,0:T(8,128)(2,1)S(1)}, bf16[1152,256]{1,0:T(8,128)(2,1)S(1)}, u32[]{:S(2)}, u32[]{:S(2)}) %collective-permute-start.18) | collective-permute-done | bytes 589856 | tf_op jit(solution)/shard_map/ppermute | solution.py:16
  111.6 6.7 %other_half.1 = (bf16[576,1152]{1,0:T(8,128)(2,1)S(1)}, bf16[1152,2048]{1,0:T(8,128)(2,1)S(1)}, bf16[1152,2048]{1,0:T(8,128)(2,1)S(1)}) custom-call(s32[5]{0:T(128)S(1)} %stack.23.coords.refs_0_, f32[32,128]{1,0:T(8,128)S(1)} %bitcast.14, bf16[1152,256]{1,0:T(8,128)(2,1)S(1)} %get-tuple-element.31.refs_1_.refs_2_, ...), custom_call_target="tpu_custom_call", output_to_operand_aliasing={{1}: (4, {})} | custom-call | tf_op jit(solution)/shard_map/other_half/pallas_call | solution.py:283
  118.3 4.8 %collective-permute-start.23 = (bf16[576,1152]{1,0:T(8,128)(2,1)S(1)}, bf16[576,1152]{1,0:T(8,128)(2,1)S(1)}, u32[]{:S(2)}, u32[]{:S(2)}) collective-permute-start(bf16[576,1152]{1,0:T(8,128)(2,1)S(1)} %get-tuple-element.56), channel_id=1, source_target_pairs={{0,1},{1,0},{2,3},{3,2},{4,5},{5,4},{6,7},{7,6},{8,9},{9,8},{10,11... | collective-permute-start | bytes 3981320 | tf_op jit(solution)/shard_map/ppermute | solution.py:20
  123.2 3.8 %own_half.1.own = f32[576,1152]{1,0:T(8,128)S(1)} custom-call(s32[5]{0:T(128)S(1)} %stack.23.coords.refs_0_, bf16[1152,2048]{1,0:T(8,128)(2,1)S(1)} %get-tuple-element.54.a_all, bf16[1152,2048]{1,0:T(8,128)(2,1)S(1)} %get-tuple-element.55.b_all), custom_call_target="tpu_custom_call" | custom-call | tf_op jit(solution)/shard_map/own_half/pallas_call | solution.py:301
  127.0 2.1 %add.50 = f32[576,1152]{1,0:T(8,128)} custom-call(f32[576,1152]{1,0:T(8,128)S(1)} %own_half.1.own, bf16[576,1152]{1,0:T(8,128)(2,1)S(1)} %collective-permute-done.23.other), custom_call_target="tpu_custom_call" | custom-call | tf_op jit(solution)/shard_map/add/pallas_call | solution.py:310
  (57 shorter events, 13.5 us)
Async XLA Ops:
  7.1 8.5 %collective-permute-start = (f32[128,256]{1,0:T(8,128)S(1)}, f32[128,256]{1,0:T(8,128)S(1)}, u32[]{:S(2)}, u32[]{:S(2)}) collective-permute-start(f32[128,256]{1,0:T(8,128)S(1)} %get-tuple-element.33), channel_id=1, source_target_pairs={{0,32},{32,64},{64,96},{96,0},{1,33},{33,65},{65,97},{97,1},{2,34}... | collective-permute-start | bytes 393224 | tf_op jit(solution)/shard_map/ppermute | solution.py:16
  9.6 9.0 %collective-permute-start.1 = (f32[128,256]{1,0:T(8,128)S(1)}, f32[128,256]{1,0:T(8,128)S(1)}, u32[]{:S(2)}, u32[]{:S(2)}) collective-permute-start(f32[128,256]{1,0:T(8,128)S(1)} %get-tuple-element.34), channel_id=1, source_target_pairs={{0,64},{32,96},{64,0},{96,32},{1,65},{33,97},{65,1},{97,33},{2,66}... | collective-permute-start | bytes 393224 | tf_op jit(solution)/shard_map/ppermute | solution.py:16
  12.9 5.7 %collective-permute-start.2 = (f32[128,256]{1,0:T(8,128)S(1)}, f32[128,256]{1,0:T(8,128)S(1)}, u32[]{:S(2)}, u32[]{:S(2)}) collective-permute-start(f32[128,256]{1,0:T(8,128)S(1)} %get-tuple-element.35), channel_id=1, source_target_pairs={{0,96},{32,0},{64,32},{96,64},{1,97},{33,1},{65,33},{97,65},{2,98}... | collective-permute-start | bytes 393224 | tf_op jit(solution)/shard_map/ppermute | solution.py:16
  13.7 17.3 %collective-permute-start.5 = (bf16[1152,256]{1,0:T(8,128)(2,1)S(1)}, bf16[1152,256]{1,0:T(8,128)(2,1)}, u32[]{:S(2)}, u32[]{:S(2)}) collective-permute-start(bf16[1152,256]{1,0:T(8,128)(2,1)S(1)} %get-tuple-element.37), channel_id=1, source_target_pairs={{0,8},{8,0},{1,9},{9,1},{2,10},{10,2},{3,11},{11,3},{4,12},{12,4},... | collective-permute-start | bytes 1769480 | tf_op jit(solution)/shard_map/ppermute | solution.py:20
  14.9 17.3 %collective-permute-start.4 = (bf16[1296,256]{1,0:T(8,128)(2,1)S(1)}, bf16[1296,256]{1,0:T(8,128)(2,1)S(1)}, u32[]{:S(2)}, u32[]{:S(2)}) collective-permute-start(bf16[1296,256]{1,0:T(8,128)(2,1)S(1)} %get-tuple-element.36), channel_id=1, source_target_pairs={{0,0},{1,1},{2,32},{3,33},{4,64},{5,65},{6,96},{7,97},{8,16},{9,17... | collective-permute-start | bytes 1990664 | tf_op jit(solution)/shard_map/ppermute | solution.py:349
  18.7 12.2 %collective-permute-start.3 = (f32[96,256]{1,0:T(8,128)S(1)}, f32[96,256]{1,0:T(8,128)S(1)}, u32[]{:S(2)}, u32[]{:S(2)}) collective-permute-start(f32[96,256]{1,0:T(8,128)S(1)} %pad_maximum_fusion.3), channel_id=1, source_target_pairs={{0,16},{16,0},{1,17},{17,1},{2,18},{18,2},{3,19},{19,3},{4,20},{20... | collective-permute-start | bytes 294920 | tf_op jit(solution)/shard_map/ppermute | solution.py:20
  32.2 37.4 %collective-permute-start.11 = (bf16[2304,256]{1,0:T(8,128)(2,1)S(1)}, bf16[2304,256]{1,0:T(8,128)(2,1)S(1)}, u32[]{:S(2)}, u32[]{:S(2)}) collective-permute-start(bf16[2304,256]{1,0:T(8,128)(2,1)S(1)} %pad_maximum_fusion.1.refs_6_.refs_9_), channel_id=1, source_target_pairs={{0,2},{2,4},{4,6},{6,0},{1,3},{3,5},{5,7},{7,1},{8,10},{10,12},{12... | collective-permute-start | bytes 3538952 | tf_op jit(solution)/shard_map/ppermute | solution.py:16
  45.3 24.4 %collective-permute-start.10 = (bf16[2304,256]{1,0:T(8,128)(2,1)S(1)}, bf16[2304,256]{1,0:T(8,128)(2,1)S(1)}, u32[]{:S(2)}, u32[]{:S(2)}) collective-permute-start(bf16[2304,256]{1,0:T(8,128)(2,1)S(1)} %pad_maximum_fusion.1.refs_6_.refs_9_), channel_id=1, source_target_pairs={{0,6},{2,0},{4,2},{6,4},{1,7},{3,1},{5,3},{7,5},{8,14},{10,8},{12,... | collective-permute-start | bytes 3538952 | tf_op jit(solution)/shard_map/ppermute | solution.py:16
  47.8 18.8 %collective-permute-start.9 = (bf16[1296,256]{1,0:T(8,128)(2,1)S(1)}, bf16[1296,256]{1,0:T(8,128)(2,1)S(1)}, u32[]{:S(2)}, u32[]{:S(2)}) collective-permute-start(bf16[1296,256]{1,0:T(8,128)(2,1)S(1)} %collective-permute-done.4), channel_id=1, source_target_pairs={{0,16},{16,0},{1,17},{17,1},{2,18},{18,2},{3,19},{19,3},{4,20},{20... | collective-permute-start | bytes 1990664 | tf_op jit(solution)/shard_map/ppermute | solution.py:20
  53.9 4.2 %collective-permute-start.8 = (bf16[32,256]{1,0:T(8,128)(2,1)S(1)}, bf16[32,256]{1,0:T(8,128)(2,1)S(1)}, u32[]{:S(2)}, u32[]{:S(2)}) collective-permute-start(bf16[32,256]{1,0:T(8,128)(2,1)S(1)} %pad_maximum_fusion.6), channel_id=1, source_target_pairs={{0,32},{32,64},{64,96},{96,0},{1,33},{33,65},{65,97},{97,1},{2,34}... | collective-permute-start | bytes 49160 | tf_op jit(solution)/shard_map/ppermute | solution.py:16
  55.3 4.4 %collective-permute-start.7 = (bf16[32,256]{1,0:T(8,128)(2,1)S(1)}, bf16[32,256]{1,0:T(8,128)(2,1)S(1)}, u32[]{:S(2)}, u32[]{:S(2)}) collective-permute-start(bf16[32,256]{1,0:T(8,128)(2,1)S(1)} %pad_maximum_fusion.6), channel_id=1, source_target_pairs={{0,64},{32,96},{64,0},{96,32},{1,65},{33,97},{65,1},{97,33},{2,66}... | collective-permute-start | bytes 49160 | tf_op jit(solution)/shard_map/ppermute | solution.py:16
  58.1 2.9 %collective-permute-start.6 = (bf16[32,256]{1,0:T(8,128)(2,1)S(1)}, bf16[32,256]{1,0:T(8,128)(2,1)S(1)}, u32[]{:S(2)}, u32[]{:S(2)}) collective-permute-start(bf16[32,256]{1,0:T(8,128)(2,1)S(1)} %pad_maximum_fusion.6), channel_id=1, source_target_pairs={{0,96},{32,0},{64,32},{96,64},{1,97},{33,1},{65,33},{97,65},{2,98}... | collective-permute-start | bytes 49160 | tf_op jit(solution)/shard_map/ppermute | solution.py:16
  66.8 29.1 %collective-permute-start.20 = (bf16[2592,256]{1,0:T(8,128)(2,1)S(1)}, bf16[2592,256]{1,0:T(8,128)(2,1)S(1)}, u32[]{:S(2)}, u32[]{:S(2)}) collective-permute-start(bf16[2592,256]{1,0:T(8,128)(2,1)S(1)} %pad_maximum_fusion.refs_7_.refs_11_), channel_id=1, source_target_pairs={{0,32},{32,64},{64,96},{96,0},{1,33},{33,65},{65,97},{97,1},{2,34}... | collective-permute-start | bytes 3981320 | tf_op jit(solution)/shard_map/ppermute | solution.py:16
  66.8 29.1 %collective-permute-start.19 = (bf16[2592,256]{1,0:T(8,128)(2,1)S(1)}, bf16[2592,256]{1,0:T(8,128)(2,1)S(1)}, u32[]{:S(2)}, u32[]{:S(2)}) collective-permute-start(bf16[2592,256]{1,0:T(8,128)(2,1)S(1)} %pad_maximum_fusion.refs_7_.refs_11_), channel_id=1, source_target_pairs={{0,96},{32,0},{64,32},{96,64},{1,97},{33,1},{65,33},{97,65},{2,98}... | collective-permute-start | bytes 3981320 | tf_op jit(solution)/shard_map/ppermute | solution.py:16
  69.7 11.1 %collective-permute-start.12 = (bf16[128,256]{1,0:T(8,128)(2,1)S(1)}, bf16[128,256]{1,0:T(8,128)(2,1)S(1)}, u32[]{:S(2)}, u32[]{:S(2)}) collective-permute-start(bf16[128,256]{1,0:T(8,128)(2,1)S(1)} %pad_maximum_fusion.5), channel_id=1, source_target_pairs={{0,16},{16,0},{1,17},{17,1},{2,18},{18,2},{3,19},{19,3},{4,20},{20... | collective-permute-start | bytes 196616 | tf_op jit(solution)/shard_map/ppermute | solution.py:20
  80.8 4.6 %collective-permute-start.13 = (bf16[256,256]{1,0:T(8,128)(2,1)S(1)}, bf16[256,256]{1,0:T(8,128)(2,1)S(1)}, u32[]{:S(2)}, u32[]{:S(2)}) collective-permute-start(bf16[256,256]{1,0:T(8,128)(2,1)S(1)} %pad_maximum_fusion.2), channel_id=1, source_target_pairs={{0,8},{8,0},{1,9},{9,1},{2,10},{10,2},{3,11},{11,3},{4,12},{12,4},... | collective-permute-start | bytes 393224 | tf_op jit(solution)/shard_map/ppermute | solution.py:20
  85.4 13.3 %collective-permute-start.16 = (bf16[512,256]{1,0:T(8,128)(2,1)S(1)}, bf16[512,256]{1,0:T(8,128)(2,1)S(1)}, u32[]{:S(2)}, u32[]{:S(2)}) collective-permute-start(bf16[512,256]{1,0:T(8,128)(2,1)S(1)} %constant_dynamic-update-slice_fusion.refs_2_), channel_id=1, source_target_pairs={{0,2},{2,4},{4,6},{6,0},{1,3},{3,5},{5,7},{7,1},{8,10},{10,12},{12... | collective-permute-start | bytes 786440 | tf_op jit(solution)/shard_map/ppermute | solution.py:16
  85.5 13.2 %collective-permute-start.15 = (bf16[512,256]{1,0:T(8,128)(2,1)S(1)}, bf16[512,256]{1,0:T(8,128)(2,1)S(1)}, u32[]{:S(2)}, u32[]{:S(2)}) collective-permute-start(bf16[512,256]{1,0:T(8,128)(2,1)S(1)} %constant_dynamic-update-slice_fusion.refs_2_), channel_id=1, source_target_pairs={{0,4},{2,6},{4,0},{6,2},{1,5},{3,7},{5,1},{7,3},{8,12},{10,14},{12... | collective-permute-start | bytes 786440 | tf_op jit(solution)/shard_map/ppermute | solution.py:16
  89.3 9.5 %collective-permute-start.14 = (bf16[512,256]{1,0:T(8,128)(2,1)S(1)}, bf16[512,256]{1,0:T(8,128)(2,1)S(1)}, u32[]{:S(2)}, u32[]{:S(2)}) collective-permute-start(bf16[512,256]{1,0:T(8,128)(2,1)S(1)} %constant_dynamic-update-slice_fusion.refs_2_), channel_id=1, source_target_pairs={{0,6},{2,0},{4,2},{6,4},{1,7},{3,1},{5,3},{7,5},{8,14},{10,8},{12,... | collective-permute-start | bytes 786440 | tf_op jit(solution)/shard_map/ppermute | solution.py:16
  95.9 15.7 %collective-permute-start.22 = (bf16[1296,256]{1,0:T(8,128)(2,1)S(1)}, bf16[1296,256]{1,0:T(8,128)(2,1)S(1)}, u32[]{:S(2)}, u32[]{:S(2)}) collective-permute-start(bf16[1296,256]{1,0:T(8,128)(2,1)S(1)} %slice.52), channel_id=1, source_target_pairs={{0,32},{32,64},{64,96},{96,0},{1,33},{33,65},{65,97},{97,1},{2,34}... | collective-permute-start | bytes 1990664 | tf_op jit(solution)/shard_map/ppermute | solution.py:16
  96.0 15.6 %collective-permute-start.21 = (bf16[1296,256]{1,0:T(8,128)(2,1)S(1)}, bf16[1296,256]{1,0:T(8,128)(2,1)S(1)}, u32[]{:S(2)}, u32[]{:S(2)}) collective-permute-start(bf16[1296,256]{1,0:T(8,128)(2,1)S(1)} %slice.51), channel_id=1, source_target_pairs={{0,96},{32,0},{64,32},{96,64},{1,97},{33,1},{65,33},{97,65},{2,98}... | collective-permute-start | bytes 1990664 | tf_op jit(solution)/shard_map/ppermute | solution.py:16
  98.9 12.8 %collective-permute-start.18 = (bf16[1152,256]{1,0:T(8,128)(2,1)S(1)}, bf16[1152,256]{1,0:T(8,128)(2,1)S(1)}, u32[]{:S(2)}, u32[]{:S(2)}) collective-permute-start(bf16[1152,256]{1,0:T(8,128)(2,1)S(1)} %slice.47), channel_id=1, source_target_pairs={{0,2},{2,4},{4,6},{6,0},{1,3},{3,5},{5,7},{7,1},{8,10},{10,12},{12... | collective-permute-start | bytes 1769480 | tf_op jit(solution)/shard_map/ppermute | solution.py:16
  99.2 12.4 %collective-permute-start.17 = (bf16[1152,256]{1,0:T(8,128)(2,1)S(1)}, bf16[1152,256]{1,0:T(8,128)(2,1)S(1)}, u32[]{:S(2)}, u32[]{:S(2)}) collective-permute-start(bf16[1152,256]{1,0:T(8,128)(2,1)S(1)} %slice.46), channel_id=1, source_target_pairs={{0,6},{2,0},{4,2},{6,4},{1,7},{3,1},{5,3},{7,5},{8,14},{10,8},{12,... | collective-permute-start | bytes 1769480 | tf_op jit(solution)/shard_map/ppermute | solution.py:16
  118.3 8.6 %collective-permute-start.23 = (bf16[576,1152]{1,0:T(8,128)(2,1)S(1)}, bf16[576,1152]{1,0:T(8,128)(2,1)S(1)}, u32[]{:S(2)}, u32[]{:S(2)}) collective-permute-start(bf16[576,1152]{1,0:T(8,128)(2,1)S(1)} %get-tuple-element.56), channel_id=1, source_target_pairs={{0,1},{1,0},{2,3},{3,2},{4,5},{5,4},{6,7},{7,6},{8,9},{9,8},{10,11... | collective-permute-start | bytes 3981320 | tf_op jit(solution)/shard_map/ppermute | solution.py:20
  (2 other events, 31.5 us)
